TPU v7x, 32 devices: a whole 2x2x4 slice. The times are simulated.
32 devices in a mesh: tp: 2 (over y), req: 16 (over z, x, core).
Axes of the slice: x: 2, y: 2, z: 4, core: 2. Of those that a mesh axis runs over, the one named last changes fastest.
Arguments:
- token_ids: int32 [8192], P('req'), may hold values from 0 to 31999, as said below
- prompt_lengths: int32 [16, 4], P('req'), may hold values from 1 to 256, 512 in all within a row
- tenant_ids: int32 [16, 4], P('req'), may hold values from 0 to 1, never falling along the last dimension, each value on 1 to 3 neighbouring positions
- embed_table: bfloat16 [32000, 1536], P('req'), may hold values from -6 to 6
- attention_gain: float32 [1536], replicated, may hold values from 0.1 to 1.9
- qkv_weight: float32 [1536, 3072], P(('tp', 'req')), may hold values from -0.25 to 0.25
- out_weight: bfloat16 [1536, 1536], P('tp'), may hold values from -0.15625 to 0.15625
- ffn_gain: float32 [1536], replicated, may hold values from 0.1 to 1.9
- gate_up_weight: float32 [1536, 8192], P(('tp', 'req')), may hold values from -0.15625 to 0.15625
- down_weight: bfloat16 [4096, 1536], P('tp'), may hold values from -0.09375 to 0.09375
Outputs:
- final_hidden: bfloat16 [8192, 1536], P('req')
- kv_cache: bfloat16 [2, 8192, 768], P(None, 'req', 'tp')
Inputs may be any that keep to these rules, and one draw needn't show every extreme that they name: Split token_ids into aligned blocks of 256 tokens and the ids into ranges of 2000 consecutive ids: no block has more than 32 ids in one range, and one range gets exactly 32 ids from every block. `prompt_lengths`: the 4 lengths of a request group sum to 512. `tenant_ids`: never falling along the prompts of a request group; every tenant has one to 3 prompts.
All inputs are finite; a program needn't handle non-finite values.
Results may differ from a plain program's by a relative error of at most 0.01.
Values may be sent and summed in bfloat16 or wider, within the bound.
No kernel may reach another device: no remote copies, remote signals or barrier semaphores. Data moves between devices by JAX's collectives and lax.ppermute only.
A program may use at most 128 MiB of HBM per device.

v0:
```python
import jax
import jax.numpy as jnp
from jax import lax
from jax.sharding import PartitionSpec as P

HEAD_DIM = 96


rope_base = 100000.0
norm_eps = 1e-05


def rms_scaled(values, gain):
    mean_square = jnp.mean(values * values, axis=-1, keepdims=True)
    return (values * lax.rsqrt(mean_square + norm_eps) * gain).astype(jnp.bfloat16)


def token_layout(lengths, tenants, row_count):
    positions = jnp.arange(row_count, dtype=jnp.int32)
    prompt_ends = jnp.cumsum(lengths)
    prompt_starts = prompt_ends - lengths
    passed = (positions[:, None] >= prompt_ends[None, :]).astype(jnp.int32)
    prompt = jnp.sum(passed, axis=1)
    in_prompt = (prompt[:, None] == jnp.arange(lengths.shape[0], dtype=jnp.int32)[None, :]).astype(
        jnp.int32
    )
    offset = positions - jnp.sum(in_prompt * prompt_starts[None, :], axis=1)
    tenant = jnp.sum(in_prompt * tenants[None, :], axis=1)
    return (offset, tenant)


def rotate(values, offset):
    half_dim = values.shape[-1] // 2
    frequency = rope_base ** (-2.0 * jnp.arange(half_dim, dtype=jnp.float32) / values.shape[-1])
    angles = offset.astype(jnp.float32)[:, None] * frequency[None, :]
    cosine = jnp.cos(angles)[:, None, :]
    sine_part = jnp.sin(angles)[:, None, :]
    lower_half = values[..., :half_dim]
    upper_half = values[..., half_dim:]
    return jnp.concatenate(
        [
            lower_half * cosine - upper_half * sine_part,
            upper_half * cosine + lower_half * sine_part,
        ],
        axis=-1,
    )


def attend(queries, key_heads, value_heads, tenant):
    row_count = queries.shape[0]
    positions = jnp.arange(row_count, dtype=jnp.int32)
    score_scale = queries.shape[-1] ** (-0.5)
    allowed = (positions[None, :] <= positions[:, None]) & (tenant[None, :] == tenant[:, None])
    scores = (
        jnp.einsum("qkgd,skd->kgqs", queries, key_heads, preferred_element_type=jnp.float32)
        * score_scale
    )
    scores = jnp.where(allowed[None, None], scores, -jnp.inf)
    row_max = jnp.max(scores, axis=-1, keepdims=True)
    expo = jnp.exp(scores - row_max)
    weights = (expo / jnp.sum(expo, axis=-1, keepdims=True)).astype(jnp.bfloat16)
    mixed_out = jnp.einsum(
        "kgqs,skd->qkgd", weights, value_heads, preferred_element_type=jnp.float32
    )
    pieces = mixed_out.astype(jnp.bfloat16)
    return pieces


def ffn_hidden(normed_ffn, gate_cols, ff_half):
    gate_up = jnp.dot(normed_ffn, gate_cols, preferred_element_type=jnp.float32)
    return (jax.nn.silu(gate_up[:, :ff_half]) * gate_up[:, ff_half:]).astype(jnp.bfloat16)


def per_device(
    token_ids,
    prompt_lengths,
    tenant_ids,
    embed_table,
    attention_gain,
    qkv_weight,
    out_weight,
    ffn_gain,
    gate_up_weight,
    down_weight,
):
    tp_count = lax.axis_size("tp")
    tp_index = lax.axis_index("tp")
    group_count = lax.axis_size("req")
    tokens = token_ids.shape[0]
    looked = tokens // tp_count
    own_rows = embed_table.shape[0]
    capacity = max(2, 2 * looked // group_count)
    my_ids = lax.dynamic_slice_in_dim(token_ids, tp_index * looked, looked)
    owner_of = my_ids // own_rows
    row_in_range = my_ids - owner_of * own_rows
    owner_hits = (owner_of[:, None] == jnp.arange(group_count, dtype=jnp.int32)[None, :]).astype(
        jnp.int32
    )
    slot_of = jnp.sum((jnp.cumsum(owner_hits, axis=0) - owner_hits) * owner_hits, axis=1)
    requests = (
        jnp.full((group_count, capacity), -1, jnp.int32).at[owner_of, slot_of].set(row_in_range)
    )
    found_rows = jnp.take(
        embed_table,
        jnp.maximum(lax.all_to_all(requests, "req", split_axis=0, concat_axis=0, tiled=True), 0),
        axis=0,
    )
    returned = lax.all_to_all(found_rows, "req", split_axis=0, concat_axis=0, tiled=True)
    embedded = lax.all_gather(returned[owner_of, slot_of], "tp", axis=0, tiled=True)
    offset, tenant = token_layout(prompt_lengths[0], tenant_ids[0], tokens)
    rows_here = qkv_weight.shape[0]
    q_half = out_weight.shape[0]
    ff_half = down_weight.shape[0]
    q_full = q_half * tp_count
    kv_half = (qkv_weight.shape[1] - q_full) // (2 * tp_count)
    kv_full = kv_half * tp_count
    packed = qkv_weight.astype(jnp.bfloat16)
    gate_up_bf = gate_up_weight.astype(jnp.bfloat16)
    packed_rows = jnp.concatenate(
        [
            packed[:, :q_full].reshape(rows_here, tp_count, q_half),
            packed[:, q_full : q_full + kv_full].reshape(rows_here, tp_count, kv_half),
            packed[:, q_full + kv_full :].reshape(rows_here, tp_count, kv_half),
            gate_up_bf.reshape(rows_here, 2, tp_count, ff_half)
            .transpose(0, 2, 1, 3)
            .reshape(rows_here, tp_count, 2 * ff_half),
        ],
        axis=2,
    )
    collected = lax.all_gather(packed_rows, "req", axis=0, tiled=True)
    columns = lax.all_to_all(collected, "tp", split_axis=1, concat_axis=0, tiled=True)
    weights = columns[:, 0, :]
    normed = rms_scaled(embedded.astype(jnp.float32), attention_gain)
    projected = jnp.dot(
        normed, weights[:, : q_half + 2 * kv_half], preferred_element_type=jnp.float32
    )
    kv_local = kv_half // HEAD_DIM
    queries = rotate(
        projected[:, :q_half].reshape(tokens, q_half // HEAD_DIM, HEAD_DIM), offset
    ).astype(jnp.bfloat16)
    key_heads = rotate(
        projected[:, q_half : q_half + kv_half].reshape(tokens, kv_local, HEAD_DIM), offset
    ).astype(jnp.bfloat16)
    value_heads = (
        projected[:, q_half + kv_half :].reshape(tokens, kv_local, HEAD_DIM).astype(jnp.bfloat16)
    )
    kv_cache = jnp.stack([key_heads.reshape(tokens, kv_half), value_heads.reshape(tokens, kv_half)])
    attended = attend(
        queries.reshape(tokens, kv_local, -1, HEAD_DIM), key_heads, value_heads, tenant
    ).reshape(tokens, q_half)
    gate_cols = weights[:, q_half + 2 * kv_half :]
    attn_sum = lax.psum(
        jnp.dot(attended, out_weight, preferred_element_type=jnp.float32).astype(jnp.bfloat16), "tp"
    ).astype(jnp.float32)
    residual = embedded.astype(jnp.float32) + attn_sum
    normed_ffn = rms_scaled(residual, ffn_gain)
    hidden = ffn_hidden(normed_ffn, gate_cols, ff_half)
    ffn_sum = lax.psum(
        jnp.dot(hidden, down_weight, preferred_element_type=jnp.float32).astype(jnp.bfloat16), "tp"
    ).astype(jnp.float32)
    final_out = (residual + ffn_sum).astype(jnp.bfloat16)
    return (final_out, kv_cache)


def solution(mesh):
    return jax.shard_map(
        per_device,
        mesh=mesh,
        in_specs=(
            P("req"),
            P("req", None),
            P("req", None),
            P("req", None),
            P(),
            P(("tp", "req"), None),
            P("tp", None),
            P(),
            P(("tp", "req"), None),
            P("tp", None),
        ),
        out_specs=(P("req", None), P(None, "req", "tp")),
        check_vma=False,
    )
```

profile of v0, /device:TPU:0, one launch (start us, length us, event | category | flops | bytes accessed | tf_op | source)
XLA Modules:
  0.0 530.0 jit_solution(3900098590027576408)
XLA Ops:
  8.1 1.2 convert_element_type.91
  9.3 2.4 convert_element_type.92
  11.7 2.6 reshape.236
  14.3 1.5 copy.85
  15.8 2.5 reshape.237
  18.4 1.1 pad_maximum_fusion
  19.5 0.1 multiply_subtract_fusion.1
  19.6 0.6 reduce-window.10
  20.1 0.2 slice_reduce_fusion
  20.4 0.1 fusion.31
  20.5 12.8 %scatter_fusion = s32[16,32]{1,0:T(8,128)S(1)} fusion(s32[16,32]{1,0:T(8,128)S(1)} %broadcast_in_dim.22, s32[256]{0:T(256)S(1)} %bitcast.107, s32[256]{0:T(256)S(1)} %get-tuple-element.4), kind=kCustom, calls=%fused_computation.2 | custom fusion | bytes 5120 | tf_op jit(solution)/shard_map/scatter | solution.py:101
  33.3 13.7 %all_to_all.29 = s32[16,1,32]{2,1,0:T(1,128)S(1)} all-to-all(s32[16,1,32]{2,1,0:T(1,128)S(1)} %bitcast.105), channel_id=1, replica_groups=mesh['tp'=2,'req'=16] {'req'}, dimensions={0} | all-to-all | bytes 4096 | tf_op jit(solution)/shard_map/all_to_all | solution.py:105
  47.0 8.0 %gather_fusion = bf16[512,1536]{1,0:T(8,128)(2,1)} fusion(bf16[2000,1536]{1,0:T(8,128)(2,1)} %param.13, s32[1024]{0:T(1024)S(1)} %pad_clamp_fusion), kind=kCustom, calls=%fused_computation | custom fusion | bytes 3147776 | tf_op jit(solution)/shard_map/jit(_take)/gather | solution.py:103
  55.0 1.7 broadcast_select_fusion
  56.7 60.0 %all_to_all.30 = bf16[16,32,1536]{2,1,0:T(8,128)(2,1)} all-to-all(bf16[16,32,1536]{2,1,0:T(8,128)(2,1)S(1)} %broadcast_select_fusion), channel_id=1, replica_groups=mesh['tp'=2,'req'=16] {'req'}, dimensions={0} | all-to-all | bytes 3145728 | tf_op jit(solution)/shard_map/all_to_all | solution.py:108
  116.7 25.0 %all-gather.5.cloned.1.call-done = bf16[768,2,5632]{2,0,1:T(8,128)(2,1)} async-done(((bf16[48,2,5632]{2,0,1:T(8,128)(2,1)}), bf16[768,2,5632]{2,0,1:T(8,128)(2,1)}) %all-gather.5.cloned.1.call-update) | async-done | bytes 17301520 | tf_op jit(solution)/shard_map/all_gather | solution.py:130
  141.7 9.8 %all-to-all-start.2 = ((bf16[768,2,5632]{2,0,1:T(8,128)(2,1)}), bf16[768,2,5632]{2,0,1:T(8,128)(2,1)}, u32[]{:S(2)}, u32[]{:S(2)}) async-start(bf16[768,2,5632]{2,0,1:T(8,128)(2,1)} %all-gather.5.cloned.1.call-done), calls=%async_computation.2 | async-start | bytes 34603008 | tf_op jit(solution)/shard_map/all_to_all | solution.py:131
  151.6 4.6 gather_fusion.1
  156.3 0.2 all-reduce.3.cloned.1.call-start
  156.5 0.2 reduce-window.14
  156.8 0.1 select_reduce_fusion
  156.9 1.1 multiply_cosine_fusion
  158.0 0.9 fusion.21
  158.9 47.1 %all-gather.3.cloned.1.call-done = bf16[512,1536]{1,0:T(8,128)(2,1)} async-done(((bf16[256,1536]{1,0:T(8,128)(2,1)}), bf16[512,1536]{1,0:T(8,128)(2,1)}) %all-gather.3.cloned.1.call-update) | async-done | bytes 1572880 | tf_op jit(solution)/shard_map/all_gather | solution.py:109
  206.0 1.8 fusion.11
  207.8 149.1 %all-to-all-done.2 = bf16[768,2,5632]{2,0,1:T(8,128)(2,1)} async-done(((bf16[768,2,5632]{2,0,1:T(8,128)(2,1)}), bf16[768,2,5632]{2,0,1:T(8,128)(2,1)}, u32[]{:S(2)}, u32[]{:S(2)}) %all-to-all-start.2) | async-done | bytes 17301536 | tf_op jit(solution)/shard_map/all_to_all | solution.py:131
  356.9 5.0 fusion.4
  362.0 1.4 slice.79
  363.4 0.8 copy-done.3
  364.2 0.9 copy.68
  365.1 3.1 copy.70
  368.3 1.1 copy.69
  369.5 2.4 subtract_convert_fusion
  371.8 1.2 multiply_subtract_fusion
  373.1 7.4 %fusion.44 = (f32[4,2,512]{2,1,0:T(2,128)S(1)}, f32[4,2,512,512]{2,3,1,0:T(8,128)}) fusion(pred[512,512]{0,1:T(8,128)(4,1)} %fusion.21, bf16[512,4,2,48]{0,3,2,1:T(8,128)(2,1)} %bitcast.117, bf16[512,4,2,48]{0,3,2,1:T(8,128)(2,1)S(1)} %bitcast.116, bf16[512,4,48]{0,2,1:T(8,128)(2,1)S(1)} %get-tuple-element.11, bf16[512,4,48]{0,2,1:T(8,128)(2,1)S(1)} %get-tuple-element.10), kind=kOutput, calls=%fused_computation.93 | convolution fusion | flops 413401600 | bytes 9846784 | tf_op jit(solution)/shard_map/sub | solution.py:60
  380.5 4.2 fusion.20
  384.7 2.6 convolution_convert_fusion.1
  387.3 0.3 all-reduce.5.cloned.1.call-start
  387.6 55.3 %all-reduce.3.cloned.1.call-done = bf16[512,1536]{1,0:T(8,128)(2,1)} async-done(((bf16[512,1536]{1,0:T(8,128)(2,1)}), bf16[512,1536]{1,0:T(8,128)(2,1)}) %all-reduce.3.cloned.1.call-update) | async-done | bytes 1572880 | tf_op jit(solution)/shard_map/psum | solution.py:152
  442.9 2.6 multiply_reduce_fusion
  445.5 0.2 copy-done.2
  445.7 12.1 %fusion.1 = f32[512,4096]{1,0:T(8,128)} fusion(bf16[1536,5632]{1,0:T(8,128)(2,1)} %bitcast.14, bf16[512,1536]{1,0:T(8,128)(2,1)S(1)} %copy-done.2, bf16[512,1536]{1,0:T(8,128)(2,1)S(1)} %copy-done.1, f32[1536]{0:T(1024)S(1)} %copy-done.10, f32[512]{0:T(512)S(1)} %add_rsqrt_fusion), kind=kOutput, calls=%fused_computation.4 | convolution fusion | flops 6447169536 | bytes 24125440 | tf_op jit(solution)/shard_map/dot_general | solution.py:70
  457.8 9.1 %convolution_convert_fusion = bf16[512,1536]{1,0:T(8,128)(2,1)} fusion(bf16[2048,1536]{1,0:T(8,128)(2,1)S(1)} %bitcast.129, f32[512,4096]{1,0:T(8,128)} %fusion.1), kind=kOutput, calls=%fused_computation.27 | convolution fusion | flops 3228303360 | bytes 16252928 | tf_op jit(solution)/shard_map/dot_general | solution.py:159
  467.0 0.2 copy.72
  467.2 1.2 slice_bitcast_fusion
  468.4 1.0 pad_maximum_fusion.2
  469.4 49.0 %all-reduce.5.cloned.1.call-done = bf16[512,1536]{1,0:T(8,128)(2,1)} async-done(((bf16[512,1536]{1,0:T(8,128)(2,1)}), bf16[512,1536]{1,0:T(8,128)(2,1)}) %all-reduce.5.cloned.1.call-update) | async-done | bytes 1572880 | tf_op jit(solution)/shard_map/psum | solution.py:158
  518.3 4.1 add_convert_fusion
  (57 shorter events, 0.6 us)
Async XLA Ops:
  8.0 376.7 %copy-start = (bf16[768,1536]{1,0:T(8,128)(2,1)S(1)}, bf16[768,1536]{1,0:T(8,128)(2,1)}, u32[]{:S(2)}) copy-start(bf16[768,1536]{1,0:T(8,128)(2,1)} %param.16) | copy-start | bytes 7077892
  8.0 133.7 %all-gather.5.cloned.1.call-start = ((), (), s32[]{:S(2)}) async-start(), calls=%async_computation.4 | async-start | bytes 18382848 | tf_op jit(solution)/shard_map/all_gather | solution.py:130
  14.3 5.2 copy-start.8
  141.7 215.2 %all-to-all-start.2 = ((bf16[768,2,5632]{2,0,1:T(8,128)(2,1)}), bf16[768,2,5632]{2,0,1:T(8,128)(2,1)}, u32[]{:S(2)}, u32[]{:S(2)}) async-start(bf16[768,2,5632]{2,0,1:T(8,128)(2,1)} %all-gather.5.cloned.1.call-done), calls=%async_computation.2 | async-start | bytes 34603008 | tf_op jit(solution)/shard_map/all_to_all | solution.py:131
  151.5 54.5 %all-gather.3.cloned.1.call-start = ((), (), s32[]{:S(2)}) async-start(), calls=%async_computation.3 | async-start | bytes 2359296 | tf_op jit(solution)/shard_map/all_gather | solution.py:109
  151.6 4.9 copy-start.11
  151.6 5.2 copy-start.7
  151.6 205.3 %copy-start.9 = (f32[1536]{0:T(1024)S(1)}, f32[1536]{0:T(1024)}, u32[]{:S(2)}) copy-start(f32[1536]{0:T(1024)} %param.14) | copy-start | bytes 18436
  156.3 286.6 %all-reduce.3.cloned.1.call-start = ((), (), s32[]{:S(2)}) async-start(), calls=%async_computation.5 | async-start | bytes 3145728 | tf_op jit(solution)/shard_map/psum | solution.py:152
  362.0 2.2 copy-start.3
  364.2 4.1 slice-start
  365.1 4.3 copy-start.4
  365.1 4.3 copy-start.5
  373.1 7.4 %copy-start.6 = (bf16[512,384]{0,1:T(8,128)(2,1)S(1)}, bf16[512,384]{0,1:T(8,128)(2,1)}, u32[]{:S(2)}) copy-start(bf16[512,384]{0,1:T(8,128)(2,1)} %copy.68) | copy-start | bytes 1179652
  387.3 58.3 %copy-start.10 = (f32[1536]{0:T(1024)S(1)}, f32[1536]{0:T(1024)}, u32[]{:S(2)}) copy-start(f32[1536]{0:T(1024)} %param.17) | copy-start | bytes 18436
  387.3 131.0 %all-reduce.5.cloned.1.call-start = ((), (), s32[]{:S(2)}) async-start(), calls=%async_computation.6 | async-start | bytes 3145728 | tf_op jit(solution)/shard_map/psum | solution.py:158
  442.9 2.6 copy-start.1
  442.9 2.8 copy-start.2
  442.9 14.9 %slice-start.1 = ((s8[6291456]{0:T(1024)(128)(4,1)}), s8[4194304]{0:T(1024)(128)(4,1)S(1)}, s32[]{:S(2)}) async-start(s8[6291456]{0:T(1024)(128)(4,1)} %bitcast.128), calls=%async_computation.8 | async-start | bytes 8388608
  445.7 12.1 %slice-start.2 = ((s8[6291456]{0:T(1024)(128)(4,1)}), s8[2097152]{0:T(1024)(128)(4,1)S(1)}, s32[]{:S(2)}) async-start(s8[6291456]{0:T(1024)(128)(4,1)} %bitcast.128), calls=%async_computation.9 | async-start | bytes 4194304
Sparse Core Ops, SparseCore 0:
  19.6 122.0 all-gather.4
Sparse Core Ops, SparseCore 1:
  156.4 49.6 all-gather.2
  387.4 55.5 all-reduce.2
  467.0 51.2 all-reduce.4
where the time goes:
time: 531 us; the launch traced here: 530 us
  waiting for transfers between devices  325 us (61%)
  blocking collectives  73.7 us (14%)
  local copies, waits for them, and re-layouts  41.4 us (8%)
  matrix products  40.4 us (8%)
  other arithmetic  22.7 us (4%)
  between operations  15.9 us (3%)
  starting transfers between devices  10.4 us (2%)
    all_to_all x1, waiting for transfers between devices, per_device(): lax.all_to_all(collected, 'tp', split_axis=1, concat_axis=0, tiled=True)  149 us
    all_to_all x1, blocking collectives, per_device(): lax.all_to_all(found_rows, 'req', split_axis=0, concat_axis=0, tiled=True)  60 us
    psum x1, waiting for transfers between devices, per_device(): lax.psum(jnp.dot(attended, out_weight, preferred_element_type=jnp.float32...  55.3 us
    psum x1, waiting for transfers between devices, per_device(): lax.psum(jnp.dot(hidden, down_weight, preferred_element_type=jnp.float32)...  49 us
    all_gather x1, waiting for transfers between devices, per_device(): lax.all_gather(returned[owner_of, slot_of], 'tp', axis=0, tiled=True)  47.1 us
    all_gather x1, waiting for transfers between devices, per_device(): collected = lax.all_gather(packed_rows, 'req', axis=0, tiled=True)  25 us
    all_to_all x1, blocking collectives, per_device(): lax.all_to_all(requests, 'req', split_axis=0, concat_axis=0, tiled=True)  13.7 us
    scatter x1, local copies, waits for them, and re-layouts, per_device(): jnp.full((group_count, capacity), -1, jnp.int32).at[owner_of, slot_of]  12.8 us
  transfers between devices with their start and end apart: 5, of which 5 were waited for; matrix products, arithmetic and copies ran while one was open for 7% of the time, Pallas kernels for 0%

commit v1 on v0

--- a/solution.py
+++ b/solution.py
@@ -66,9 +66,22 @@
     return pieces
 
 
-def ffn_hidden(normed_ffn, gate_cols, ff_half):
-    gate_up = jnp.dot(normed_ffn, gate_cols, preferred_element_type=jnp.float32)
-    return (jax.nn.silu(gate_up[:, :ff_half]) * gate_up[:, ff_half:]).astype(jnp.bfloat16)
+PAIR = [(0, 1), (1, 0)]
+
+
+def two_part_dot(left, right, split, tp_index):
+    width = right.shape[1] // 2
+    own = lax.dynamic_slice_in_dim(left, tp_index * split, split, axis=1)
+    other = lax.dynamic_slice_in_dim(left, (1 - tp_index) * split, split, axis=1)
+    return jnp.dot(own, right[:, :width], preferred_element_type=jnp.float32) + jnp.dot(
+        other, right[:, width:], preferred_element_type=jnp.float32
+    )
+
+
+def in_order(own, other, tp_index, axis):
+    first = jnp.where(tp_index == 0, own, other)
+    second = jnp.where(tp_index == 0, other, own)
+    return jnp.concatenate([first, second], axis=axis)
 
 
 def per_device(
@@ -89,51 +102,86 @@
     tokens = token_ids.shape[0]
     looked = tokens // tp_count
     own_rows = embed_table.shape[0]
+    width = embed_table.shape[1]
     capacity = max(2, 2 * looked // group_count)
-    my_ids = lax.dynamic_slice_in_dim(token_ids, tp_index * looked, looked)
-    owner_of = my_ids // own_rows
-    row_in_range = my_ids - owner_of * own_rows
-    owner_hits = (owner_of[:, None] == jnp.arange(group_count, dtype=jnp.int32)[None, :]).astype(
-        jnp.int32
-    )
-    slot_of = jnp.sum((jnp.cumsum(owner_hits, axis=0) - owner_hits) * owner_hits, axis=1)
-    requests = (
-        jnp.full((group_count, capacity), -1, jnp.int32).at[owner_of, slot_of].set(row_in_range)
-    )
-    found_rows = jnp.take(
-        embed_table,
-        jnp.maximum(lax.all_to_all(requests, "req", split_axis=0, concat_axis=0, tiled=True), 0),
-        axis=0,
-    )
-    returned = lax.all_to_all(found_rows, "req", split_axis=0, concat_axis=0, tiled=True)
-    embedded = lax.all_gather(returned[owner_of, slot_of], "tp", axis=0, tiled=True)
-    offset, tenant = token_layout(prompt_lengths[0], tenant_ids[0], tokens)
-    rows_here = qkv_weight.shape[0]
     q_half = out_weight.shape[0]
     ff_half = down_weight.shape[0]
     q_full = q_half * tp_count
     kv_half = (qkv_weight.shape[1] - q_full) // (2 * tp_count)
     kv_full = kv_half * tp_count
-    packed = qkv_weight.astype(jnp.bfloat16)
-    gate_up_bf = gate_up_weight.astype(jnp.bfloat16)
-    packed_rows = jnp.concatenate(
-        [
-            packed[:, :q_full].reshape(rows_here, tp_count, q_half),
-            packed[:, q_full : q_full + kv_full].reshape(rows_here, tp_count, kv_half),
-            packed[:, q_full + kv_full :].reshape(rows_here, tp_count, kv_half),
-            gate_up_bf.reshape(rows_here, 2, tp_count, ff_half)
-            .transpose(0, 2, 1, 3)
-            .reshape(rows_here, tp_count, 2 * ff_half),
-        ],
-        axis=2,
-    )
-    collected = lax.all_gather(packed_rows, "req", axis=0, tiled=True)
-    columns = lax.all_to_all(collected, "tp", split_axis=1, concat_axis=0, tiled=True)
-    weights = columns[:, 0, :]
-    normed = rms_scaled(embedded.astype(jnp.float32), attention_gain)
-    projected = jnp.dot(
-        normed, weights[:, : q_half + 2 * kv_half], preferred_element_type=jnp.float32
-    )
+    ff_full = ff_half * tp_count
+    half_width = width // tp_count
+
+    def qkv_cols(half):
+        return jnp.concatenate(
+            [
+                lax.dynamic_slice_in_dim(qkv_weight, base + half * size, size, axis=1)
+                for base, size in ((0, q_half), (q_full, kv_half), (q_full + kv_full, kv_half))
+            ],
+            axis=1,
+        ).astype(jnp.bfloat16)
+
+    def ffn_cols(half):
+        return jnp.concatenate(
+            [
+                lax.dynamic_slice_in_dim(gate_up_weight, base + half * ff_half, ff_half, axis=1)
+                for base in (0, ff_full)
+            ],
+            axis=1,
+        ).astype(jnp.bfloat16)
+
+    other_qkv = lax.ppermute(qkv_cols(1 - tp_index), "tp", PAIR)
+    qkv_all = lax.all_gather(
+        jnp.concatenate([qkv_cols(tp_index), other_qkv], axis=1), "req", axis=0, tiled=True
+    )
+    other_ffn = lax.ppermute(ffn_cols(1 - tp_index), "tp", PAIR)
+    ffn_all = lax.all_gather(
+        jnp.concatenate([ffn_cols(tp_index), other_ffn], axis=1), "req", axis=0, tiled=True
+    )
+    out_other = lax.ppermute(out_weight, "tp", PAIR)
+
+    my_ids = lax.dynamic_slice_in_dim(token_ids, tp_index * looked, looked)
+    owner_of = my_ids // own_rows
+    row_in_range = my_ids - owner_of * own_rows
+    owners = jnp.arange(group_count, dtype=jnp.int32)
+    owner_hits = owner_of[:, None] == owners[None, :]
+    earlier = jnp.arange(looked)[None, :] < jnp.arange(looked)[:, None]
+    same = (owner_of[:, None] == owner_of[None, :]) & earlier
+    slot_of = jnp.sum(same.astype(jnp.int32), axis=1)
+    place = owner_of * capacity + slot_of
+    chosen = place[None, :] == jnp.arange(group_count * capacity, dtype=jnp.int32)[:, None]
+    requests = (
+        jnp.sum(jnp.where(chosen, row_in_range[None, :] + 1, 0), axis=1).reshape(
+            group_count, capacity
+        )
+        - 1
+    )
+    asked = lax.all_to_all(requests, "req", split_axis=0, concat_axis=0, tiled=True).reshape(-1)
+    pick_rows = (asked[:, None] == jnp.arange(own_rows, dtype=jnp.int32)[None, :]).astype(
+        jnp.bfloat16
+    )
+    found_rows = jnp.dot(pick_rows, embed_table, preferred_element_type=jnp.float32).astype(
+        jnp.bfloat16
+    )
+    returned = lax.all_to_all(
+        found_rows.reshape(group_count, capacity, width),
+        "req",
+        split_axis=0,
+        concat_axis=0,
+        tiled=True,
+    ).reshape(group_count * capacity, width)
+    pick_mine = (
+        place[:, None] == jnp.arange(group_count * capacity, dtype=jnp.int32)[None, :]
+    ).astype(jnp.bfloat16)
+    embedded_own = jnp.dot(pick_mine, returned, preferred_element_type=jnp.float32).astype(
+        jnp.bfloat16
+    )
+    embedded_other = lax.ppermute(embedded_own, "tp", PAIR)
+    embedded = in_order(embedded_own, embedded_other, tp_index, 0).astype(jnp.float32)
+
+    offset, tenant = token_layout(prompt_lengths[0], tenant_ids[0], tokens)
+    normed = rms_scaled(embedded, attention_gain)
+    projected = two_part_dot(normed, qkv_all, half_width, tp_index)
     kv_local = kv_half // HEAD_DIM
     queries = rotate(
         projected[:, :q_half].reshape(tokens, q_half // HEAD_DIM, HEAD_DIM), offset
@@ -148,18 +196,25 @@
     attended = attend(
         queries.reshape(tokens, kv_local, -1, HEAD_DIM), key_heads, value_heads, tenant
     ).reshape(tokens, q_half)
-    gate_cols = weights[:, q_half + 2 * kv_half :]
-    attn_sum = lax.psum(
-        jnp.dot(attended, out_weight, preferred_element_type=jnp.float32).astype(jnp.bfloat16), "tp"
-    ).astype(jnp.float32)
-    residual = embedded.astype(jnp.float32) + attn_sum
+    attended_other = lax.ppermute(attended, "tp", PAIR)
+    residual = (
+        embedded
+        + jnp.dot(attended, out_weight, preferred_element_type=jnp.float32)
+        + jnp.dot(attended_other, out_other, preferred_element_type=jnp.float32)
+    )
     normed_ffn = rms_scaled(residual, ffn_gain)
-    hidden = ffn_hidden(normed_ffn, gate_cols, ff_half)
-    ffn_sum = lax.psum(
-        jnp.dot(hidden, down_weight, preferred_element_type=jnp.float32).astype(jnp.bfloat16), "tp"
-    ).astype(jnp.float32)
-    final_out = (residual + ffn_sum).astype(jnp.bfloat16)
-    return (final_out, kv_cache)
+    gate_up = two_part_dot(normed_ffn, ffn_all, half_width, tp_index)
+    hidden = (jax.nn.silu(gate_up[:, :ff_half]) * gate_up[:, ff_half:]).astype(jnp.bfloat16)
+    chunks = 4
+    step = width // chunks
+    finals = []
+    for c in range(chunks):
+        part = jnp.dot(
+            hidden, down_weight[:, c * step : (c + 1) * step], preferred_element_type=jnp.float32
+        ).astype(jnp.bfloat16)
+        total = part.astype(jnp.float32) + lax.ppermute(part, "tp", PAIR).astype(jnp.float32)
+        finals.append((residual[:, c * step : (c + 1) * step] + total).astype(jnp.bfloat16))
+    return (jnp.concatenate(finals, axis=1), kv_cache)
 
 
 def solution(mesh):

time: 531 us -> 262 us (0.49)
  waiting for transfers between devices: 325 us -> 138 us
  blocking collectives: 73.7 us -> 12 us
  local copies, waits for them, and re-layouts: 41.4 us -> 12.6 us
  matrix products: 40.4 us -> 51.8 us
  other arithmetic: 22.7 us -> 14.9 us
  starting transfers between devices: 10.4 us -> 17.4 us
    all_to_all x1, waiting for transfers between devices: 149 us -> 39 us  [per_device(): lax.all_to_all(found_rows.reshape(group_count, capacity, width), 'req', s...]
    psum x2 -> x0, waiting for transfers between devices: 104 us -> none  [the longest x1 55.3 us: per_device(): lax.psum(jnp.dot(attended, out_weight, preferred_element_type=jnp.float32...]
    ppermute x0 -> x9, waiting for transfers between devices: none -> 85.2 us  [the longest x4 28.7 us: per_device(): lax.ppermute(part, 'tp', PAIR).astype(jnp.float32)]
    all_to_all x1 -> x0, blocking collectives: 60 us -> none  [per_device(): lax.all_to_all(found_rows, 'req', split_axis=0, concat_axis=0, tiled=True)]
    all_gather x2, waiting for transfers between devices: 72.1 us -> 13.8 us  [the longest x1 13.8 us: per_device(): lax.all_gather(jnp.concatenate([ffn_cols(tp_index), other_ffn], axis=1),...]
    ppermute x0 -> x9, starting transfers between devices: none -> 13.3 us  [the longest x4 4.05 us: per_device(): lax.ppermute(part, 'tp', PAIR).astype(jnp.float32)]
    scatter x1 -> x0, local copies, waits for them, and re-layouts: 12.8 us -> none  [per_device(): jnp.full((group_count, capacity), -1, jnp.int32).at[owner_of, slot_of]]
    gather x2 -> x0, local copies, waits for them, and re-layouts: 12.6 us -> none  [the longest x1 7.96 us: per_device(): jnp.take(embed_table, jnp.maximum(lax.all_to_all(requests, 'req', split_a...]
  transfers between devices with their start and end apart: 5 -> 12, of which waited for: 5 -> 10; matrix products, arithmetic and copies ran while one was open for 7% -> 18% of each run, Pallas kernels for 0% -> 0%
where the time goes in v1:
time: 262 us; the launch traced here: 261 us
  waiting for transfers between devices  138 us (53%)
  matrix products  51.8 us (20%)
  starting transfers between devices  17.4 us (7%)
  other arithmetic  14.9 us (6%)
  between operations  14.4 us (5%)
  local copies, waits for them, and re-layouts  12.6 us (5%)
  blocking collectives  12 us (5%)
    all_to_all x1, waiting for transfers between devices, per_device(): lax.all_to_all(found_rows.reshape(group_count, capacity, width), 'req', s...  39 us
    ppermute x4, waiting for transfers between devices, per_device(): lax.ppermute(part, 'tp', PAIR).astype(jnp.float32)  28.7 us
    ppermute x1, waiting for transfers between devices, per_device(): embedded_other = lax.ppermute(embedded_own, 'tp', PAIR)  26.2 us
    ppermute x1, waiting for transfers between devices, per_device(): attended_other = lax.ppermute(attended, 'tp', PAIR)  17.9 us
    all_gather x1, waiting for transfers between devices, per_device(): lax.all_gather(jnp.concatenate([ffn_cols(tp_index), other_ffn], axis=1),...  13.8 us
    all_to_all x1, blocking collectives, per_device(): lax.all_to_all(requests, 'req', split_axis=0, concat_axis=0, tiled=True)  12 us
    dot_general x4, matrix products, per_device(): jnp.dot(hidden, down_weight[:, c * step:(c + 1) * step], preferred_elemen...  11 us
    dot_general x2, matrix products, two_part_dot(): jnp.dot(other, right[:, width:], preferred_element_type=jnp.float32)  9.05 us
  transfers between devices with their start and end apart: 12, of which 10 were waited for; matrix products, arithmetic and copies ran while one was open for 18% of the time, Pallas kernels for 0%

profile of v1, /device:TPU:0, one launch (start us, length us, event | category | flops | bytes accessed | tf_op | source)
XLA Modules:
  0.0 261.1 jit_solution(12481638949398354279)
XLA Ops:
  7.2 1.0 dynamic-slice_convert_fusion.5
  8.2 1.0 dynamic-slice_convert_fusion.9
  9.3 3.0 %collective-permute-start.1 = (bf16[48,1536]{1,0:T(8,128)(2,1)S(1)}, bf16[48,1536]{1,0:T(8,128)(2,1)S(1)}, u32[]{:S(2)}, u32[]{:S(2)}) collective-permute-start(bf16[48,1536]{1,0:T(8,128)(2,1)S(1)} %pad_maximum_fusion.13), channel_id=1, source_target_pairs={{0,16},{16,0},{1,17},{17,1},{2,18},{18,2},{3,19},{19,3},{4,20},{20... | collective-permute-start | bytes 442376 | tf_op jit(solution)/shard_map/ppermute | solution.py:133
  12.3 3.8 %collective-permute-done.1 = bf16[48,1536]{1,0:T(8,128)(2,1)S(1)} collective-permute-done((bf16[48,1536]{1,0:T(8,128)(2,1)S(1)}, bf16[48,1536]{1,0:T(8,128)(2,1)S(1)}, u32[]{:S(2)}, u32[]{:S(2)}) %collective-permute-start.1) | collective-permute-done | bytes 147488 | tf_op jit(solution)/shard_map/ppermute | solution.py:133
  17.0 1.5 dynamic-slice_convert_fusion.3
  18.5 1.8 collective-permute-start.4
  20.3 8.6 %collective-permute-done.4 = bf16[48,4096]{1,0:T(8,128)(2,1)S(1)} collective-permute-done((bf16[48,4096]{1,0:T(8,128)(2,1)S(1)}, bf16[48,4096]{1,0:T(8,128)(2,1)S(1)}, u32[]{:S(2)}, u32[]{:S(2)}) %collective-permute-start.4) | collective-permute-done | bytes 393248 | tf_op jit(solution)/shard_map/ppermute | solution.py:137
  28.9 1.0 pad_maximum_fusion.3
  30.4 12.0 %all_to_all.11 = s32[16,1,32]{2,1,0:T(1,128)S(1)} all-to-all(s32[16,1,32]{2,1,0:T(1,128)S(1)} %sub.49), channel_id=1, replica_groups=mesh['tp'=2,'req'=16] {'req'}, dimensions={0} | all-to-all | bytes 4096 | tf_op jit(solution)/shard_map/all_to_all | solution.py:159
  43.7 7.7 %fusion.19 = bf16[512,1536]{1,0:T(8,128)(2,1)} fusion(bf16[2000,1536]{1,0:T(8,128)(2,1)} %param.13, s32[512]{0:T(512)S(1)} %eq.98), kind=kOutput, calls=%fused_computation.28 | convolution fusion | flops 3147538432 | bytes 7718912 | tf_op jit(solution)/shard_map/dot_general | solution.py:163
  51.4 4.0 %all-to-all-start.1 = ((bf16[16,32,1536]{2,1,0:T(8,128)(2,1)}), bf16[16,32,1536]{2,1,0:T(8,128)(2,1)S(1)}, u32[]{:S(2)}, u32[]{:S(2)}) async-start(bf16[16,32,1536]{2,1,0:T(8,128)(2,1)} %bitcast), calls=%async_computation.1 | async-start | bytes 3145728 | tf_op jit(solution)/shard_map/all_to_all | solution.py:166
  55.4 1.3 collective-permute-start.3
  57.1 39.0 %all-to-all-done.1 = bf16[16,32,1536]{2,1,0:T(8,128)(2,1)S(1)} async-done(((bf16[16,32,1536]{2,1,0:T(8,128)(2,1)}), bf16[16,32,1536]{2,1,0:T(8,128)(2,1)S(1)}, u32[]{:S(2)}, u32[]{:S(2)}) %all-to-all-start.1) | async-done | bytes 1572896 | tf_op jit(solution)/shard_map/all_to_all | solution.py:166
  96.7 1.5 collective-permute-start
  99.6 26.2 %collective-permute-done = bf16[256,1536]{1,0:T(8,128)(2,1)S(1)} collective-permute-done((bf16[256,1536]{1,0:T(8,128)(2,1)S(1)}, bf16[256,1536]{1,0:T(8,128)(2,1)S(1)}, u32[]{:S(2)}, u32[]{:S(2)}) %collective-permute-start) | collective-permute-done | bytes 786464 | tf_op jit(solution)/shard_map/ppermute | solution.py:179
  127.5 3.2 %fusion.20 = f32[512,1536]{1,0:T(8,128)S(1)} fusion(bf16[768,3072]{1,0:T(8,128)(2,1)} %all-gather.3.cloned.1.call-done, bf16[512,1536]{1,0:T(8,128)(2,1)S(1)} %fusion.18, s32[]{:T(128)S(6)} %select_n.79), kind=kOutput, calls=%fused_computation.30 | convolution fusion | flops 1207959552 | bytes 6291460 | tf_op jit(solution)/shard_map/dot_general | solution.py:76
  130.7 1.4 convolution_add_fusion
  132.1 1.0 slice.87
  133.2 0.9 copy-done.5
  134.7 1.4 copy.35
  136.1 1.0 subtract_convert_fusion
  137.2 1.4 slice.152
  138.8 7.3 %fusion.74 = (f32[4,2,512]{2,1,0:T(2,128)S(1)}, f32[4,2,512,512]{2,3,1,0:T(8,128)}) fusion(pred[512,512]{0,1:T(8,128)(4,1)} %fusion.45, bf16[512,4,2,48]{0,3,2,1:T(8,128)(2,1)} %bitcast.66, bf16[512,4,2,48]{0,3,2,1:T(8,128)(2,1)S(1)} %bitcast.65, bf16[512,4,48]{0,2,1:T(8,128)(2,1)S(1)} %get-tuple-element.19, bf16[512,4,48]{0,2,1:T(8,128)(2,1)S(1)} %get-tuple-element.18), kind=kOutput, calls=%fused_computation.123 | convolution fusion | flops 413401600 | bytes 9846784 | tf_op jit(solution)/shard_map/sub | solution.py:60
  146.1 4.2 %fusion.32 = bf16[4,96,2,512]{3,1,2,0:T(8,128)(2,1)S(1)} fusion(bf16[512,4,96,1]{0,2,3,1:T(8,128)(2,1)S(1)} %bitcast.67, f32[4,2,512,512]{2,3,1,0:T(8,128)} %get-tuple-element.29, f32[4,2,512]{2,1,0:T(2,128)S(1)} %get-tuple-element.28), kind=kOutput, calls=%fused_computation.44 | convolution fusion | flops 407240704 | bytes 9584640 | tf_op jit(solution)/shard_map/kgqs,skd->qkgd/dot_general | solution.py:62
  150.3 1.5 collective-permute-start.2
  151.9 17.9 %collective-permute-done.2 = bf16[512,768]{0,1:T(8,128)(2,1)S(1)} collective-permute-done((bf16[512,768]{0,1:T(8,128)(2,1)S(1)}, bf16[512,768]{0,1:T(8,128)(2,1)S(1)}, u32[]{:S(2)}, u32[]{:S(2)}) %collective-permute-start.2) | collective-permute-done | bytes 786464 | tf_op jit(solution)/shard_map/ppermute | solution.py:199
  169.8 3.1 %fusion.79 = f32[512,1536]{1,0:T(8,128)S(1)} fusion(bf16[512,768]{0,1:T(8,128)(2,1)S(1)} %collective-permute-done.2, bf16[768,1536]{1,0:T(8,128)(2,1)} %collective-permute-done.3), kind=kOutput, calls=%fused_computation.125 | convolution fusion | flops 1207959552 | bytes 6291456 | tf_op jit(solution)/shard_map/dot_general | solution.py:203
  172.9 1.9 multiply_reduce_fusion
  174.8 1.5 multiply_convert_fusion
  176.3 13.8 %all-gather.5.cloned.1.call-done = bf16[768,8192]{1,0:T(8,128)(2,1)} async-done(((bf16[48,8192]{1,0:T(8,128)(2,1)}), bf16[768,8192]{1,0:T(8,128)(2,1)}) %all-gather.5.cloned.1.call-update) | async-done | bytes 12582928 | tf_op jit(solution)/shard_map/all_gather | solution.py:138
  190.1 5.8 %fusion.2 = f32[512,4096]{1,0:T(8,128)S(1)} fusion(bf16[768,8192]{1,0:T(8,128)(2,1)} %all-gather.5.cloned.1.call-done, bf16[512,1536]{1,0:T(8,128)(2,1)} %multiply_convert_fusion, s32[]{:T(128)S(6)} %select_n.79), kind=kOutput, calls=%fused_computation.5 | convolution fusion | flops 3221225472 | bytes 15466500 | tf_op jit(solution)/shard_map/dot_general | solution.py:76
  195.9 5.5 %fusion.6 = f32[512,4096]{1,0:T(8,128)S(1)} fusion(f32[512,4096]{1,0:T(8,128)S(1)} %fusion.2, bf16[768,8192]{1,0:T(8,128)(2,1)} %all-gather.5.cloned.1.call-done, bf16[512,1536]{1,0:T(8,128)(2,1)S(1)} %copy-done.4, s32[]{:T(128)S(6)} %select_n.72), kind=kOutput, calls=%fused_computation.9 | convolution fusion | flops 3223322624 | bytes 23855108 | tf_op jit(solution)/shard_map/dot_general | solution.py:76
  201.5 1.2 fusion.9
  202.7 3.6 %fusion.42 = bf16[512,384]{1,0:T(8,128)(2,1)} fusion(bf16[512,2048]{1,0:T(8,128)(2,1)S(1)} %fusion.9, bf16[2048,1536]{1,0:T(8,128)(2,1)} %param.19), kind=kOutput, calls=%fused_computation.48 | convolution fusion | flops 805502976 | bytes 4063232 | tf_op jit(solution)/shard_map/dot_general | solution.py:212
  206.3 3.4 %fusion.39 = bf16[512,384]{1,0:T(8,128)(2,1)} fusion(bf16[512,2048]{1,0:T(8,128)(2,1)S(1)} %fusion.9, bf16[2048,1536]{1,0:T(8,128)(2,1)} %param.19), kind=kOutput, calls=%fused_computation.47 | convolution fusion | flops 805502976 | bytes 4063232 | tf_op jit(solution)/shard_map/dot_general | solution.py:212
  209.7 2.0 fusion.36
  211.7 2.0 fusion.33
  213.7 1.7 collective-permute-start.5
  215.8 1.7 collective-permute-start.7
  217.8 0.9 copy.42
  218.8 1.2 slice_bitcast_fusion
  219.9 2.0 pad_maximum_fusion.4
  221.9 4.1 %collective-permute-done.5 = bf16[512,384]{1,0:T(8,128)(2,1)} collective-permute-done((bf16[512,384]{1,0:T(8,128)(2,1)}, bf16[512,384]{1,0:T(8,128)(2,1)}, u32[]{:S(2)}, u32[]{:S(2)}) %collective-permute-start.5) | collective-permute-done | bytes 393248 | tf_op jit(solution)/shard_map/ppermute | solution.py:215
  226.0 8.4 %collective-permute-done.6 = bf16[512,384]{1,0:T(8,128)(2,1)} collective-permute-done((bf16[512,384]{1,0:T(8,128)(2,1)}, bf16[512,384]{1,0:T(8,128)(2,1)}, u32[]{:S(2)}, u32[]{:S(2)}) %collective-permute-start.6) | collective-permute-done | bytes 393248 | tf_op jit(solution)/shard_map/ppermute | solution.py:215
  234.4 8.4 %collective-permute-done.7 = bf16[512,384]{1,0:T(8,128)(2,1)} collective-permute-done((bf16[512,384]{1,0:T(8,128)(2,1)}, bf16[512,384]{1,0:T(8,128)(2,1)}, u32[]{:S(2)}, u32[]{:S(2)}) %collective-permute-start.7) | collective-permute-done | bytes 393248 | tf_op jit(solution)/shard_map/ppermute | solution.py:215
  242.8 7.8 %collective-permute-done.8 = bf16[512,384]{1,0:T(8,128)(2,1)} collective-permute-done((bf16[512,384]{1,0:T(8,128)(2,1)}, bf16[512,384]{1,0:T(8,128)(2,1)}, u32[]{:S(2)}, u32[]{:S(2)}) %collective-permute-start.8) | collective-permute-done | bytes 393248 | tf_op jit(solution)/shard_map/ppermute | solution.py:215
  250.6 2.3 fusion.51
  252.9 1.3 pad_maximum_fusion.1
  (77 shorter events, 8.3 us)
Async XLA Ops:
  7.2 120.3 %all-gather.3.cloned.1.call-start = ((), (), s32[]{:S(2)}) async-start(), calls=%async_computation.2 | async-start | bytes 5013504 | tf_op jit(solution)/shard_map/all_gather | solution.py:134
  8.2 21.6 %copy-start.13 = (s32[512]{0:T(512)S(1)}, s32[512]{0:T(512)}, u32[]{:S(2)}) copy-start(s32[512]{0:T(512)} %param.10) | copy-start | bytes 6148
  9.3 6.9 %collective-permute-start.1 = (bf16[48,1536]{1,0:T(8,128)(2,1)S(1)}, bf16[48,1536]{1,0:T(8,128)(2,1)S(1)}, u32[]{:S(2)}, u32[]{:S(2)}) collective-permute-start(bf16[48,1536]{1,0:T(8,128)(2,1)S(1)} %pad_maximum_fusion.13), channel_id=1, source_target_pairs={{0,16},{16,0},{1,17},{17,1},{2,18},{18,2},{3,19},{19,3},{4,20},{20... | collective-permute-start | bytes 442376 | tf_op jit(solution)/shard_map/ppermute | solution.py:133
  16.9 173.1 %all-gather.5.cloned.1.call-start = ((), (), s32[]{:S(2)}) async-start(), calls=%async_computation.3 | async-start | bytes 13369344 | tf_op jit(solution)/shard_map/all_gather | solution.py:138
  18.5 10.4 %collective-permute-start.4 = (bf16[48,4096]{1,0:T(8,128)(2,1)S(1)}, bf16[48,4096]{1,0:T(8,128)(2,1)S(1)}, u32[]{:S(2)}, u32[]{:S(2)}) collective-permute-start(bf16[48,4096]{1,0:T(8,128)(2,1)S(1)} %pad_maximum_fusion.11), channel_id=1, source_target_pairs={{0,16},{16,0},{1,17},{17,1},{2,18},{18,2},{3,19},{19,3},{4,20},{20... | collective-permute-start | bytes 1179656 | tf_op jit(solution)/shard_map/ppermute | solution.py:137
  51.4 5.4 %copy-start.16 = (s32[1,4]{1,0:T(1,128)S(1)}, s32[1,4]{1,0:T(1,128)}, u32[]{:S(2)}) copy-start(s32[1,4]{1,0:T(1,128)} %param.11) | copy-start | bytes 52
  51.4 5.6 %copy-start.12 = (s32[1,4]{1,0:T(1,128)S(1)}, s32[1,4]{1,0:T(1,128)}, u32[]{:S(2)}) copy-start(s32[1,4]{1,0:T(1,128)} %param.12) | copy-start | bytes 52
  51.4 44.7 %all-to-all-start.1 = ((bf16[16,32,1536]{2,1,0:T(8,128)(2,1)}), bf16[16,32,1536]{2,1,0:T(8,128)(2,1)S(1)}, u32[]{:S(2)}, u32[]{:S(2)}) async-start(bf16[16,32,1536]{2,1,0:T(8,128)(2,1)} %bitcast), calls=%async_computation.1 | async-start | bytes 3145728 | tf_op jit(solution)/shard_map/all_to_all | solution.py:166
  55.4 96.5 %collective-permute-start.3 = (bf16[768,1536]{1,0:T(8,128)(2,1)}, bf16[768,1536]{1,0:T(8,128)(2,1)}, u32[]{:S(2)}, u32[]{:S(2)}) collective-permute-start(bf16[768,1536]{1,0:T(8,128)(2,1)} %param.16), channel_id=1, source_target_pairs={{0,16},{16,0},{1,17},{17,1},{2,18},{18,2},{3,19},{19,3},{4,20},{20... | collective-permute-start | bytes 7077896 | tf_op jit(solution)/shard_map/ppermute | solution.py:141
  96.7 30.3 %copy-start.10 = (f32[1536]{0:T(1024)S(1)}, f32[1536]{0:T(1024)}, u32[]{:S(2)}) copy-start(f32[1536]{0:T(1024)} %param.14) | copy-start | bytes 18436
  96.7 29.1 %collective-permute-start = (bf16[256,1536]{1,0:T(8,128)(2,1)S(1)}, bf16[256,1536]{1,0:T(8,128)(2,1)S(1)}, u32[]{:S(2)}, u32[]{:S(2)}) collective-permute-start(bf16[256,1536]{1,0:T(8,128)(2,1)S(1)} %convolution_convert_fusion), channel_id=1, source_target_pairs={{0,16},{16,0},{1,17},{17,1},{2,18},{18,2},{3,19},{19,3},{4,20},{20... | collective-permute-start | bytes 2359304 | tf_op jit(solution)/shard_map/ppermute | solution.py:179
  125.9 0.9 copy-start
  125.9 1.1 copy-start.2
  127.5 3.2 %copy-start.14 = (bf16[768,3072]{1,0:T(8,128)(2,1)S(1)}, bf16[768,3072]{1,0:T(8,128)(2,1)}, u32[]{:S(2)}) copy-start(bf16[768,3072]{1,0:T(8,128)(2,1)} %all-gather.3.cloned.1.call-done) | copy-start | bytes 14155780
  132.1 2.0 copy-start.5
  137.2 8.9 %copy-start.6 = (bf16[512,4,48]{0,2,1:T(8,128)(2,1)}, bf16[512,4,48]{0,2,1:T(8,128)(2,1)S(1)}, u32[]{:S(2)}) copy-start(bf16[512,4,48]{0,2,1:T(8,128)(2,1)S(1)} %get-tuple-element.18) | copy-start | bytes 589828
  137.2 8.9 %copy-start.8 = (bf16[512,4,48]{0,2,1:T(8,128)(2,1)}, bf16[512,4,48]{0,2,1:T(8,128)(2,1)S(1)}, u32[]{:S(2)}) copy-start(bf16[512,4,48]{0,2,1:T(8,128)(2,1)S(1)} %get-tuple-element.19) | copy-start | bytes 589828
  150.3 22.6 %copy-start.1 = (bf16[256,1536]{1,0:T(8,128)(2,1)S(1)}, bf16[256,1536]{1,0:T(8,128)(2,1)}, u32[]{:S(2)}) copy-start(bf16[256,1536]{1,0:T(8,128)(2,1)} %copy-done) | copy-start | bytes 2359300
  150.3 22.6 %copy-start.3 = (bf16[256,1536]{1,0:T(8,128)(2,1)S(1)}, bf16[256,1536]{1,0:T(8,128)(2,1)}, u32[]{:S(2)}) copy-start(bf16[256,1536]{1,0:T(8,128)(2,1)} %copy-done.2) | copy-start | bytes 2359300
  150.3 22.6 %copy-start.15 = (bf16[768,1536]{1,0:T(8,128)(2,1)S(1)}, bf16[768,1536]{1,0:T(8,128)(2,1)}, u32[]{:S(2)}) copy-start(bf16[768,1536]{1,0:T(8,128)(2,1)} %param.16) | copy-start | bytes 7077892
  150.3 19.4 %collective-permute-start.2 = (bf16[512,768]{0,1:T(8,128)(2,1)S(1)}, bf16[512,768]{0,1:T(8,128)(2,1)S(1)}, u32[]{:S(2)}, u32[]{:S(2)}) collective-permute-start(bf16[512,768]{0,1:T(8,128)(2,1)S(1)} %bitcast.72), channel_id=1, source_target_pairs={{0,16},{16,0},{1,17},{17,1},{2,18},{18,2},{3,19},{19,3},{4,20},{20... | collective-permute-start | bytes 2359304 | tf_op jit(solution)/shard_map/ppermute | solution.py:199
  172.9 1.9 copy-start.11
  190.1 5.8 %copy-start.4 = (bf16[512,1536]{1,0:T(8,128)(2,1)S(1)}, bf16[512,1536]{1,0:T(8,128)(2,1)}, u32[]{:S(2)}) copy-start(bf16[512,1536]{1,0:T(8,128)(2,1)} %multiply_convert_fusion) | copy-start | bytes 4718596
  201.5 8.3 %slice-start = ((s8[6291456]{0:T(1024)(128)(4,1)}), s8[4194304]{0:T(1024)(128)(4,1)S(1)}, s32[]{:S(2)}) async-start(s8[6291456]{0:T(1024)(128)(4,1)} %bitcast.70), calls=%async_computation.4 | async-start | bytes 8388608
  202.7 7.0 %slice-start.1 = ((s8[6291456]{0:T(1024)(128)(4,1)}), s8[2097152]{0:T(1024)(128)(4,1)S(1)}, s32[]{:S(2)}) async-start(s8[6291456]{0:T(1024)(128)(4,1)} %bitcast.70), calls=%async_computation.5 | async-start | bytes 4194304
  211.7 6.1 %copy-start.7 = (bf16[512,4,48]{0,2,1:T(8,128)(2,1)S(1)}, bf16[512,4,48]{0,2,1:T(8,128)(2,1)}, u32[]{:S(2)}) copy-start(bf16[512,4,48]{0,2,1:T(8,128)(2,1)} %copy-done.6) | copy-start | bytes 589828
  211.7 6.1 %copy-start.9 = (bf16[512,4,48]{0,2,1:T(8,128)(2,1)S(1)}, bf16[512,4,48]{0,2,1:T(8,128)(2,1)}, u32[]{:S(2)}) copy-start(bf16[512,4,48]{0,2,1:T(8,128)(2,1)} %copy-done.8) | copy-start | bytes 589828
  213.7 12.3 %collective-permute-start.5 = (bf16[512,384]{1,0:T(8,128)(2,1)}, bf16[512,384]{1,0:T(8,128)(2,1)}, u32[]{:S(2)}, u32[]{:S(2)}) collective-permute-start(bf16[512,384]{1,0:T(8,128)(2,1)} %fusion.33), channel_id=1, source_target_pairs={{0,16},{16,0},{1,17},{17,1},{2,18},{18,2},{3,19},{19,3},{4,20},{20... | collective-permute-start | bytes 1179656 | tf_op jit(solution)/shard_map/ppermute | solution.py:215
  215.4 19.0 %collective-permute-start.6 = (bf16[512,384]{1,0:T(8,128)(2,1)}, bf16[512,384]{1,0:T(8,128)(2,1)}, u32[]{:S(2)}, u32[]{:S(2)}) collective-permute-start(bf16[512,384]{1,0:T(8,128)(2,1)} %fusion.36), channel_id=1, source_target_pairs={{0,16},{16,0},{1,17},{17,1},{2,18},{18,2},{3,19},{19,3},{4,20},{20... | collective-permute-start | bytes 1179656 | tf_op jit(solution)/shard_map/ppermute | solution.py:215
  215.8 27.1 %collective-permute-start.7 = (bf16[512,384]{1,0:T(8,128)(2,1)}, bf16[512,384]{1,0:T(8,128)(2,1)}, u32[]{:S(2)}, u32[]{:S(2)}) collective-permute-start(bf16[512,384]{1,0:T(8,128)(2,1)} %fusion.39), channel_id=1, source_target_pairs={{0,16},{16,0},{1,17},{17,1},{2,18},{18,2},{3,19},{19,3},{4,20},{20... | collective-permute-start | bytes 1179656 | tf_op jit(solution)/shard_map/ppermute | solution.py:215
  217.5 33.2 %collective-permute-start.8 = (bf16[512,384]{1,0:T(8,128)(2,1)}, bf16[512,384]{1,0:T(8,128)(2,1)}, u32[]{:S(2)}, u32[]{:S(2)}) collective-permute-start(bf16[512,384]{1,0:T(8,128)(2,1)} %fusion.42), channel_id=1, source_target_pairs={{0,16},{16,0},{1,17},{17,1},{2,18},{18,2},{3,19},{19,3},{4,20},{20... | collective-permute-start | bytes 1179656 | tf_op jit(solution)/shard_map/ppermute | solution.py:215
Sparse Core Ops, SparseCore 0:
  17.1 65.8 all-gather.2
  85.2 104.8 all-gather.4

commit v2 on v0

v2 whole, which is shorter than its diff:
```python
import functools
import math

import jax
import jax.numpy as jnp
from jax import lax
from jax.experimental import pallas as pl
from jax.experimental.pallas import tpu as pltpu
from jax.sharding import PartitionSpec as P

HEAD_DIM = 96
HALF = HEAD_DIM // 2
LANES = 128

rope_base = 100000.0
norm_eps = 1e-05

BF = jnp.bfloat16
F32 = jnp.float32
PAIR = [(0, 1), (1, 0)]
VMEM_LIMIT = 48 * 1024 * 1024


def token_layout(lengths, tenants, row_count):
    positions = jnp.arange(row_count, dtype=jnp.int32)
    ends, offset, tenant, start = 0, positions, jnp.full_like(positions, 0), 0
    for i in range(lengths.shape[0]):
        inside = positions >= start
        offset = jnp.where(inside, positions - start, offset)
        tenant = jnp.where(inside, tenants[i], tenant)
        start = start + lengths[i]
    return (offset, tenant)


def chip_ring(chips):
    order = list(range(0, chips, 2)) + list(range(chips - 1 - chips % 2, 0, -2))
    following = {order[i]: order[(i + 1) % chips] for i in range(chips)}
    pairs = [(2 * c, 2 * d) for c, d in following.items()]
    pairs += [(2 * d + 1, 2 * c + 1) for c, d in following.items()]
    return order, pairs


def ring_gather(block, pairs, chips):
    blocks = [block]
    for _ in range(chips - 1):
        blocks.append(lax.ppermute(blocks[-1], "req", pairs))
    return blocks


def whole(shape):
    return pl.BlockSpec(shape, lambda: (0,) * len(shape), memory_space=pltpu.VMEM)


def in_vmem(count):
    return [pl.BlockSpec(memory_space=pltpu.VMEM)] * count


def params():
    return pltpu.CompilerParams(vmem_limit_bytes=VMEM_LIMIT)


def spread_columns(heads):
    column = jnp.arange(heads * HEAD_DIM, dtype=jnp.int32)
    within = column % HEAD_DIM
    target = column // HEAD_DIM * LANES + jnp.where(within < HALF, within, within + 64 - HALF)
    return (target[:, None] == jnp.arange(heads * LANES, dtype=jnp.int32)[None, :]).astype(BF)


def prep_kernel(chips, place_ref, *refs):
    blocks = refs[: chips + 1]
    spread_ref, out_ref, raw, sems = refs[chips + 1 :]
    copies = []
    for s in range(chips):
        copies.append(pltpu.make_async_copy(blocks[s], raw.at[place_ref[s]], sems.at[s]))
    for s in range(chips):
        copies.append(
            pltpu.make_async_copy(
                blocks[chips].at[s], raw.at[place_ref[chips + s]], sems.at[chips + s]
            )
        )
    for copy in copies:
        copy.start()
    for copy in copies:
        copy.wait()
    count, rows, _ = raw.shape
    narrow, wide = spread_ref.shape
    for b in range(raw.shape[2] // narrow):
        part = raw[:, :, b * narrow : (b + 1) * narrow].reshape(count * rows, narrow)
        out_ref[:, b * wide : (b + 1) * wide] = jnp.dot(
            part, spread_ref[...], preferred_element_type=F32
        ).astype(BF)


def prepare_qkv(place, blocks, got, spread):
    chips = len(blocks)
    rows, cols = blocks[0].shape
    wide = cols // spread.shape[0] * spread.shape[1]
    return pl.pallas_call(
        functools.partial(prep_kernel, chips),
        out_shape=jax.ShapeDtypeStruct((2 * chips * rows, wide), BF),
        in_specs=[pl.BlockSpec(memory_space=pltpu.SMEM)]
        + [pl.BlockSpec(memory_space=pl.ANY)] * (chips + 1)
        + in_vmem(1),
        out_specs=pl.BlockSpec(memory_space=pltpu.VMEM),
        scratch_shapes=[
            pltpu.VMEM((2 * chips, rows, cols), BF),
            pltpu.SemaphoreType.DMA((2 * chips,)),
        ],
        compiler_params=params(),
        name="prepare_qkv",
        cost_estimate=pl.CostEstimate(
            flops=4 * chips * rows * cols * spread.shape[1],
            bytes_accessed=8 * chips * rows * cols,
            transcendentals=0,
        ),
    )(place, *blocks, got, spread)


def attention_kernel(
    q_heads,
    kv_heads,
    emb_ref,
    gain_ref,
    weight_ref,
    cos_ref,
    sin_ref,
    ten_col_ref,
    ten_row_ref,
    pack_ref,
    att_ref,
    cache_ref,
    normed,
    keys,
    values,
    mixed,
    bias,
):
    tokens = emb_ref.shape[0]
    step = tokens // 2
    group = q_heads // kv_heads
    for r in range(0, tokens, step):
        x = emb_ref[r : r + step, :].astype(F32)
        scale = lax.rsqrt(jnp.mean(x * x, axis=-1, keepdims=True) + norm_eps)
        normed[r : r + step, :] = (x * scale * gain_ref[...]).astype(BF)
        row = lax.broadcasted_iota(jnp.int32, (step, tokens), 0) + r
        col = lax.broadcasted_iota(jnp.int32, (step, tokens), 1)
        allowed = (col <= row) & (ten_col_ref[r : r + step, :] == ten_row_ref[...])
        bias[r : r + step, :] = jnp.where(allowed, 0.0, -1e30)

    def turned(x):
        return (x * cos_ref[...] + pltpu.roll(x, 64, 1) * sin_ref[...]).astype(BF)

    def project(first, heads):
        return jnp.dot(
            normed[...],
            weight_ref[:, first * LANES : (first + heads) * LANES],
            preferred_element_type=F32,
        )

    k_all = project(q_heads, kv_heads)
    for h in range(kv_heads):
        keys[:, h * LANES : (h + 1) * LANES] = turned(k_all[:, h * LANES : (h + 1) * LANES])
    values[...] = project(q_heads + kv_heads, kv_heads).astype(BF)
    factor = HEAD_DIM**-0.5 * math.log2(math.e)
    for kv in range(kv_heads):
        lanes = slice(kv * LANES, (kv + 1) * LANES)
        q_all = project(kv * group, group)
        for g in range(group):
            q = turned(q_all[:, g * LANES : (g + 1) * LANES])
            for r in range(0, tokens, step):
                seen = r + step
                scores = (
                    lax.dot_general(
                        q[r : r + step, :],
                        keys[:seen, lanes],
                        (((1,), (1,)), ((), ())),
                        preferred_element_type=F32,
                    )
                    + bias[r : r + step, :seen]
                )
                top = jnp.max(scores, axis=-1, keepdims=True)
                expo = jnp.exp2((scores - top) * factor)
                total = jnp.sum(expo, axis=-1, keepdims=True)
                out = jnp.dot(expo.astype(BF), values[:seen, lanes], preferred_element_type=F32)
                h = kv * group + g
                mixed[r : r + step, h * LANES : (h + 1) * LANES] = (out / total).astype(BF)
    wide, narrow = pack_ref.shape
    for b in range(q_heads * LANES // wide):
        att_ref[:, b * narrow : (b + 1) * narrow] = jnp.dot(
            mixed[:, b * wide : (b + 1) * wide], pack_ref[...], preferred_element_type=F32
        ).astype(BF)
    cache_ref[0] = jnp.dot(keys[...], pack_ref[...], preferred_element_type=F32).astype(BF)
    cache_ref[1] = jnp.dot(values[...], pack_ref[...], preferred_element_type=F32).astype(BF)


def attention(embedded, gain, weight, cosine, sine, tenant, pack, q_heads, kv_heads):
    tokens, width = embedded.shape
    return pl.pallas_call(
        functools.partial(attention_kernel, q_heads, kv_heads),
        out_shape=(
            jax.ShapeDtypeStruct((tokens, q_heads * HEAD_DIM), BF),
            jax.ShapeDtypeStruct((2, tokens, kv_heads * HEAD_DIM), BF),
        ),
        in_specs=in_vmem(8),
        out_specs=tuple(in_vmem(2)),
        scratch_shapes=[
            pltpu.VMEM((tokens, width), BF),
            pltpu.VMEM((tokens, kv_heads * LANES), BF),
            pltpu.VMEM((tokens, kv_heads * LANES), BF),
            pltpu.VMEM((tokens, q_heads * LANES), BF),
            pltpu.VMEM((tokens, tokens), F32),
        ],
        compiler_params=params(),
        name="attention",
        cost_estimate=pl.CostEstimate(
            flops=2 * tokens * width * weight.shape[1],
            bytes_accessed=2 * weight.size + 6 * embedded.size,
            transcendentals=q_heads * tokens * tokens,
        ),
    )(embedded, gain, weight, cosine, sine, tenant[:, None], tenant[None, :], pack)


def output_kernel(emb_ref, own_ref, other_ref, w_own_ref, w_other_ref, gain_ref, res_ref, norm_ref):
    tokens = emb_ref.shape[0]
    step = tokens // 4
    for r in range(0, tokens, step):
        rows = slice(r, r + step)
        x = (
            emb_ref[rows, :].astype(F32)
            + jnp.dot(own_ref[rows, :], w_own_ref[...], preferred_element_type=F32)
            + jnp.dot(other_ref[rows, :], w_other_ref[...], preferred_element_type=F32)
        )
        res_ref[rows, :] = x
        scale = lax.rsqrt(jnp.mean(x * x, axis=-1, keepdims=True) + norm_eps)
        norm_ref[rows, :] = (x * scale * gain_ref[...]).astype(BF)


def output_part(embedded, own, other, w_own, w_other, gain):
    tokens, width = embedded.shape
    return pl.pallas_call(
        output_kernel,
        out_shape=(
            jax.ShapeDtypeStruct((tokens, width), F32),
            jax.ShapeDtypeStruct((tokens, width), BF),
        ),
        in_specs=in_vmem(6),
        out_specs=tuple(in_vmem(2)),
        compiler_params=params(),
        name="output_part",
        cost_estimate=pl.CostEstimate(
            flops=8 * tokens * w_own.size // 2,
            bytes_accessed=4 * w_own.size + 8 * embedded.size,
            transcendentals=0,
        ),
    )(embedded, own, other, w_own, w_other, gain)


def hidden_kernel(chips, place_ref, x_ref, *refs):
    blocks = refs[: chips + 1]
    out_ref, buf, sems = refs[chips + 1 :]
    ff_half = out_ref.shape[1]
    _, _, count, rows, wide = buf.shape
    width = count * rows

    def copies(j):
        made = []
        for part in range(2):
            cols = pl.ds(part * ff_half + j * wide, wide)
            for s in range(2 * chips):
                source = (
                    blocks[s].at[:, cols] if s < chips else blocks[chips].at[s - chips, :, cols]
                )
                made.append(
                    pltpu.make_async_copy(
                        source, buf.at[j % 2, part, place_ref[s]], sems.at[j % 2, part, s]
                    )
                )
        return made

    steps = ff_half // wide
    pending = copies(0)
    for copy in pending:
        copy.start()
    for j in range(steps):
        current = pending
        if j + 1 < steps:
            pending = copies(j + 1)
            for copy in pending:
                copy.start()
        for copy in current:
            copy.wait()
        gate = jnp.dot(
            x_ref[...], buf[j % 2, 0].reshape(width, wide), preferred_element_type=F32
        )
        up = jnp.dot(x_ref[...], buf[j % 2, 1].reshape(width, wide), preferred_element_type=F32)
        out_ref[:, j * wide : (j + 1) * wide] = (gate / (1.0 + jnp.exp(-gate)) * up).astype(BF)


def hidden_part(place, normed, blocks, got):
    chips = len(blocks)
    rows, cols = blocks[0].shape
    tokens, width = normed.shape
    wide = min(512, cols // 2)
    return pl.pallas_call(
        functools.partial(hidden_kernel, chips),
        out_shape=jax.ShapeDtypeStruct((tokens, cols // 2), BF),
        in_specs=[pl.BlockSpec(memory_space=pltpu.SMEM)]
        + in_vmem(1)
        + [pl.BlockSpec(memory_space=pl.ANY)] * (chips + 1),
        out_specs=pl.BlockSpec(memory_space=pltpu.VMEM),
        scratch_shapes=[
            pltpu.VMEM((2, 2, 2 * chips, rows, wide), BF),
            pltpu.SemaphoreType.DMA((2, 2, 2 * chips)),
        ],
        compiler_params=params(),
        name="hidden_part",
        cost_estimate=pl.CostEstimate(
            flops=2 * tokens * width * cols,
            bytes_accessed=2 * width * cols + 4 * normed.size,
            transcendentals=tokens * cols // 2,
        ),
    )(place, normed, *blocks, got)


def per_device(
    token_ids,
    prompt_lengths,
    tenant_ids,
    embed_table,
    attention_gain,
    qkv_weight,
    out_weight,
    ffn_gain,
    gate_up_weight,
    down_weight,
):
    tp_count = lax.axis_size("tp")
    tp_index = lax.axis_index("tp")
    group_count = lax.axis_size("req")
    req_index = lax.axis_index("req")
    tokens = token_ids.shape[0]
    looked = tokens // tp_count
    own_rows, width = embed_table.shape
    capacity = max(2, 2 * looked // group_count)
    q_half = out_weight.shape[0]
    ff_half = down_weight.shape[0]
    q_full = q_half * tp_count
    kv_half = (qkv_weight.shape[1] - q_full) // (2 * tp_count)
    kv_full = kv_half * tp_count
    ff_full = ff_half * tp_count
    chips = group_count // 2
    core = req_index % 2
    chip = req_index // 2
    core_swap = [(i, i ^ 1) for i in range(group_count)]
    order, ring_pairs = chip_ring(chips)

    my_ids = lax.dynamic_slice_in_dim(token_ids, tp_index * looked, looked)
    owner_of = my_ids // own_rows
    row_in_range = my_ids - owner_of * own_rows
    earlier = jnp.arange(looked)[None, :] < jnp.arange(looked)[:, None]
    same = (owner_of[:, None] == owner_of[None, :]) & earlier
    place = owner_of * capacity + jnp.sum(same.astype(jnp.int32), axis=1)
    slots = jnp.arange(group_count * capacity, dtype=jnp.int32)
    chosen = place[None, :] == slots[:, None]
    requests = jnp.sum(jnp.where(chosen, row_in_range[None, :] + 1, 0), axis=1) - 1
    asked = lax.all_to_all(
        requests.reshape(group_count, capacity), "req", split_axis=0, concat_axis=0, tiled=True
    ).reshape(-1)

    def columns(weight, parts, half):
        return jnp.concatenate(
            [
                lax.dynamic_slice_in_dim(weight, base + half * size, size, axis=1)
                for base, size in parts
            ],
            axis=1,
        ).astype(BF)

    def chip_block(weight, parts):
        own = columns(weight, parts, tp_index)
        other = lax.ppermute(columns(weight, parts, 1 - tp_index), "tp", PAIR)
        kept = jnp.where(core == 0, own, other)
        moved = lax.ppermute(jnp.where(core == 0, other, own), "req", core_swap)
        return jnp.concatenate(
            [jnp.where(core == 0, kept, moved), jnp.where(core == 0, moved, kept)], axis=0
        )

    qkv_block = chip_block(
        qkv_weight, ((0, q_half), (q_full, kv_half), (q_full + kv_full, kv_half))
    )
    ffn_block = chip_block(gate_up_weight, ((0, ff_half), (ff_full, ff_half)))
    qkv_blocks = ring_gather(qkv_block, ring_pairs, chips)
    ffn_blocks = ring_gather(ffn_block, ring_pairs, chips)
    qkv_got = lax.ppermute(jnp.stack(qkv_blocks), "req", core_swap)
    ffn_got = lax.ppermute(jnp.stack(ffn_blocks), "req", core_swap)
    steps = jnp.arange(chips, dtype=jnp.int32)
    here = jnp.where(chip % 2 == 0, chip // 2, chips - 1 - chip // 2)

    def source_chip(position):
        position = position % chips
        return jnp.where(position < (chips + 1) // 2, 2 * position, 2 * (chips - 1 - position) + 1)

    up_chip, down_chip = source_chip(here - steps), source_chip(here + steps)
    mine_half = (tp_index + core) % 2
    spots = jnp.concatenate(
        [
            jnp.where(core == 0, up_chip, down_chip) + mine_half * chips,
            jnp.where(core == 0, down_chip, up_chip) + (1 - mine_half) * chips,
        ]
    )

    out_other = lax.ppermute(out_weight, "tp", PAIR)

    pick_rows = (asked[:, None] == jnp.arange(own_rows, dtype=jnp.int32)[None, :]).astype(BF)
    found_rows = jnp.dot(pick_rows, embed_table, preferred_element_type=F32).astype(BF)
    returned = lax.all_to_all(
        found_rows.reshape(group_count, capacity, width),
        "req",
        split_axis=0,
        concat_axis=0,
        tiled=True,
    ).reshape(group_count * capacity, width)
    pick_mine = (place[:, None] == slots[None, :]).astype(BF)
    embedded_own = jnp.dot(pick_mine, returned, preferred_element_type=F32).astype(BF)
    embedded_other = lax.ppermute(embedded_own, "tp", PAIR)
    embedded = jnp.concatenate(
        [
            jnp.where(tp_index == 0, embedded_own, embedded_other),
            jnp.where(tp_index == 0, embedded_other, embedded_own),
        ],
        axis=0,
    )

    offset, tenant = token_layout(prompt_lengths[0], tenant_ids[0], tokens)
    lane = jnp.arange(LANES, dtype=jnp.int32)
    index = lane % 64
    frequency = rope_base ** (-2.0 * index.astype(F32) / HEAD_DIM)
    angles = offset.astype(F32)[:, None] * frequency[None, :]
    cosine = jnp.cos(angles)
    sine = jnp.where(lane < 64, -1.0, 1.0)[None, :] * jnp.sin(angles)

    kv_local = kv_half // HEAD_DIM
    spread = spread_columns(kv_local)
    weight = prepare_qkv(spots, qkv_blocks, qkv_got, spread)
    attended, kv_cache = attention(
        embedded,
        attention_gain[None, :],
        weight,
        cosine,
        sine,
        tenant,
        spread.T,
        q_half // HEAD_DIM,
        kv_local,
    )
    attended_other = lax.ppermute(attended, "tp", PAIR)
    residual, normed_ffn = output_part(
        embedded, attended, attended_other, out_weight, out_other, ffn_gain[None, :]
    )
    hidden = hidden_part(spots, normed_ffn, ffn_blocks, ffn_got)
    chunks = 4
    step = width // chunks
    finals = []
    for c in range(chunks):
        cols = slice(c * step, (c + 1) * step)
        part = jnp.dot(hidden, down_weight[:, cols], preferred_element_type=F32).astype(BF)
        total = part.astype(F32) + lax.ppermute(part, "tp", PAIR).astype(F32)
        finals.append((residual[:, cols] + total).astype(BF))
    return (jnp.concatenate(finals, axis=1), kv_cache)


def solution(mesh):
    return jax.shard_map(
        per_device,
        mesh=mesh,
        in_specs=(
            P("req"),
            P("req", None),
            P("req", None),
            P("req", None),
            P(),
            P(("tp", "req"), None),
            P("tp", None),
            P(),
            P(("tp", "req"), None),
            P("tp", None),
        ),
        out_specs=(P("req", None), P(None, "req", "tp")),
        check_vma=False,
    )
```

time: 531 us -> 328 us (0.62)
  waiting for transfers between devices: 325 us -> 172 us
  blocking collectives: 73.7 us -> 0 us
  starting transfers between devices: 10.4 us -> 55.3 us
  Pallas kernels: 0 us -> 41.8 us
  local copies, waits for them, and re-layouts: 41.4 us -> 18.5 us
  matrix products: 40.4 us -> 21 us
  between operations: 15.9 us -> 3.02 us
  other arithmetic: 22.7 us -> 16.4 us
    ppermute x0 -> x27, waiting for transfers between devices: none -> 172 us  [the longest x14 105 us: ring_gather(): blocks.append(lax.ppermute(blocks[-1], 'req', pairs))]
    all_to_all x1 -> x2, waiting for transfers between devices: 149 us -> 0.01 us  [the longest x1 0.01 us: per_device(): lax.all_to_all(requests.reshape(group_count, capacity), 'req', split_axis...]
    psum x2 -> x0, waiting for transfers between devices: 104 us -> none  [the longest x1 55.3 us: per_device(): lax.psum(jnp.dot(attended, out_weight, preferred_element_type=jnp.float32...]
    all_to_all x2 -> x0, blocking collectives: 73.7 us -> none  [the longest x1 60 us: per_device(): lax.all_to_all(found_rows, 'req', split_axis=0, concat_axis=0, tiled=True)]
    all_gather x2 -> x0, waiting for transfers between devices: 72.1 us -> none  [the longest x1 47.1 us: per_device(): lax.all_gather(returned[owner_of, slot_of], 'tp', axis=0, tiled=True)]
    ppermute x0 -> x27, starting transfers between devices: none -> 43.9 us  [the longest x14 31.7 us: ring_gather(): blocks.append(lax.ppermute(blocks[-1], 'req', pairs))]
    pallas_call x0 -> x4, Pallas kernels: none -> 41.8 us  [the longest x1 13.9 us: attention(): pl.pallas_call(functools.partial(attention_kernel, q_heads, kv_heads), ou...]
    scatter x1 -> x0, local copies, waits for them, and re-layouts: 12.8 us -> none  [per_device(): jnp.full((group_count, capacity), -1, jnp.int32).at[owner_of, slot_of]]
  transfers between devices with their start and end apart: 5 -> 29, of which waited for: 5 -> 18; matrix products, arithmetic and copies ran while one was open for 7% -> 12% of each run, Pallas kernels for 0% -> 9%
where the time goes in v2:
time: 328 us
  waiting for transfers between devices  172 us (52%)
  starting transfers between devices  55.3 us (17%)
  Pallas kernels  41.8 us (13%)
  matrix products  21 us (6%)
  local copies, waits for them, and re-layouts  18.5 us (6%)
  other arithmetic  16.4 us (5%)
    ppermute x14, waiting for transfers between devices, ring_gather(): blocks.append(lax.ppermute(blocks[-1], 'req', pairs))  105 us
    ppermute x14, starting transfers between devices, ring_gather(): blocks.append(lax.ppermute(blocks[-1], 'req', pairs))  31.7 us
    ppermute x4, waiting for transfers between devices, per_device(): total = part.astype(F32) + lax.ppermute(part, 'tp', PAIR).astype(F32)  31.1 us
    ppermute x1, waiting for transfers between devices, per_device(): attended_other = lax.ppermute(attended, 'tp', PAIR)  17.5 us
    ppermute x1, waiting for transfers between devices, per_device(): embedded_other = lax.ppermute(embedded_own, 'tp', PAIR)  16.4 us
    pallas_call x1, Pallas kernels, attention(): pl.pallas_call(functools.partial(attention_kernel, q_heads, kv_heads), ou...  13.9 us
    pallas_call x1, Pallas kernels, hidden_part(): pl.pallas_call(functools.partial(hidden_kernel, chips), out_shape=jax.Sha...  13 us
    unnamed x84, local copies, waits for them, and re-layouts  12.5 us
  transfers between devices with their start and end apart: 29, of which 18 were waited for; matrix products, arithmetic and copies ran while one was open for 12% of the time, Pallas kernels for 9%

profile of v2, /device:TPU:0, one launch (start us, length us, event | category | flops | bytes accessed | tf_op | source)
XLA Modules:
  0.0 327.8 jit_solution(10420805756101258458)
XLA Ops:
  0.7 1.5 dynamic-slice_convert_fusion.3
  2.2 3.0 collective-permute-start.13
  6.6 6.4 %all-to-all-start = ((s32[16,1,32]{2,1,0:T(1,128)}), s32[16,1,32]{2,1,0:T(1,128)S(1)}, u32[]{:S(2)}, u32[]{:S(2)}) async-start(s32[16,1,32]{2,1,0:T(1,128)} %sub.87), calls=%async_computation | async-start | bytes 16384 | tf_op jit(solution)/shard_map/all_to_all | solution.py:366
  13.0 1.6 collective-permute-start.12
  17.0 1.3 collective-permute-done.1
  21.6 2.2 collective-permute-start.3
  24.1 7.4 %fusion.1 = bf16[512,1536]{1,0:T(8,128)(2,1)} fusion(bf16[2000,1536]{1,0:T(8,128)(2,1)} %param.13, s32[512]{0:T(512)S(1)} %eq.114), kind=kOutput, calls=%fused_computation.2 | convolution fusion | flops 3147538432 | bytes 7718912 | tf_op jit(solution)/shard_map/dot_general | solution.py:415
  31.5 5.0 %all-to-all-start.1 = ((bf16[16,32,1536]{2,1,0:T(8,128)(2,1)}), bf16[16,32,1536]{2,1,0:T(8,128)(2,1)}, u32[]{:S(2)}, u32[]{:S(2)}) async-start(bf16[16,32,1536]{2,1,0:T(8,128)(2,1)} %bitcast), calls=%async_computation.1 | async-start | bytes 3145728 | tf_op jit(solution)/shard_map/all_to_all | solution.py:416
  37.2 1.9 collective-permute-start.4
  39.4 1.5 collective-permute-start.15
  42.6 23.6 %collective-permute-done.4.refs_2_ = bf16[96,1536]{1,0:T(8,128)(2,1)S(1)} collective-permute-done((bf16[96,1536]{1,0:T(8,128)(2,1)S(1)}, bf16[96,1536]{1,0:T(8,128)(2,1)S(1)}, u32[]{:S(2)}, u32[]{:S(2)}) %collective-permute-start.4) | collective-permute-done | bytes 294944 | tf_op jit(solution)/shard_map/ppermute | solution.py:46
  66.1 10.1 %collective-permute-start.5 = (bf16[96,1536]{1,0:T(8,128)(2,1)S(1)}, bf16[96,1536]{1,0:T(8,128)(2,1)S(1)}, u32[]{:S(2)}, u32[]{:S(2)}) collective-permute-start(bf16[96,1536]{1,0:T(8,128)(2,1)S(1)} %collective-permute-done.4.refs_2_), channel_id=1, source_target_pairs={{0,4},{4,8},{8,12},{12,14},{14,10},{10,6},{6,2},{2,0},{5,1},{9,5},... | collective-permute-start | bytes 884744 | tf_op jit(solution)/shard_map/ppermute | solution.py:46
  76.2 8.4 %collective-permute-start.16 = (bf16[96,4096]{1,0:T(8,128)(2,1)S(1)}, bf16[96,4096]{1,0:T(8,128)(2,1)S(1)}, u32[]{:S(2)}, u32[]{:S(2)}) collective-permute-start(bf16[96,4096]{1,0:T(8,128)(2,1)S(1)} %collective-permute-done.15.refs_1_), channel_id=1, source_target_pairs={{0,4},{4,8},{8,12},{12,14},{14,10},{10,6},{6,2},{2,0},{5,1},{9,5},... | collective-permute-start | bytes 2359304 | tf_op jit(solution)/shard_map/ppermute | solution.py:46
  85.7 8.5 %collective-permute-done.16.refs_2_ = bf16[96,4096]{1,0:T(8,128)(2,1)S(1)} collective-permute-done((bf16[96,4096]{1,0:T(8,128)(2,1)S(1)}, bf16[96,4096]{1,0:T(8,128)(2,1)S(1)}, u32[]{:S(2)}, u32[]{:S(2)}) %collective-permute-start.16) | collective-permute-done | bytes 786464 | tf_op jit(solution)/shard_map/ppermute | solution.py:46
  94.1 2.5 collective-permute-start.17
  97.6 10.3 %collective-permute-done.17.refs_3_ = bf16[96,4096]{1,0:T(8,128)(2,1)S(1)} collective-permute-done((bf16[96,4096]{1,0:T(8,128)(2,1)S(1)}, bf16[96,4096]{1,0:T(8,128)(2,1)S(1)}, u32[]{:S(2)}, u32[]{:S(2)}) %collective-permute-start.17) | collective-permute-done | bytes 786464 | tf_op jit(solution)/shard_map/ppermute | solution.py:46
  109.6 10.4 %collective-permute-done.18.refs_4_ = bf16[96,4096]{1,0:T(8,128)(2,1)S(1)} collective-permute-done((bf16[96,4096]{1,0:T(8,128)(2,1)S(1)}, bf16[96,4096]{1,0:T(8,128)(2,1)S(1)}, u32[]{:S(2)}, u32[]{:S(2)}) %collective-permute-start.18) | collective-permute-done | bytes 786464 | tf_op jit(solution)/shard_map/ppermute | solution.py:46
  121.6 10.4 %collective-permute-done.19.refs_5_ = bf16[96,4096]{1,0:T(8,128)(2,1)S(1)} collective-permute-done((bf16[96,4096]{1,0:T(8,128)(2,1)S(1)}, bf16[96,4096]{1,0:T(8,128)(2,1)S(1)}, u32[]{:S(2)}, u32[]{:S(2)}) %collective-permute-start.19) | collective-permute-done | bytes 786464 | tf_op jit(solution)/shard_map/ppermute | solution.py:46
  133.5 10.4 %collective-permute-done.20.refs_6_ = bf16[96,4096]{1,0:T(8,128)(2,1)S(1)} collective-permute-done((bf16[96,4096]{1,0:T(8,128)(2,1)S(1)}, bf16[96,4096]{1,0:T(8,128)(2,1)S(1)}, u32[]{:S(2)}, u32[]{:S(2)}) %collective-permute-start.20) | collective-permute-done | bytes 786464 | tf_op jit(solution)/shard_map/ppermute | solution.py:46
  145.6 10.4 %collective-permute-done.21.refs_7_ = bf16[96,4096]{1,0:T(8,128)(2,1)S(1)} collective-permute-done((bf16[96,4096]{1,0:T(8,128)(2,1)S(1)}, bf16[96,4096]{1,0:T(8,128)(2,1)S(1)}, u32[]{:S(2)}, u32[]{:S(2)}) %collective-permute-start.21) | collective-permute-done | bytes 786464 | tf_op jit(solution)/shard_map/ppermute | solution.py:46
  159.1 5.3 %collective-permute-done.6.refs_4_ = bf16[96,1536]{1,0:T(8,128)(2,1)S(1)} collective-permute-done((bf16[96,1536]{1,0:T(8,128)(2,1)S(1)}, bf16[96,1536]{1,0:T(8,128)(2,1)S(1)}, u32[]{:S(2)}, u32[]{:S(2)}) %collective-permute-start.6) | collective-permute-done | bytes 294944 | tf_op jit(solution)/shard_map/ppermute | solution.py:46
  165.9 5.3 %collective-permute-done.7.refs_5_ = bf16[96,1536]{1,0:T(8,128)(2,1)S(1)} collective-permute-done((bf16[96,1536]{1,0:T(8,128)(2,1)S(1)}, bf16[96,1536]{1,0:T(8,128)(2,1)S(1)}, u32[]{:S(2)}, u32[]{:S(2)}) %collective-permute-start.7) | collective-permute-done | bytes 294944 | tf_op jit(solution)/shard_map/ppermute | solution.py:46
  172.6 5.3 %collective-permute-done.8.refs_6_ = bf16[96,1536]{1,0:T(8,128)(2,1)S(1)} collective-permute-done((bf16[96,1536]{1,0:T(8,128)(2,1)S(1)}, bf16[96,1536]{1,0:T(8,128)(2,1)S(1)}, u32[]{:S(2)}, u32[]{:S(2)}) %collective-permute-start.8) | collective-permute-done | bytes 294944 | tf_op jit(solution)/shard_map/ppermute | solution.py:46
  179.3 5.3 %collective-permute-done.9.refs_7_ = bf16[96,1536]{1,0:T(8,128)(2,1)S(1)} collective-permute-done((bf16[96,1536]{1,0:T(8,128)(2,1)S(1)}, bf16[96,1536]{1,0:T(8,128)(2,1)S(1)}, u32[]{:S(2)}, u32[]{:S(2)}) %collective-permute-start.9) | collective-permute-done | bytes 294944 | tf_op jit(solution)/shard_map/ppermute | solution.py:46
  186.7 3.1 compare_select_fusion.2.ten_row_ref
  189.8 3.8 %select_select_fusion.ten_col_ref = s32[512,1]{1,0:T(8,128)} fusion(s32[]{:T(128)} %bitcast.16, s32[]{:T(128)} %bitcast.15, s32[]{:T(128)} %bitcast.10, s32[]{:T(128)} %bitcast.14, s32[]{:T(128)S(6)} %add.233, s32[]{:T(128)} %bitcast.13, s32[]{:T(128)S(6)} %add.234), kind=kLoop, calls=%fused_computation.63 | loop fusion | flops 3072 | bytes 2076 | tf_op jit(solution)/shard_map/jit(_where)/select_n | solution.py:30
  193.6 2.0 convolution_convert_fusion
  195.7 1.6 collective-permute-start
  197.5 1.7 fusion.25
  199.3 16.4 %collective-permute-done = bf16[256,1536]{1,0:T(8,128)(2,1)S(1)} collective-permute-done((bf16[256,1536]{1,0:T(8,128)(2,1)S(1)}, bf16[256,1536]{1,0:T(8,128)(2,1)S(1)}, u32[]{:S(2)}, u32[]{:S(2)}) %collective-permute-start) | collective-permute-done | bytes 786464 | tf_op jit(solution)/shard_map/ppermute | solution.py:425
  217.0 8.0 %prepare_qkv.1.weight_ref = bf16[1536,2048]{1,0:T(8,128)(2,1)} custom-call(s32[16]{0:T(128)S(1)} %pad_add_fusion.place_ref, bf16[96,1536]{1,0:T(8,128)(2,1)S(1)} %pad_maximum_fusion.5.refs_0_, bf16[96,1536]{1,0:T(8,128)(2,1)S(1)} %collective-permute-done.3.refs_1_, bf16[96,1536]{1,0:T(8,128)(2,1)S(1)} %collective-permute-done.4.refs_2_, ...), custom_call_target="tpu_custom_call" | custom-call | flops 2415919104 | bytes 9437184 | tf_op jit(solution)/shard_map/prepare_qkv/pallas_call | solution.py:98
  225.0 13.9 %attention.1 = (bf16[512,768]{1,0:T(8,128)(2,1)S(1)}, bf16[2,512,384]{2,1,0:T(8,128)(2,1)}) custom-call(bf16[512,1536]{1,0:T(8,128)(2,1)S(1)} %pad_maximum_fusion.emb_ref, f32[1,1536]{1,0:T(1,128)S(1)} %broadcast_in_dim.62.gain_ref, bf16[1536,2048]{1,0:T(8,128)(2,1)} %prepare_qkv.1.weight_ref, f32[512,128]{1,0:T(8,128)S(1)} %get-tuple-element.33.cos_ref, ...), custom_call_target="tpu_custom_call" | custom-call | flops 3221225472 | bytes 11010048 | tf_op jit(solution)/shard_map/attention/pallas_call | solution.py:198
  238.9 1.5 collective-permute-start.11
  240.5 17.5 %collective-permute-done.11.other_ref = bf16[512,768]{1,0:T(8,128)(2,1)S(1)} collective-permute-done((bf16[512,768]{1,0:T(8,128)(2,1)S(1)}, bf16[512,768]{1,0:T(8,128)(2,1)S(1)}, u32[]{:S(2)}, u32[]{:S(2)}) %collective-permute-start.11) | collective-permute-done | bytes 786464 | tf_op jit(solution)/shard_map/ppermute | solution.py:456
  258.0 7.0 %output_part.1 = (f32[512,1536]{1,0:T(8,128)}, bf16[512,1536]{1,0:T(8,128)(2,1)S(1)}) custom-call(bf16[512,1536]{1,0:T(8,128)(2,1)S(1)} %pad_maximum_fusion.emb_ref, bf16[512,768]{1,0:T(8,128)(2,1)S(1)} %get-tuple-element.6.own_ref, bf16[512,768]{1,0:T(8,128)(2,1)S(1)} %collective-permute-done.11.other_ref, bf16[768,1536]{1,0:T(8,128)(2,1)} %w_own_ref.1, ...), custom_call_target="tpu_custom_call" | custom-call | flops 2415919104 | bytes 11010048 | tf_op jit(solution)/shard_map/output_part/pallas_call | solution.py:240
  265.0 1.1 copy-done.23
  266.2 13.0 %hidden_part.1 = bf16[512,2048]{1,0:T(8,128)(2,1)} custom-call(s32[16]{0:T(128)S(1)} %pad_add_fusion.place_ref, bf16[512,1536]{1,0:T(8,128)(2,1)} %copy-done.23, bf16[96,4096]{1,0:T(8,128)(2,1)S(1)} %copy-done.9, bf16[96,4096]{1,0:T(8,128)(2,1)S(1)} %copy-done.11, bf16[96,4096]{1,0:T(8,128)(2,1)S(1)} %copy-done.13, bf16[96,4096]{1,0:T(8,128)(2,1)S(1)} %copy-done.15, ...), custom_call_target="tpu_custom_call" | custom-call | flops 6442450944 | bytes 15728640 | tf_op jit(solution)/shard_map/hidden_part/pallas_call | solution.py:304
  279.2 3.4 %fusion.11 = bf16[512,384]{1,0:T(8,128)(2,1)S(1)} fusion(bf16[512,2048]{1,0:T(8,128)(2,1)} %hidden_part.1, bf16[2048,1536]{1,0:T(8,128)(2,1)} %param.19), kind=kOutput, calls=%fused_computation.15 | convolution fusion | flops 805502976 | bytes 4063232 | tf_op jit(solution)/shard_map/dot_general | solution.py:466
  282.7 2.7 fusion.14
  285.4 2.7 fusion.17
  288.0 2.8 fusion.20
  290.9 1.6 collective-permute-start.23
  293.0 1.5 collective-permute-start.25
  295.0 8.0 %collective-permute-done.23 = bf16[512,384]{1,0:T(8,128)(2,1)S(1)} collective-permute-done((bf16[512,384]{1,0:T(8,128)(2,1)S(1)}, bf16[512,384]{1,0:T(8,128)(2,1)S(1)}, u32[]{:S(2)}, u32[]{:S(2)}) %collective-permute-start.23) | collective-permute-done | bytes 393248 | tf_op jit(solution)/shard_map/ppermute | solution.py:467
  303.0 8.4 %collective-permute-done.24 = bf16[512,384]{1,0:T(8,128)(2,1)S(1)} collective-permute-done((bf16[512,384]{1,0:T(8,128)(2,1)S(1)}, bf16[512,384]{1,0:T(8,128)(2,1)S(1)}, u32[]{:S(2)}, u32[]{:S(2)}) %collective-permute-start.24) | collective-permute-done | bytes 393248 | tf_op jit(solution)/shard_map/ppermute | solution.py:467
  311.4 8.4 %collective-permute-done.25 = bf16[512,384]{1,0:T(8,128)(2,1)S(1)} collective-permute-done((bf16[512,384]{1,0:T(8,128)(2,1)S(1)}, bf16[512,384]{1,0:T(8,128)(2,1)S(1)}, u32[]{:S(2)}, u32[]{:S(2)}) %collective-permute-start.25) | collective-permute-done | bytes 393248 | tf_op jit(solution)/shard_map/ppermute | solution.py:467
  319.8 6.2 %collective-permute-done.26 = bf16[512,384]{1,0:T(8,128)(2,1)S(1)} collective-permute-done((bf16[512,384]{1,0:T(8,128)(2,1)S(1)}, bf16[512,384]{1,0:T(8,128)(2,1)S(1)}, u32[]{:S(2)}, u32[]{:S(2)}) %collective-permute-start.26) | collective-permute-done | bytes 393248 | tf_op jit(solution)/shard_map/ppermute | solution.py:467
  326.6 1.3 pad_maximum_fusion.1
  (146 shorter events, 29.1 us)
Async XLA Ops:
  0.7 19.6 %copy-start.28 = (f32[1536]{0:T(1024)S(1)}, f32[1536]{0:T(1024)}, u32[]{:S(2)}) copy-start(f32[1536]{0:T(1024)} %param.14) | copy-start | bytes 18436
  2.2 21.6 %collective-permute-start.13 = (bf16[48,4096]{1,0:T(8,128)(2,1)S(1)}, bf16[48,4096]{1,0:T(8,128)(2,1)S(1)}, u32[]{:S(2)}, u32[]{:S(2)}) collective-permute-start(bf16[48,4096]{1,0:T(8,128)(2,1)S(1)} %pad_maximum_fusion.4), channel_id=1, source_target_pairs={{0,16},{16,0},{1,17},{17,1},{2,18},{18,2},{3,19},{19,3},{4,20},{20... | collective-permute-start | bytes 1179656 | tf_op jit(solution)/shard_map/ppermute | solution.py:381
  5.4 13.0 %collective-permute-start.1 = (bf16[48,1536]{1,0:T(8,128)(2,1)S(1)}, bf16[48,1536]{1,0:T(8,128)(2,1)S(1)}, u32[]{:S(2)}, u32[]{:S(2)}) collective-permute-start(bf16[48,1536]{1,0:T(8,128)(2,1)S(1)} %pad_maximum_fusion.7), channel_id=1, source_target_pairs={{0,16},{16,0},{1,17},{17,1},{2,18},{18,2},{3,19},{19,3},{4,20},{20... | collective-permute-start | bytes 442376 | tf_op jit(solution)/shard_map/ppermute | solution.py:381
  6.6 13.6 %all-to-all-start = ((s32[16,1,32]{2,1,0:T(1,128)}), s32[16,1,32]{2,1,0:T(1,128)S(1)}, u32[]{:S(2)}, u32[]{:S(2)}) async-start(s32[16,1,32]{2,1,0:T(1,128)} %sub.87), calls=%async_computation | async-start | bytes 16384 | tf_op jit(solution)/shard_map/all_to_all | solution.py:366
  13.0 227.5 %collective-permute-start.12 = (bf16[768,1536]{1,0:T(8,128)(2,1)}, bf16[768,1536]{1,0:T(8,128)(2,1)}, u32[]{:S(2)}, u32[]{:S(2)}) collective-permute-start(bf16[768,1536]{1,0:T(8,128)(2,1)} %w_own_ref.1), channel_id=1, source_target_pairs={{0,16},{16,0},{1,17},{17,1},{2,18},{18,2},{3,19},{19,3},{4,20},{20... | collective-permute-start | bytes 7077896 | tf_op jit(solution)/shard_map/ppermute | solution.py:412
  18.4 3.1 collective-permute-start.2
  21.6 15.6 %collective-permute-start.3 = (bf16[96,1536]{1,0:T(8,128)(2,1)S(1)}, bf16[96,1536]{1,0:T(8,128)(2,1)S(1)}, u32[]{:S(2)}, u32[]{:S(2)}) collective-permute-start(bf16[96,1536]{1,0:T(8,128)(2,1)S(1)} %pad_maximum_fusion.5.refs_0_), channel_id=1, source_target_pairs={{0,4},{4,8},{8,12},{12,14},{14,10},{10,6},{6,2},{2,0},{5,1},{9,5},... | collective-permute-start | bytes 884744 | tf_op jit(solution)/shard_map/ppermute | solution.py:46
  23.9 15.2 %collective-permute-start.14 = (bf16[48,4096]{1,0:T(8,128)(2,1)S(1)}, bf16[48,4096]{1,0:T(8,128)(2,1)S(1)}, u32[]{:S(2)}, u32[]{:S(2)}) collective-permute-start(bf16[48,4096]{1,0:T(8,128)(2,1)S(1)} %broadcast_select_fusion.4), channel_id=1, source_target_pairs={{0,1},{1,0},{2,3},{3,2},{4,5},{5,4},{6,7},{7,6},{8,9},{9,8},{10,11... | collective-permute-start | bytes 1179656 | tf_op jit(solution)/shard_map/ppermute | solution.py:383
  31.5 162.2 %all-to-all-start.1 = ((bf16[16,32,1536]{2,1,0:T(8,128)(2,1)}), bf16[16,32,1536]{2,1,0:T(8,128)(2,1)}, u32[]{:S(2)}, u32[]{:S(2)}) async-start(bf16[16,32,1536]{2,1,0:T(8,128)(2,1)} %bitcast), calls=%async_computation.1 | async-start | bytes 3145728 | tf_op jit(solution)/shard_map/all_to_all | solution.py:416
  37.2 28.9 %collective-permute-start.4 = (bf16[96,1536]{1,0:T(8,128)(2,1)S(1)}, bf16[96,1536]{1,0:T(8,128)(2,1)S(1)}, u32[]{:S(2)}, u32[]{:S(2)}) collective-permute-start(bf16[96,1536]{1,0:T(8,128)(2,1)S(1)} %collective-permute-done.3.refs_1_), channel_id=1, source_target_pairs={{0,4},{4,8},{8,12},{12,14},{14,10},{10,6},{6,2},{2,0},{5,1},{9,5},... | collective-permute-start | bytes 884744 | tf_op jit(solution)/shard_map/ppermute | solution.py:46
  39.4 58.3 %copy-start.8 = (bf16[96,4096]{1,0:T(8,128)(2,1)}, bf16[96,4096]{1,0:T(8,128)(2,1)S(1)}, u32[]{:S(2)}) copy-start(bf16[96,4096]{1,0:T(8,128)(2,1)S(1)} %pad_maximum_fusion.2.refs_0_) | copy-start | bytes 2359300
  39.4 36.8 %collective-permute-start.15 = (bf16[96,4096]{1,0:T(8,128)(2,1)S(1)}, bf16[96,4096]{1,0:T(8,128)(2,1)S(1)}, u32[]{:S(2)}, u32[]{:S(2)}) collective-permute-start(bf16[96,4096]{1,0:T(8,128)(2,1)S(1)} %pad_maximum_fusion.2.refs_0_), channel_id=1, source_target_pairs={{0,4},{4,8},{8,12},{12,14},{14,10},{10,6},{6,2},{2,0},{5,1},{9,5},... | collective-permute-start | bytes 2359304 | tf_op jit(solution)/shard_map/ppermute | solution.py:46
  66.1 91.6 %collective-permute-start.5 = (bf16[96,1536]{1,0:T(8,128)(2,1)S(1)}, bf16[96,1536]{1,0:T(8,128)(2,1)S(1)}, u32[]{:S(2)}, u32[]{:S(2)}) collective-permute-start(bf16[96,1536]{1,0:T(8,128)(2,1)S(1)} %collective-permute-done.4.refs_2_), channel_id=1, source_target_pairs={{0,4},{4,8},{8,12},{12,14},{14,10},{10,6},{6,2},{2,0},{5,1},{9,5},... | collective-permute-start | bytes 884744 | tf_op jit(solution)/shard_map/ppermute | solution.py:46
  76.2 33.3 %copy-start.10 = (bf16[96,4096]{1,0:T(8,128)(2,1)}, bf16[96,4096]{1,0:T(8,128)(2,1)S(1)}, u32[]{:S(2)}) copy-start(bf16[96,4096]{1,0:T(8,128)(2,1)S(1)} %collective-permute-done.15.refs_1_) | copy-start | bytes 2359300
  76.2 17.9 %collective-permute-start.16 = (bf16[96,4096]{1,0:T(8,128)(2,1)S(1)}, bf16[96,4096]{1,0:T(8,128)(2,1)S(1)}, u32[]{:S(2)}, u32[]{:S(2)}) collective-permute-start(bf16[96,4096]{1,0:T(8,128)(2,1)S(1)} %collective-permute-done.15.refs_1_), channel_id=1, source_target_pairs={{0,4},{4,8},{8,12},{12,14},{14,10},{10,6},{6,2},{2,0},{5,1},{9,5},... | collective-permute-start | bytes 2359304 | tf_op jit(solution)/shard_map/ppermute | solution.py:46
  94.1 27.4 %copy-start.12 = (bf16[96,4096]{1,0:T(8,128)(2,1)}, bf16[96,4096]{1,0:T(8,128)(2,1)S(1)}, u32[]{:S(2)}) copy-start(bf16[96,4096]{1,0:T(8,128)(2,1)S(1)} %collective-permute-done.16.refs_2_) | copy-start | bytes 2359300
  94.1 13.8 %collective-permute-start.17 = (bf16[96,4096]{1,0:T(8,128)(2,1)S(1)}, bf16[96,4096]{1,0:T(8,128)(2,1)S(1)}, u32[]{:S(2)}, u32[]{:S(2)}) collective-permute-start(bf16[96,4096]{1,0:T(8,128)(2,1)S(1)} %collective-permute-done.16.refs_2_), channel_id=1, source_target_pairs={{0,4},{4,8},{8,12},{12,14},{14,10},{10,6},{6,2},{2,0},{5,1},{9,5},... | collective-permute-start | bytes 2359304 | tf_op jit(solution)/shard_map/ppermute | solution.py:46
  108.0 25.6 %copy-start.14 = (bf16[96,4096]{1,0:T(8,128)(2,1)}, bf16[96,4096]{1,0:T(8,128)(2,1)S(1)}, u32[]{:S(2)}) copy-start(bf16[96,4096]{1,0:T(8,128)(2,1)S(1)} %collective-permute-done.17.refs_3_) | copy-start | bytes 2359300
  108.0 12.0 %collective-permute-start.18 = (bf16[96,4096]{1,0:T(8,128)(2,1)S(1)}, bf16[96,4096]{1,0:T(8,128)(2,1)S(1)}, u32[]{:S(2)}, u32[]{:S(2)}) collective-permute-start(bf16[96,4096]{1,0:T(8,128)(2,1)S(1)} %collective-permute-done.17.refs_3_), channel_id=1, source_target_pairs={{0,4},{4,8},{8,12},{12,14},{14,10},{10,6},{6,2},{2,0},{5,1},{9,5},... | collective-permute-start | bytes 2359304 | tf_op jit(solution)/shard_map/ppermute | solution.py:46
  120.0 25.6 %copy-start.16 = (bf16[96,4096]{1,0:T(8,128)(2,1)}, bf16[96,4096]{1,0:T(8,128)(2,1)S(1)}, u32[]{:S(2)}) copy-start(bf16[96,4096]{1,0:T(8,128)(2,1)S(1)} %collective-permute-done.18.refs_4_) | copy-start | bytes 2359300
  120.0 12.0 %collective-permute-start.19 = (bf16[96,4096]{1,0:T(8,128)(2,1)S(1)}, bf16[96,4096]{1,0:T(8,128)(2,1)S(1)}, u32[]{:S(2)}, u32[]{:S(2)}) collective-permute-start(bf16[96,4096]{1,0:T(8,128)(2,1)S(1)} %collective-permute-done.18.refs_4_), channel_id=1, source_target_pairs={{0,4},{4,8},{8,12},{12,14},{14,10},{10,6},{6,2},{2,0},{5,1},{9,5},... | collective-permute-start | bytes 2359304 | tf_op jit(solution)/shard_map/ppermute | solution.py:46
  132.0 25.0 %copy-start.18 = (bf16[96,4096]{1,0:T(8,128)(2,1)}, bf16[96,4096]{1,0:T(8,128)(2,1)S(1)}, u32[]{:S(2)}) copy-start(bf16[96,4096]{1,0:T(8,128)(2,1)S(1)} %collective-permute-done.19.refs_5_) | copy-start | bytes 2359300
  132.0 12.0 %collective-permute-start.20 = (bf16[96,4096]{1,0:T(8,128)(2,1)S(1)}, bf16[96,4096]{1,0:T(8,128)(2,1)S(1)}, u32[]{:S(2)}, u32[]{:S(2)}) collective-permute-start(bf16[96,4096]{1,0:T(8,128)(2,1)S(1)} %collective-permute-done.19.refs_5_), channel_id=1, source_target_pairs={{0,4},{4,8},{8,12},{12,14},{14,10},{10,6},{6,2},{2,0},{5,1},{9,5},... | collective-permute-start | bytes 2359304 | tf_op jit(solution)/shard_map/ppermute | solution.py:46
  144.0 21.9 %copy-start.20 = (bf16[96,4096]{1,0:T(8,128)(2,1)}, bf16[96,4096]{1,0:T(8,128)(2,1)S(1)}, u32[]{:S(2)}) copy-start(bf16[96,4096]{1,0:T(8,128)(2,1)S(1)} %collective-permute-done.20.refs_6_) | copy-start | bytes 2359300
  144.0 12.0 %collective-permute-start.21 = (bf16[96,4096]{1,0:T(8,128)(2,1)S(1)}, bf16[96,4096]{1,0:T(8,128)(2,1)S(1)}, u32[]{:S(2)}, u32[]{:S(2)}) collective-permute-start(bf16[96,4096]{1,0:T(8,128)(2,1)S(1)} %collective-permute-done.20.refs_6_), channel_id=1, source_target_pairs={{0,4},{4,8},{8,12},{12,14},{14,10},{10,6},{6,2},{2,0},{5,1},{9,5},... | collective-permute-start | bytes 2359304 | tf_op jit(solution)/shard_map/ppermute | solution.py:46
  145.5 40.5 %copy-start.30 = (s32[1,4]{1,0:T(1,128)S(1)}, s32[1,4]{1,0:T(1,128)}, u32[]{:S(2)}) copy-start(s32[1,4]{1,0:T(1,128)} %param.12) | copy-start | bytes 52
  155.9 29.5 %copy-start.25 = (bf16[96,4096]{1,0:T(8,128)(2,1)}, bf16[96,4096]{1,0:T(8,128)(2,1)S(1)}, u32[]{:S(2)}) copy-start(bf16[96,4096]{1,0:T(8,128)(2,1)S(1)} %collective-permute-done.21.refs_7_) | copy-start | bytes 2359300
  157.0 109.1 %collective-permute-start.22 = (bf16[8,96,4096]{2,1,0:T(8,128)(2,1)}, bf16[8,96,4096]{2,1,0:T(8,128)(2,1)}, u32[]{:S(2)}, u32[]{:S(2)}) collective-permute-start(bf16[8,96,4096]{2,1,0:T(8,128)(2,1)} %bitcast_dynamic-update-slice_fusion), channel_id=1, source_target_pairs={{0,1},{1,0},{2,3},{3,2},{4,5},{5,4},{6,7},{7,6},{8,9},{9,8},{10,11... | collective-permute-start | bytes 18874376 | tf_op jit(solution)/shard_map/ppermute | solution.py:395
  157.8 6.7 %collective-permute-start.6 = (bf16[96,1536]{1,0:T(8,128)(2,1)S(1)}, bf16[96,1536]{1,0:T(8,128)(2,1)S(1)}, u32[]{:S(2)}, u32[]{:S(2)}) collective-permute-start(bf16[96,1536]{1,0:T(8,128)(2,1)S(1)} %collective-permute-done.5.refs_3_), channel_id=1, source_target_pairs={{0,4},{4,8},{8,12},{12,14},{14,10},{10,6},{6,2},{2,0},{5,1},{9,5},... | collective-permute-start | bytes 884744 | tf_op jit(solution)/shard_map/ppermute | solution.py:46
  164.5 20.2 %copy-start = (bf16[96,1536]{1,0:T(8,128)(2,1)}, bf16[96,1536]{1,0:T(8,128)(2,1)S(1)}, u32[]{:S(2)}) copy-start(bf16[96,1536]{1,0:T(8,128)(2,1)S(1)} %collective-permute-done.6.refs_4_) | copy-start | bytes 884740
  164.5 6.7 %collective-permute-start.7 = (bf16[96,1536]{1,0:T(8,128)(2,1)S(1)}, bf16[96,1536]{1,0:T(8,128)(2,1)S(1)}, u32[]{:S(2)}, u32[]{:S(2)}) collective-permute-start(bf16[96,1536]{1,0:T(8,128)(2,1)S(1)} %collective-permute-done.6.refs_4_), channel_id=1, source_target_pairs={{0,4},{4,8},{8,12},{12,14},{14,10},{10,6},{6,2},{2,0},{5,1},{9,5},... | collective-permute-start | bytes 884744 | tf_op jit(solution)/shard_map/ppermute | solution.py:46
  171.2 6.7 %collective-permute-start.8 = (bf16[96,1536]{1,0:T(8,128)(2,1)S(1)}, bf16[96,1536]{1,0:T(8,128)(2,1)S(1)}, u32[]{:S(2)}, u32[]{:S(2)}) collective-permute-start(bf16[96,1536]{1,0:T(8,128)(2,1)S(1)} %collective-permute-done.7.refs_5_), channel_id=1, source_target_pairs={{0,4},{4,8},{8,12},{12,14},{14,10},{10,6},{6,2},{2,0},{5,1},{9,5},... | collective-permute-start | bytes 884744 | tf_op jit(solution)/shard_map/ppermute | solution.py:46
  177.9 6.7 %collective-permute-start.9 = (bf16[96,1536]{1,0:T(8,128)(2,1)S(1)}, bf16[96,1536]{1,0:T(8,128)(2,1)S(1)}, u32[]{:S(2)}, u32[]{:S(2)}) collective-permute-start(bf16[96,1536]{1,0:T(8,128)(2,1)S(1)} %collective-permute-done.8.refs_6_), channel_id=1, source_target_pairs={{0,4},{4,8},{8,12},{12,14},{14,10},{10,6},{6,2},{2,0},{5,1},{9,5},... | collective-permute-start | bytes 884744 | tf_op jit(solution)/shard_map/ppermute | solution.py:46
  185.5 30.5 %collective-permute-start.10 = (bf16[8,96,1536]{2,1,0:T(8,128)(2,1)}, bf16[8,96,1536]{2,1,0:T(8,128)(2,1)S(1)}, u32[]{:S(2)}, u32[]{:S(2)}) collective-permute-start(bf16[8,96,1536]{2,1,0:T(8,128)(2,1)} %bitcast_dynamic-update-slice_fusion.8), channel_id=1, source_target_pairs={{0,1},{1,0},{2,3},{3,2},{4,5},{5,4},{6,7},{7,6},{8,9},{9,8},{10,11... | collective-permute-start | bytes 7077896 | tf_op jit(solution)/shard_map/ppermute | solution.py:394
  195.7 20.0 %collective-permute-start = (bf16[256,1536]{1,0:T(8,128)(2,1)S(1)}, bf16[256,1536]{1,0:T(8,128)(2,1)S(1)}, u32[]{:S(2)}, u32[]{:S(2)}) collective-permute-start(bf16[256,1536]{1,0:T(8,128)(2,1)S(1)} %convolution_convert_fusion), channel_id=1, source_target_pairs={{0,16},{16,0},{1,17},{17,1},{2,18},{18,2},{3,19},{19,3},{4,20},{20... | collective-permute-start | bytes 2359304 | tf_op jit(solution)/shard_map/ppermute | solution.py:425
  238.9 19.2 %collective-permute-start.11 = (bf16[512,768]{1,0:T(8,128)(2,1)S(1)}, bf16[512,768]{1,0:T(8,128)(2,1)S(1)}, u32[]{:S(2)}, u32[]{:S(2)}) collective-permute-start(bf16[512,768]{1,0:T(8,128)(2,1)S(1)} %get-tuple-element.6.own_ref), channel_id=1, source_target_pairs={{0,16},{16,0},{1,17},{17,1},{2,18},{18,2},{3,19},{19,3},{4,20},{20... | collective-permute-start | bytes 2359304 | tf_op jit(solution)/shard_map/ppermute | solution.py:456
  240.4 25.8 %copy-start.9 = (bf16[96,4096]{1,0:T(8,128)(2,1)S(1)}, bf16[96,4096]{1,0:T(8,128)(2,1)}, u32[]{:S(2)}) copy-start(bf16[96,4096]{1,0:T(8,128)(2,1)} %copy-done.8) | copy-start | bytes 2359300
  240.4 25.7 %copy-start.11 = (bf16[96,4096]{1,0:T(8,128)(2,1)S(1)}, bf16[96,4096]{1,0:T(8,128)(2,1)}, u32[]{:S(2)}) copy-start(bf16[96,4096]{1,0:T(8,128)(2,1)} %copy-done.10) | copy-start | bytes 2359300
  240.4 25.7 %copy-start.13 = (bf16[96,4096]{1,0:T(8,128)(2,1)S(1)}, bf16[96,4096]{1,0:T(8,128)(2,1)}, u32[]{:S(2)}) copy-start(bf16[96,4096]{1,0:T(8,128)(2,1)} %copy-done.12) | copy-start | bytes 2359300
  240.4 25.7 %copy-start.15 = (bf16[96,4096]{1,0:T(8,128)(2,1)S(1)}, bf16[96,4096]{1,0:T(8,128)(2,1)}, u32[]{:S(2)}) copy-start(bf16[96,4096]{1,0:T(8,128)(2,1)} %copy-done.14) | copy-start | bytes 2359300
  240.4 25.7 %copy-start.17 = (bf16[96,4096]{1,0:T(8,128)(2,1)S(1)}, bf16[96,4096]{1,0:T(8,128)(2,1)}, u32[]{:S(2)}) copy-start(bf16[96,4096]{1,0:T(8,128)(2,1)} %copy-done.16) | copy-start | bytes 2359300
  240.5 25.7 %copy-start.19 = (bf16[96,4096]{1,0:T(8,128)(2,1)S(1)}, bf16[96,4096]{1,0:T(8,128)(2,1)}, u32[]{:S(2)}) copy-start(bf16[96,4096]{1,0:T(8,128)(2,1)} %copy-done.18) | copy-start | bytes 2359300
  240.5 25.7 %copy-start.21 = (bf16[96,4096]{1,0:T(8,128)(2,1)S(1)}, bf16[96,4096]{1,0:T(8,128)(2,1)}, u32[]{:S(2)}) copy-start(bf16[96,4096]{1,0:T(8,128)(2,1)} %copy-done.20) | copy-start | bytes 2359300
  288.0 38.0 %copy-start.24 = (f32[512,1536]{1,0:T(8,128)S(1)}, f32[512,1536]{1,0:T(8,128)}, u32[]{:S(2)}) copy-start(f32[512,1536]{1,0:T(8,128)} %get-tuple-element.7) | copy-start | bytes 9437188
  290.9 12.1 %collective-permute-start.23 = (bf16[512,384]{1,0:T(8,128)(2,1)S(1)}, bf16[512,384]{1,0:T(8,128)(2,1)S(1)}, u32[]{:S(2)}, u32[]{:S(2)}) collective-permute-start(bf16[512,384]{1,0:T(8,128)(2,1)S(1)} %fusion.11), channel_id=1, source_target_pairs={{0,16},{16,0},{1,17},{17,1},{2,18},{18,2},{3,19},{19,3},{4,20},{20... | collective-permute-start | bytes 1179656 | tf_op jit(solution)/shard_map/ppermute | solution.py:467
  292.5 19.0 %collective-permute-start.24 = (bf16[512,384]{1,0:T(8,128)(2,1)S(1)}, bf16[512,384]{1,0:T(8,128)(2,1)S(1)}, u32[]{:S(2)}, u32[]{:S(2)}) collective-permute-start(bf16[512,384]{1,0:T(8,128)(2,1)S(1)} %fusion.14), channel_id=1, source_target_pairs={{0,16},{16,0},{1,17},{17,1},{2,18},{18,2},{3,19},{19,3},{4,20},{20... | collective-permute-start | bytes 1179656 | tf_op jit(solution)/shard_map/ppermute | solution.py:467
  293.0 26.9 %collective-permute-start.25 = (bf16[512,384]{1,0:T(8,128)(2,1)S(1)}, bf16[512,384]{1,0:T(8,128)(2,1)S(1)}, u32[]{:S(2)}, u32[]{:S(2)}) collective-permute-start(bf16[512,384]{1,0:T(8,128)(2,1)S(1)} %fusion.17), channel_id=1, source_target_pairs={{0,16},{16,0},{1,17},{17,1},{2,18},{18,2},{3,19},{19,3},{4,20},{20... | collective-permute-start | bytes 1179656 | tf_op jit(solution)/shard_map/ppermute | solution.py:467
  294.5 31.6 %collective-permute-start.26 = (bf16[512,384]{1,0:T(8,128)(2,1)S(1)}, bf16[512,384]{1,0:T(8,128)(2,1)S(1)}, u32[]{:S(2)}, u32[]{:S(2)}) collective-permute-start(bf16[512,384]{1,0:T(8,128)(2,1)S(1)} %fusion.20), channel_id=1, source_target_pairs={{0,16},{16,0},{1,17},{17,1},{2,18},{18,2},{3,19},{19,3},{4,20},{20... | collective-permute-start | bytes 1179656 | tf_op jit(solution)/shard_map/ppermute | solution.py:467
  (17 other events, 99.9 us)

commit v3 on v0

v3 whole, which is shorter than its diff:
```python
import functools
import math

import jax
import jax.numpy as jnp
from jax import lax
from jax.experimental import pallas as pl
from jax.experimental.pallas import tpu as pltpu
from jax.sharding import PartitionSpec as P

HEAD_DIM = 96
HALF = HEAD_DIM // 2
LANES = 128

rope_base = 100000.0
norm_eps = 1e-05

BF = jnp.bfloat16
F32 = jnp.float32
PAIR = [(0, 1), (1, 0)]
VMEM_LIMIT = 48 * 1024 * 1024


def token_offsets(starts, row_count):
    positions = jnp.arange(row_count, dtype=jnp.int32)
    offset = positions
    for i in range(1, starts.shape[0]):
        offset = jnp.where(positions >= starts[i], positions - starts[i], offset)
    return offset


def after(value, *others):
    return lax.optimization_barrier((value, *others))[0]


def chip_ring(chips):
    order = list(range(0, chips, 2)) + list(range(chips - 1 - chips % 2, 0, -2))
    following = {order[i]: order[(i + 1) % chips] for i in range(chips)}
    pairs = [(2 * c, 2 * d) for c, d in following.items()]
    pairs += [(2 * d + 1, 2 * c + 1) for c, d in following.items()]
    return order, pairs


def ring_more(blocks, count, pairs, *ready):
    blocks = list(blocks)
    for i in range(count):
        last = after(blocks[-1], *ready) if ready and i == 0 else blocks[-1]
        blocks.append(lax.ppermute(last, "req", pairs))
    return blocks


def in_vmem(count):
    return [pl.BlockSpec(memory_space=pltpu.VMEM)] * count


def params():
    return pltpu.CompilerParams(vmem_limit_bytes=VMEM_LIMIT)


def spread_columns(heads):
    column = jnp.arange(heads * HEAD_DIM, dtype=jnp.int32)
    within = column % HEAD_DIM
    target = column // HEAD_DIM * LANES + jnp.where(within < HALF, within, within + 64 - HALF)
    return (target[:, None] == jnp.arange(heads * LANES, dtype=jnp.int32)[None, :]).astype(BF)


def tenant_at(start_ref, tenant_ref, positions):
    tenant = jnp.full(positions.shape, tenant_ref[0], jnp.int32)
    for i in range(1, tenant_ref.shape[0]):
        tenant = jnp.where(positions >= start_ref[i], tenant_ref[i], tenant)
    return tenant


def bias_of(start_ref, tenant_ref, first, count, seen):
    row = lax.broadcasted_iota(jnp.int32, (count, seen), 0) + first
    col = lax.broadcasted_iota(jnp.int32, (count, seen), 1)
    query_tenant = tenant_at(
        start_ref, tenant_ref, lax.broadcasted_iota(jnp.int32, (count, 1), 0) + first
    )
    key_tenant = tenant_at(start_ref, tenant_ref, lax.broadcasted_iota(jnp.int32, (1, seen), 1))
    return jnp.where((col <= row) & (query_tenant == key_tenant), 0.0, -1e30)


def attend_head(q, keys, values, bias):
    scores = lax.dot_general(q, keys, (((1,), (1,)), ((), ())), preferred_element_type=F32) + bias
    top = jnp.max(scores, axis=-1, keepdims=True)
    expo = jnp.exp2((scores - top) * (HEAD_DIM**-0.5 * math.log2(math.e)))
    total = jnp.sum(expo, axis=-1, keepdims=True)
    out = jnp.dot(expo.astype(BF), values, preferred_element_type=F32)
    return (out / total).astype(BF)


def packed(x, pack_ref):
    wide = pack_ref.shape[0]
    return jnp.concatenate(
        [
            jnp.dot(x[:, b : b + wide], pack_ref[...], preferred_element_type=F32).astype(BF)
            for b in range(0, x.shape[1], wide)
        ],
        axis=1,
    )


def project_kernel(
    q_heads,
    kv_heads,
    blocks,
    spots_ref,
    start_ref,
    tenant_ref,
    emb_ref,
    gain_ref,
    cos_ref,
    sin_ref,
    spread_ref,
    pack_ref,
    *refs,
):
    sources, refs = block_list(refs[:blocks]), refs[blocks:]
    att_ref, cache_ref, late_ref, keys, values, raw, weight_ref, normed, mixed, bias, sems = refs
    tokens = emb_ref.shape[0]
    step = tokens // 2
    group = q_heads // kv_heads
    _, count, rows, cols = raw.shape
    copies = block_copies(spots_ref, sources, raw, sems, pl.ds(0, cols))
    for copy in copies:
        copy.start()
    for r in range(0, tokens, step):
        x = emb_ref[r : r + step, :].astype(F32)
        scale = lax.rsqrt(jnp.mean(x * x, axis=-1, keepdims=True) + norm_eps)
        normed[r : r + step, :] = (x * scale * gain_ref[...]).astype(BF)
    bias[...] = bias_of(start_ref, tenant_ref, 0, step, step)
    for copy in copies:
        copy.wait()
    narrow, wide = spread_ref.shape
    target = 0
    for part in range(2):
        for b in range(cols // narrow):
            piece = raw[part, :, :, b * narrow : (b + 1) * narrow].reshape(count * rows, narrow)
            weight_ref[:, target : target + wide] = jnp.dot(
                piece, spread_ref[...], preferred_element_type=F32
            ).astype(BF)
            target += wide

    def turned(x):
        return (x * cos_ref[...] + pltpu.roll(x, 64, 1) * sin_ref[...]).astype(BF)

    def project(first, heads):
        return jnp.dot(
            normed[...],
            weight_ref[:, first * LANES : (first + heads) * LANES],
            preferred_element_type=F32,
        )

    k_all = project(q_heads, kv_heads)
    for h in range(kv_heads):
        keys[:, h * LANES : (h + 1) * LANES] = turned(k_all[:, h * LANES : (h + 1) * LANES])
    values[...] = project(q_heads + kv_heads, kv_heads).astype(BF)
    for kv in range(kv_heads):
        lanes = slice(kv * LANES, (kv + 1) * LANES)
        q_all = project(kv * group, group)
        for g in range(group):
            h = kv * group + g
            head = slice(h * LANES, (h + 1) * LANES)
            q = turned(q_all[:, g * LANES : (g + 1) * LANES])
            late_ref[:, head] = q[step:, :]
            mixed[:, head] = attend_head(
                q[:step, :], keys[:step, lanes], values[:step, lanes], bias[...]
            )
    att_ref[...] = packed(mixed[...], pack_ref)
    cache_ref[0] = packed(keys[...], pack_ref)
    cache_ref[1] = packed(values[...], pack_ref)


def late_kernel(
    q_heads, kv_heads, start_ref, tenant_ref, q_ref, keys, values, pack_ref, att_ref, mixed, bias
):
    step = q_ref.shape[0]
    seen = keys.shape[0]
    group = q_heads // kv_heads
    bias[...] = bias_of(start_ref, tenant_ref, seen - step, step, seen)
    for h in range(q_heads):
        head = slice(h * LANES, (h + 1) * LANES)
        lanes = slice(h // group * LANES, (h // group + 1) * LANES)
        mixed[:, head] = attend_head(q_ref[:, head], keys[:, lanes], values[:, lanes], bias[...])
    att_ref[...] = packed(mixed[...], pack_ref)


def block_list(refs):
    blocks = []
    for ref in refs:
        blocks += [ref] if len(ref.shape) == 2 else [ref.at[i] for i in range(ref.shape[0])]
    return blocks


def block_copies(spots_ref, sources, target, sems, cols):
    return [
        pltpu.make_async_copy(
            source.at[:, cols], target.at[spots_ref[0, s], spots_ref[1, s]], sems.at[s]
        )
        for s, source in enumerate(sources)
    ]


def attention_early(
    spots, starts, tenants, embedded, gain, cosine, sine, spread, blocks, cols, q_heads, kv_heads
):
    tokens, width = embedded.shape
    rows = blocks[0].shape[0]
    total = spots.shape[1]
    wide = 2 * cols // spread.shape[0] * spread.shape[1]
    step = tokens // 2
    return pl.pallas_call(
        functools.partial(project_kernel, q_heads, kv_heads, len(blocks)),
        out_shape=(
            jax.ShapeDtypeStruct((step, q_heads * HEAD_DIM), BF),
            jax.ShapeDtypeStruct((2, tokens, kv_heads * HEAD_DIM), BF),
            jax.ShapeDtypeStruct((step, q_heads * LANES), BF),
            jax.ShapeDtypeStruct((tokens, kv_heads * LANES), BF),
            jax.ShapeDtypeStruct((tokens, kv_heads * LANES), BF),
        ),
        in_specs=[pl.BlockSpec(memory_space=pltpu.SMEM)] * 3
        + in_vmem(6)
        + [pl.BlockSpec(memory_space=pl.ANY)] * len(blocks),
        out_specs=tuple(in_vmem(5)),
        scratch_shapes=[
            pltpu.VMEM((2, total // 2, rows, cols), BF),
            pltpu.VMEM((width, wide), BF),
            pltpu.VMEM((tokens, width), BF),
            pltpu.VMEM((step, q_heads * LANES), BF),
            pltpu.VMEM((step, step), F32),
            pltpu.SemaphoreType.DMA((total,)),
        ],
        compiler_params=params(),
        name="attention_early",
        cost_estimate=pl.CostEstimate(
            flops=2 * tokens * width * wide + 2 * width * wide * spread.shape[0],
            bytes_accessed=4 * width * wide + 6 * embedded.size,
            transcendentals=q_heads * step * step,
        ),
    )(spots, starts, tenants, embedded, gain, cosine, sine, spread, spread.T, *blocks)


def attention_late(starts, tenants, queries, keys, values, pack, q_heads, kv_heads):
    step, tokens = queries.shape[0], keys.shape[0]
    return pl.pallas_call(
        functools.partial(late_kernel, q_heads, kv_heads),
        out_shape=jax.ShapeDtypeStruct((step, q_heads * HEAD_DIM), BF),
        in_specs=[pl.BlockSpec(memory_space=pltpu.SMEM)] * 2 + in_vmem(4),
        out_specs=pl.BlockSpec(memory_space=pltpu.VMEM),
        scratch_shapes=[
            pltpu.VMEM((step, q_heads * LANES), BF),
            pltpu.VMEM((step, tokens), F32),
        ],
        compiler_params=params(),
        name="attention_late",
        cost_estimate=pl.CostEstimate(
            flops=4 * q_heads * step * tokens * LANES,
            bytes_accessed=8 * keys.size,
            transcendentals=q_heads * step * tokens,
        ),
    )(starts, tenants, queries, keys, values, pack)


def ffn_kernel(
    blocks,
    first_col,
    spots_ref,
    core_ref,
    emb_ref,
    own_ref,
    other_ref,
    w_own_ref,
    w_first_ref,
    w_second_ref,
    gain_ref,
    down_ref,
    *refs,
):
    sources, refs = block_list(refs[:blocks]), refs[blocks:]
    res_ref, part_ref, buf, down_buf, normed, total, sems, down_sems = refs
    _, _, count, rows, wide = buf.shape
    width = count * rows
    steps = down_ref.shape[0] // wide

    def copies(j):
        slot = j % 2
        made = block_copies(
            spots_ref, sources, buf.at[slot], sems.at[slot], pl.ds(first_col + j * wide, wide)
        )
        made.append(
            pltpu.make_async_copy(
                down_ref.at[pl.ds(j * wide, wide), :], down_buf.at[slot], down_sems.at[slot]
            )
        )
        return made

    pending = copies(0)
    for copy in pending:
        copy.start()
    depth = w_first_ref.shape[0]
    core = core_ref[0]
    first = pl.ds(pl.multiple_of(core * depth, LANES), depth)
    second = pl.ds(pl.multiple_of((1 - core) * depth, LANES), depth)
    x = (
        emb_ref[...].astype(F32)
        + jnp.dot(own_ref[...], w_own_ref[...], preferred_element_type=F32)
        + jnp.dot(other_ref[:, first], w_first_ref[...], preferred_element_type=F32)
        + jnp.dot(other_ref[:, second], w_second_ref[...], preferred_element_type=F32)
    )
    res_ref[...] = x
    scale = lax.rsqrt(jnp.mean(x * x, axis=-1, keepdims=True) + norm_eps)
    normed[...] = (x * scale * gain_ref[...]).astype(BF)
    for j in range(steps):
        current, slot = pending, j % 2
        if j + 1 < steps:
            pending = copies(j + 1)
            for copy in pending:
                copy.start()
        for copy in current:
            copy.wait()
        gate = jnp.dot(normed[...], buf[slot, 0].reshape(width, wide), preferred_element_type=F32)
        up = jnp.dot(normed[...], buf[slot, 1].reshape(width, wide), preferred_element_type=F32)
        hidden = (gate / (1.0 + jnp.exp(-gate)) * up).astype(BF)
        term = jnp.dot(hidden, down_buf[slot], preferred_element_type=F32)
        if j == 0:
            total[...] = term
        elif j + 1 < steps:
            total[...] += term
        else:
            part_ref[...] = (total[...] + term).astype(BF)


def ffn_part(
    spots, core, embedded, own, other, w_own, w_first, w_second, gain, down, blocks, first_col
):
    tokens, width = embedded.shape
    rows = blocks[0].shape[0]
    total = spots.shape[1]
    ff_half = down.shape[0]
    wide = min(512, ff_half)
    return pl.pallas_call(
        functools.partial(ffn_kernel, len(blocks), first_col),
        out_shape=(
            jax.ShapeDtypeStruct((tokens, width), F32),
            jax.ShapeDtypeStruct((tokens, width), BF),
        ),
        in_specs=[pl.BlockSpec(memory_space=pltpu.SMEM)] * 2
        + in_vmem(7)
        + [pl.BlockSpec(memory_space=pl.ANY)] * (1 + len(blocks)),
        out_specs=tuple(in_vmem(2)),
        scratch_shapes=[
            pltpu.VMEM((2, 2, total // 2, rows, wide), BF),
            pltpu.VMEM((2, wide, width), BF),
            pltpu.VMEM((tokens, width), BF),
            pltpu.VMEM((tokens, width), F32),
            pltpu.SemaphoreType.DMA((2, total)),
            pltpu.SemaphoreType.DMA((2,)),
        ],
        compiler_params=params(),
        name="ffn_part",
        cost_estimate=pl.CostEstimate(
            flops=2 * tokens * width * (3 * ff_half + 2 * w_own.shape[0]),
            bytes_accessed=6 * width * ff_half + 4 * w_own.size,
            transcendentals=tokens * ff_half,
        ),
    )(spots, core, embedded, own, other, w_own, w_first, w_second, gain, down, *blocks)


def per_device(
    token_ids,
    prompt_lengths,
    tenant_ids,
    embed_table,
    attention_gain,
    qkv_weight,
    out_weight,
    ffn_gain,
    gate_up_weight,
    down_weight,
):
    tp_count = lax.axis_size("tp")
    tp_index = lax.axis_index("tp")
    group_count = lax.axis_size("req")
    req_index = lax.axis_index("req")
    tokens = token_ids.shape[0]
    looked = tokens // tp_count
    own_rows, width = embed_table.shape
    capacity = max(2, 2 * looked // group_count)
    q_half = out_weight.shape[0]
    ff_half = down_weight.shape[0]
    q_full = q_half * tp_count
    kv_half = (qkv_weight.shape[1] - q_full) // (2 * tp_count)
    kv_full = kv_half * tp_count
    ff_full = ff_half * tp_count
    chips = group_count // 2
    core = req_index % 2
    chip = req_index // 2
    core_swap = [(i, i ^ 1) for i in range(group_count)]
    order, ring_pairs = chip_ring(chips)

    my_ids = lax.dynamic_slice_in_dim(token_ids, tp_index * looked, looked)
    owner_of = my_ids // own_rows
    row_in_range = my_ids - owner_of * own_rows
    earlier = jnp.arange(looked)[None, :] < jnp.arange(looked)[:, None]
    same = (owner_of[:, None] == owner_of[None, :]) & earlier
    place = owner_of * capacity + jnp.sum(same.astype(jnp.int32), axis=1)
    slots = jnp.arange(group_count * capacity, dtype=jnp.int32)
    chosen = place[None, :] == slots[:, None]
    requests = jnp.sum(jnp.where(chosen, row_in_range[None, :] + 1, 0), axis=1) - 1
    lengths = prompt_lengths[0]
    starts = jnp.stack([jnp.sum(lengths[:i]) for i in range(lengths.shape[0])]).astype(jnp.int32)
    offset = token_offsets(starts, tokens)
    lane = jnp.arange(LANES, dtype=jnp.int32)
    frequency = rope_base ** (-2.0 * (lane % 64).astype(F32) / HEAD_DIM)
    angles = offset.astype(F32)[:, None] * frequency[None, :]
    cosine = jnp.cos(angles)
    sine = jnp.where(lane < 64, -1.0, 1.0)[None, :] * jnp.sin(angles)

    asked = lax.all_to_all(
        requests.reshape(group_count, capacity), "req", split_axis=0, concat_axis=0, tiled=True
    ).reshape(-1)

    q_parts = ((0, q_half),)
    kv_parts = ((q_full, kv_half), (q_full + kv_full, kv_half))

    def columns(half, part):
        pieces = [
            lax.dynamic_slice_in_dim(qkv_weight, base + half * size, size, axis=1)
            for base, size in (q_parts, kv_parts)[part]
        ]
        pieces.append(
            lax.dynamic_slice_in_dim(
                gate_up_weight, part * ff_full + half * ff_half, ff_half, axis=1
            )
        )
        return jnp.concatenate([piece.astype(BF) for piece in pieces], axis=1)

    def chip_block(parts):
        kept = jnp.where(core == 0, parts[0], parts[1])
        moved = lax.ppermute(jnp.where(core == 0, parts[1], parts[0]), "req", core_swap)
        return jnp.concatenate(
            [jnp.where(core == 0, kept, moved), jnp.where(core == 0, moved, kept)], axis=0
        )

    own_ring = [chip_block([columns(tp_index, part) for part in range(2)])]
    away = jnp.stack([columns(1 - tp_index, part) for part in range(2)])
    came = lax.ppermute(away, "tp", PAIR)
    other_ring = [chip_block([came[part] for part in range(2)])]

    steps = jnp.arange(chips, dtype=jnp.int32)
    here = jnp.where(chip % 2 == 0, chip // 2, chips - 1 - chip // 2)

    def source_chip(position):
        position = position % chips
        return jnp.where(position < (chips + 1) // 2, 2 * position, 2 * (chips - 1 - position) + 1)

    up_chip, down_chip = source_chip(here - steps), source_chip(here + steps)
    mine = jnp.where(core == 0, up_chip, down_chip)
    theirs = jnp.where(core == 0, down_chip, up_chip)
    own_row, other_row = tp_index * chips, (1 - tp_index) * chips
    spots = jnp.stack(
        [
            jnp.repeat(jnp.stack([core, 1 - core]), 2 * chips),
            jnp.concatenate(
                [own_row + mine, other_row + mine, own_row + theirs, other_row + theirs]
            ),
        ]
    ).astype(jnp.int32)

    asked = after(asked, cosine, sine)
    pick_rows = (asked[:, None] == jnp.arange(own_rows, dtype=jnp.int32)[None, :]).astype(BF)
    found_rows = jnp.dot(pick_rows, embed_table, preferred_element_type=F32).astype(BF)
    returned = lax.all_to_all(
        found_rows.reshape(group_count, capacity, width),
        "req",
        split_axis=0,
        concat_axis=0,
        tiled=True,
    ).reshape(group_count * capacity, width)
    pick_mine = (place[:, None] == slots[None, :]).astype(BF)
    embedded_own = jnp.dot(pick_mine, returned, preferred_element_type=F32).astype(BF)
    embedded_other = lax.ppermute(embedded_own, "tp", PAIR)
    embedded = [
        jnp.where(tp_index == 0, embedded_own, embedded_other),
        jnp.where(tp_index == 0, embedded_other, embedded_own),
    ]

    out_rows = q_half // 2
    out_first = lax.ppermute(
        lax.dynamic_slice_in_dim(out_weight, core * out_rows, out_rows), "tp", PAIR
    )
    out_second = lax.ppermute(out_first, "req", core_swap)

    def swapped(blocks):
        return lax.ppermute(jnp.stack(blocks), "req", core_swap)

    cut = (chips + 2) // 2
    for i in range(chips - 1):
        ready = {2: (embedded_own,), 4: (embedded_other, out_second)}.get(i, ())
        own_ring = ring_more(own_ring, 1, ring_pairs, *ready)
        other_ring = ring_more(other_ring, 1, ring_pairs, *ready)
    blocks = [
        *own_ring,
        *other_ring,
        swapped(own_ring[:cut]),
        swapped(own_ring[cut:]),
        swapped(other_ring[:cut]),
        swapped(other_ring[cut:]),
    ]

    kv_local = kv_half // HEAD_DIM
    spread = spread_columns(kv_local)
    pack = spread.T
    q_local = q_half // HEAD_DIM
    early, kv_cache, queries, keys, values = attention_early(
        spots,
        starts,
        tenant_ids[0],
        jnp.concatenate(embedded, axis=0),
        attention_gain[None, :],
        cosine,
        sine,
        spread,
        blocks,
        q_half,
        q_local,
        kv_local,
    )
    late = attention_late(starts, tenant_ids[0], queries, keys, values, pack, q_local, kv_local)
    finals = []
    for start, attended in zip(embedded, (early, late)):
        residual, part = ffn_part(
            spots,
            core[None],
            start,
            attended,
            lax.ppermute(attended, "tp", PAIR),
            out_weight,
            out_first,
            out_second,
            ffn_gain[None, :],
            down_weight,
            blocks,
            q_half,
        )
        total = part.astype(F32) + lax.ppermute(part, "tp", PAIR).astype(F32)
        finals.append((residual + total).astype(BF))
    return (jnp.concatenate(finals, axis=0), kv_cache)


def solution(mesh):
    return jax.shard_map(
        per_device,
        mesh=mesh,
        in_specs=(
            P("req"),
            P("req", None),
            P("req", None),
            P("req", None),
            P(),
            P(("tp", "req"), None),
            P("tp", None),
            P(),
            P(("tp", "req"), None),
            P("tp", None),
        ),
        out_specs=(P("req", None), P(None, "req", "tp")),
        check_vma=False,
    )
```

time: 531 us -> 249 us (0.47)
  waiting for transfers between devices: 325 us -> 83.6 us
  blocking collectives: 73.7 us -> 0 us
  starting transfers between devices: 10.4 us -> 70.3 us
  Pallas kernels: 0 us -> 51.1 us
  matrix products: 40.4 us -> 9.39 us
  local copies, waits for them, and re-layouts: 41.4 us -> 16.8 us
  between operations: 15.9 us -> 1.21 us
  other arithmetic: 22.7 us -> 15.1 us
    all_to_all x1 -> x2, waiting for transfers between devices: 149 us -> 0.01 us  [the longest x1 0.01 us: per_device(): lax.all_to_all(requests.reshape(group_count, capacity), 'req', split_axis...]
    psum x2 -> x0, waiting for transfers between devices: 104 us -> none  [the longest x1 55.3 us: per_device(): lax.psum(jnp.dot(attended, out_weight, preferred_element_type=jnp.float32...]
    ppermute x0 -> x28, waiting for transfers between devices: none -> 83.6 us  [the longest x14 39.3 us: ring_more(): blocks.append(lax.ppermute(last, 'req', pairs))]
    all_to_all x2 -> x0, blocking collectives: 73.7 us -> none  [the longest x1 60 us: per_device(): lax.all_to_all(found_rows, 'req', split_axis=0, concat_axis=0, tiled=True)]
    all_gather x2 -> x0, waiting for transfers between devices: 72.1 us -> none  [the longest x1 47.1 us: per_device(): lax.all_gather(returned[owner_of, slot_of], 'tp', axis=0, tiled=True)]
    ppermute x0 -> x28, starting transfers between devices: none -> 57 us  [the longest x14 45.5 us: ring_more(): blocks.append(lax.ppermute(last, 'req', pairs))]
    pallas_call x0 -> x4, Pallas kernels: none -> 51.1 us  [the longest x2 30.5 us: ffn_part(): pl.pallas_call(functools.partial(ffn_kernel, len(blocks), first_col), out...]
    dot_general x5 -> x2, matrix products: 33 us -> 9.39 us  [the longest x1 7.37 us: per_device(): jnp.dot(pick_rows, embed_table, preferred_element_type=F32).astype(BF)]
  transfers between devices with their start and end apart: 5 -> 30, of which waited for: 5 -> 17; matrix products, arithmetic and copies ran while one was open for 7% -> 14% of each run, Pallas kernels for 0% -> 12%
where the time goes in v3:
time: 249 us; the launch traced here: 247 us
  waiting for transfers between devices  83.6 us (34%)
  starting transfers between devices  70.3 us (28%)
  Pallas kernels  51.1 us (21%)
  local copies, waits for them, and re-layouts  16.8 us (7%)
  other arithmetic  15.1 us (6%)
  matrix products  9.39 us (4%)
    ppermute x14, starting transfers between devices, ring_more(): blocks.append(lax.ppermute(last, 'req', pairs))  45.5 us
    ppermute x14, waiting for transfers between devices, ring_more(): blocks.append(lax.ppermute(last, 'req', pairs))  39.3 us
    pallas_call x2, Pallas kernels, ffn_part(): pl.pallas_call(functools.partial(ffn_kernel, len(blocks), first_col), out...  30.5 us
    ppermute x2, waiting for transfers between devices, per_device(): total = part.astype(F32) + lax.ppermute(part, 'tp', PAIR).astype(F32)  17.2 us
    pallas_call x1, Pallas kernels, attention_early(): pl.pallas_call(functools.partial(project_kernel, q_heads, kv_heads, len(b...  17.1 us
    ppermute x1, waiting for transfers between devices, per_device(): came = lax.ppermute(away, 'tp', PAIR)  16.5 us
    ppermute x2, waiting for transfers between devices, per_device(): lax.ppermute(attended, 'tp', PAIR)  9.87 us
    unnamed x88, local copies, waits for them, and re-layouts  9.02 us
  transfers between devices with their start and end apart: 30, of which 17 were waited for; matrix products, arithmetic and copies ran while one was open for 14% of the time, Pallas kernels for 12%

profile of v3, /device:TPU:0, one launch (start us, length us, event | category | flops | bytes accessed | tf_op | source)
XLA Modules:
  0.0 247.5 jit_solution(11361678426167015354)
XLA Ops:
  2.6 7.4 %all-to-all-start = ((s32[16,1,32]{2,1,0:T(1,128)}), s32[16,1,32]{2,1,0:T(1,128)S(1)}, u32[]{:S(2)}, u32[]{:S(2)}) async-start(s32[16,1,32]{2,1,0:T(1,128)} %sub.101), calls=%async_computation | async-start | bytes 16384 | tf_op jit(solution)/shard_map/all_to_all | solution.py:420
  12.1 1.4 dynamic-slice_convert_fusion.1
  16.5 1.5 collective-permute-start.6
  21.3 1.8 fusion.5
  24.4 7.4 %fusion.1 = bf16[512,1536]{1,0:T(8,128)(2,1)} fusion(bf16[2000,1536]{1,0:T(8,128)(2,1)} %param.13, s32[512]{0:T(512)S(1)} %reshape.105), kind=kOutput, calls=%fused_computation.2 | convolution fusion | flops 3147538432 | bytes 7718912 | tf_op jit(solution)/shard_map/dot_general | solution.py:473
  31.7 5.9 %all-to-all-start.1 = ((bf16[16,32,1536]{2,1,0:T(8,128)(2,1)}), bf16[16,32,1536]{2,1,0:T(8,128)(2,1)}, u32[]{:S(2)}, u32[]{:S(2)}) async-start(bf16[16,32,1536]{2,1,0:T(8,128)(2,1)} %bitcast.4), calls=%async_computation.1 | async-start | bytes 3145728 | tf_op jit(solution)/shard_map/all_to_all | solution.py:474
  37.9 1.9 collective-permute-start.2
  39.8 16.5 %collective-permute-done.11 = bf16[2,48,2816]{2,1,0:T(8,128)(2,1)S(1)} collective-permute-done((bf16[2,48,2816]{2,1,0:T(8,128)(2,1)S(1)}, bf16[2,48,2816]{2,1,0:T(8,128)(2,1)S(1)}, u32[]{:S(2)}, u32[]{:S(2)}) %collective-permute-start.11) | collective-permute-done | bytes 540704 | tf_op jit(solution)/shard_map/ppermute | solution.py:448
  58.1 1.9 collective-permute-start.13
  60.0 10.0 %collective-permute-done.2.refs_1_ = bf16[96,2816]{1,0:T(8,128)(2,1)S(1)} collective-permute-done((bf16[96,2816]{1,0:T(8,128)(2,1)S(1)}, bf16[96,2816]{1,0:T(8,128)(2,1)S(1)}, u32[]{:S(2)}, u32[]{:S(2)}) %collective-permute-start.2) | collective-permute-done | bytes 540704 | tf_op jit(solution)/shard_map/ppermute | solution.py:48
  69.9 10.1 %collective-permute-start.3 = (bf16[96,2816]{1,0:T(8,128)(2,1)S(1)}, bf16[96,2816]{1,0:T(8,128)(2,1)S(1)}, u32[]{:S(2)}, u32[]{:S(2)}) collective-permute-start(bf16[96,2816]{1,0:T(8,128)(2,1)S(1)} %collective-permute-done.2.refs_1_), channel_id=1, source_target_pairs={{0,4},{4,8},{8,12},{12,14},{14,10},{10,6},{6,2},{2,0},{5,1},{9,5},... | collective-permute-start | bytes 1622024 | tf_op jit(solution)/shard_map/ppermute | solution.py:48
  80.9 4.9 %collective-permute-start.14 = (bf16[96,2816]{1,0:T(8,128)(2,1)S(1)}, bf16[96,2816]{1,0:T(8,128)(2,1)}, u32[]{:S(2)}, u32[]{:S(2)}) collective-permute-start(bf16[96,2816]{1,0:T(8,128)(2,1)S(1)} %collective-permute-done.13.refs_9_), channel_id=1, source_target_pairs={{0,4},{4,8},{8,12},{12,14},{14,10},{10,6},{6,2},{2,0},{5,1},{9,5},... | collective-permute-start | bytes 1622024 | tf_op jit(solution)/shard_map/ppermute | solution.py:48
  88.3 2.0 convolution_convert_fusion
  90.4 1.6 collective-permute-start
  92.0 4.2 %collective-permute-start.4 = (bf16[96,2816]{1,0:T(8,128)(2,1)S(1)}, bf16[96,2816]{1,0:T(8,128)(2,1)S(1)}, u32[]{:S(2)}, u32[]{:S(2)}) collective-permute-start(bf16[96,2816]{1,0:T(8,128)(2,1)S(1)} %collective-permute-done.3.refs_2_), channel_id=1, source_target_pairs={{0,4},{4,8},{8,12},{12,14},{14,10},{10,6},{6,2},{2,0},{5,1},{9,5},... | collective-permute-start | bytes 1622024 | tf_op jit(solution)/shard_map/ppermute | solution.py:48
  96.2 2.5 %collective-permute-start.15 = (bf16[96,2816]{1,0:T(8,128)(2,1)}, bf16[96,2816]{1,0:T(8,128)(2,1)S(1)}, u32[]{:S(2)}, u32[]{:S(2)}) collective-permute-start(bf16[96,2816]{1,0:T(8,128)(2,1)} %collective-permute-done.14.refs_10_), channel_id=1, source_target_pairs={{0,4},{4,8},{8,12},{12,14},{14,10},{10,6},{6,2},{2,0},{5,1},{9,5},... | collective-permute-start | bytes 1622024 | tf_op jit(solution)/shard_map/ppermute | solution.py:48
  98.7 1.9 bitcast_dynamic-update-slice_fusion.2
  100.6 2.5 collective-permute-done.4.refs_3_
  103.0 2.5 %collective-permute-start.5 = (bf16[96,2816]{1,0:T(8,128)(2,1)S(1)}, bf16[96,2816]{1,0:T(8,128)(2,1)S(1)}, u32[]{:S(2)}, u32[]{:S(2)}) collective-permute-start(bf16[96,2816]{1,0:T(8,128)(2,1)S(1)} %collective-permute-done.4.refs_3_), channel_id=1, source_target_pairs={{0,4},{4,8},{8,12},{12,14},{14,10},{10,6},{6,2},{2,0},{5,1},{9,5},... | collective-permute-start | bytes 1622024 | tf_op jit(solution)/shard_map/ppermute | solution.py:48
  105.5 3.4 %collective-permute-done.15.refs_11_ = bf16[96,2816]{1,0:T(8,128)(2,1)S(1)} collective-permute-done((bf16[96,2816]{1,0:T(8,128)(2,1)}, bf16[96,2816]{1,0:T(8,128)(2,1)S(1)}, u32[]{:S(2)}, u32[]{:S(2)}) %collective-permute-start.15) | collective-permute-done | bytes 540704 | tf_op jit(solution)/shard_map/ppermute | solution.py:48
  108.9 2.5 %collective-permute-start.16 = (bf16[96,2816]{1,0:T(8,128)(2,1)S(1)}, bf16[96,2816]{1,0:T(8,128)(2,1)S(1)}, u32[]{:S(2)}, u32[]{:S(2)}) collective-permute-start(bf16[96,2816]{1,0:T(8,128)(2,1)S(1)} %collective-permute-done.15.refs_11_), channel_id=1, source_target_pairs={{0,4},{4,8},{8,12},{12,14},{14,10},{10,6},{6,2},{2,0},{5,1},{9,5},... | collective-permute-start | bytes 1622024 | tf_op jit(solution)/shard_map/ppermute | solution.py:48
  112.3 2.3 collective-permute-done.5.refs_4_
  114.6 2.5 %collective-permute-start.8 = (bf16[96,2816]{1,0:T(8,128)(2,1)S(1)}, bf16[96,2816]{1,0:T(8,128)(2,1)S(1)}, u32[]{:S(2)}, u32[]{:S(2)}) collective-permute-start(bf16[96,2816]{1,0:T(8,128)(2,1)S(1)} %collective-permute-done.5.refs_4_), channel_id=1, source_target_pairs={{0,4},{4,8},{8,12},{12,14},{14,10},{10,6},{6,2},{2,0},{5,1},{9,5},... | collective-permute-start | bytes 1622024 | tf_op jit(solution)/shard_map/ppermute | solution.py:48
  117.9 2.5 %collective-permute-done.16.refs_12_ = bf16[96,2816]{1,0:T(8,128)(2,1)S(1)} collective-permute-done((bf16[96,2816]{1,0:T(8,128)(2,1)S(1)}, bf16[96,2816]{1,0:T(8,128)(2,1)S(1)}, u32[]{:S(2)}, u32[]{:S(2)}) %collective-permute-start.16) | collective-permute-done | bytes 540704 | tf_op jit(solution)/shard_map/ppermute | solution.py:48
  120.4 2.5 %collective-permute-start.17 = (bf16[96,2816]{1,0:T(8,128)(2,1)S(1)}, bf16[96,2816]{1,0:T(8,128)(2,1)S(1)}, u32[]{:S(2)}, u32[]{:S(2)}) collective-permute-start(bf16[96,2816]{1,0:T(8,128)(2,1)S(1)} %collective-permute-done.16.refs_12_), channel_id=1, source_target_pairs={{0,4},{4,8},{8,12},{12,14},{14,10},{10,6},{6,2},{2,0},{5,1},{9,5},... | collective-permute-start | bytes 1622024 | tf_op jit(solution)/shard_map/ppermute | solution.py:48
  122.9 3.3 %collective-permute-done.8.refs_5_ = bf16[96,2816]{1,0:T(8,128)(2,1)S(1)} collective-permute-done((bf16[96,2816]{1,0:T(8,128)(2,1)S(1)}, bf16[96,2816]{1,0:T(8,128)(2,1)S(1)}, u32[]{:S(2)}, u32[]{:S(2)}) %collective-permute-start.8) | collective-permute-done | bytes 540704 | tf_op jit(solution)/shard_map/ppermute | solution.py:48
  126.2 2.5 %collective-permute-start.9 = (bf16[96,2816]{1,0:T(8,128)(2,1)S(1)}, bf16[96,2816]{1,0:T(8,128)(2,1)S(1)}, u32[]{:S(2)}, u32[]{:S(2)}) collective-permute-start(bf16[96,2816]{1,0:T(8,128)(2,1)S(1)} %collective-permute-done.8.refs_5_), channel_id=1, source_target_pairs={{0,4},{4,8},{8,12},{12,14},{14,10},{10,6},{6,2},{2,0},{5,1},{9,5},... | collective-permute-start | bytes 1622024 | tf_op jit(solution)/shard_map/ppermute | solution.py:48
  129.6 2.4 collective-permute-done.17.refs_13_
  132.0 2.5 %collective-permute-start.18 = (bf16[96,2816]{1,0:T(8,128)(2,1)S(1)}, bf16[96,2816]{1,0:T(8,128)(2,1)}, u32[]{:S(2)}, u32[]{:S(2)}) collective-permute-start(bf16[96,2816]{1,0:T(8,128)(2,1)S(1)} %collective-permute-done.17.refs_13_), channel_id=1, source_target_pairs={{0,4},{4,8},{8,12},{12,14},{14,10},{10,6},{6,2},{2,0},{5,1},{9,5},... | collective-permute-start | bytes 1622024 | tf_op jit(solution)/shard_map/ppermute | solution.py:48
  134.5 3.3 %collective-permute-done.9.refs_6_ = bf16[96,2816]{1,0:T(8,128)(2,1)S(1)} collective-permute-done((bf16[96,2816]{1,0:T(8,128)(2,1)S(1)}, bf16[96,2816]{1,0:T(8,128)(2,1)S(1)}, u32[]{:S(2)}, u32[]{:S(2)}) %collective-permute-start.9) | collective-permute-done | bytes 540704 | tf_op jit(solution)/shard_map/ppermute | solution.py:48
  137.8 2.5 %collective-permute-start.10 = (bf16[96,2816]{1,0:T(8,128)(2,1)S(1)}, bf16[96,2816]{1,0:T(8,128)(2,1)S(1)}, u32[]{:S(2)}, u32[]{:S(2)}) collective-permute-start(bf16[96,2816]{1,0:T(8,128)(2,1)S(1)} %collective-permute-done.9.refs_6_), channel_id=1, source_target_pairs={{0,4},{4,8},{8,12},{12,14},{14,10},{10,6},{6,2},{2,0},{5,1},{9,5},... | collective-permute-start | bytes 1622024 | tf_op jit(solution)/shard_map/ppermute | solution.py:48
  141.2 2.4 collective-permute-done.18.refs_14_
  143.6 2.6 %collective-permute-start.19 = (bf16[96,2816]{1,0:T(8,128)(2,1)}, bf16[96,2816]{1,0:T(8,128)(2,1)}, u32[]{:S(2)}, u32[]{:S(2)}) collective-permute-start(bf16[96,2816]{1,0:T(8,128)(2,1)} %collective-permute-done.18.refs_14_), channel_id=1, source_target_pairs={{0,4},{4,8},{8,12},{12,14},{14,10},{10,6},{6,2},{2,0},{5,1},{9,5},... | collective-permute-start | bytes 1622024 | tf_op jit(solution)/shard_map/ppermute | solution.py:48
  146.5 2.9 %collective-permute-done.10.refs_7_ = bf16[96,2816]{1,0:T(8,128)(2,1)S(1)} collective-permute-done((bf16[96,2816]{1,0:T(8,128)(2,1)S(1)}, bf16[96,2816]{1,0:T(8,128)(2,1)S(1)}, u32[]{:S(2)}, u32[]{:S(2)}) %collective-permute-start.10) | collective-permute-done | bytes 540704 | tf_op jit(solution)/shard_map/ppermute | solution.py:48
  150.2 1.8 collective-permute-start.21
  152.0 3.3 %collective-permute-done.19.refs_15_ = bf16[96,2816]{1,0:T(8,128)(2,1)} collective-permute-done((bf16[96,2816]{1,0:T(8,128)(2,1)}, bf16[96,2816]{1,0:T(8,128)(2,1)}, u32[]{:S(2)}, u32[]{:S(2)}) %collective-permute-start.19) | collective-permute-done | bytes 540704 | tf_op jit(solution)/shard_map/ppermute | solution.py:48
  155.3 1.5 pad_maximum_fusion.1
  156.8 1.4 collective-permute-start.23
  158.2 1.3 pad_add_fusion.2.start_ref
  163.1 17.1 %attention_early.1 = (bf16[256,768]{1,0:T(8,128)(2,1)S(1)}, bf16[2,512,384]{2,1,0:T(8,128)(2,1)}, bf16[256,1024]{1,0:T(8,128)(2,1)S(1)}, bf16[512,512]{1,0:T(8,128)(2,1)S(1)}, bf16[512,512]{1,0:T(8,128)(2,1)S(1)}) custom-call(s32[2,32]{1,0:T(2,128)S(1)} %pad_add_fusion.spots_ref, s32[4]{0:T(128)S(1)} %pad_add_fusion.2.start_ref, s32[4]{0:T(128)S(1)} %bitcast.52, ...), custom_call_target="tpu_custom_call" | custom-call | flops 5637144576 | bytes 17301504 | tf_op jit(solution)/shard_map/attention_early/pallas_call | solution.py:213
  180.3 3.5 %attention_late.1.own_ref = bf16[256,768]{1,0:T(8,128)(2,1)S(1)} custom-call(s32[4]{0:T(128)S(1)} %pad_add_fusion.2.start_ref, s32[4]{0:T(128)S(1)} %bitcast.53, bf16[256,1024]{1,0:T(8,128)(2,1)S(1)} %get-tuple-element.24.q_ref, bf16[512,512]{1,0:T(8,128)(2,1)S(1)} %get-tuple-element.25.keys, bf16[512,512]{1,0:T(8,128)(2,1)S(1)} %get-tuple-element.26.values, ...), custom_call_target="tpu_custom_call" | custom-call | flops 536870912 | bytes 2097152 | tf_op jit(solution)/shard_map/attention_late/pallas_call | solution.py:246
  184.3 1.6 collective-permute-start.24
  185.9 9.9 %collective-permute-done.26.other_ref = bf16[256,768]{1,0:T(8,128)(2,1)S(1)} collective-permute-done((bf16[256,768]{1,0:T(8,128)(2,1)S(1)}, bf16[256,768]{1,0:T(8,128)(2,1)S(1)}, u32[]{:S(2)}, u32[]{:S(2)}) %collective-permute-start.26) | collective-permute-done | bytes 393248 | tf_op jit(solution)/shard_map/ppermute | solution.py:538
  195.8 15.2 %ffn_part.3 = (f32[256,1536]{1,0:T(8,128)}, bf16[256,1536]{1,0:T(8,128)(2,1)}) custom-call(s32[2,32]{1,0:T(2,128)S(1)} %pad_add_fusion.spots_ref, s32[1]{0:T(128)} %bitcast.core_ref, bf16[256,1536]{1,0:T(8,128)(2,1)} %copy-done.18, bf16[256,768]{1,0:T(8,128)(2,1)S(1)} %attention_late.1.own_ref, bf16[256,768]{1,0:T(8,128)(2,1)S(1)} %collective-permute-done.26.other_ref, ...), custom_call_target="tpu_custom_call" | custom-call | flops 6039797760 | bytes 23592960 | tf_op jit(solution)/shard_map/ffn_part/pallas_call | solution.py:342
  211.6 15.3 %ffn_part.2 = (f32[256,1536]{1,0:T(8,128)}, bf16[256,1536]{1,0:T(8,128)(2,1)}) custom-call(s32[2,32]{1,0:T(2,128)S(1)} %pad_add_fusion.spots_ref, s32[1]{0:T(128)} %bitcast.core_ref, bf16[256,1536]{1,0:T(8,128)(2,1)} %copy-done.17, bf16[256,768]{1,0:T(8,128)(2,1)S(1)} %get-tuple-element.21.own_ref, bf16[256,768]{1,0:T(8,128)(2,1)S(1)} %collective-permute-done.24.other_ref, ...), custom_call_target="tpu_custom_call" | custom-call | flops 6039797760 | bytes 23592960 | tf_op jit(solution)/shard_map/ffn_part/pallas_call | solution.py:342
  226.9 1.5 collective-permute-start.25
  228.4 1.8 collective-permute-done.27
  230.5 15.4 %collective-permute-done.25 = bf16[256,1536]{1,0:T(8,128)(2,1)S(1)} collective-permute-done((bf16[256,1536]{1,0:T(8,128)(2,1)}, bf16[256,1536]{1,0:T(8,128)(2,1)S(1)}, u32[]{:S(2)}, u32[]{:S(2)}) %collective-permute-start.25) | collective-permute-done | bytes 786464 | tf_op jit(solution)/shard_map/ppermute | solution.py:547
  (156 shorter events, 27.8 us)
Async XLA Ops:
  2.6 20.5 %all-to-all-start = ((s32[16,1,32]{2,1,0:T(1,128)}), s32[16,1,32]{2,1,0:T(1,128)S(1)}, u32[]{:S(2)}, u32[]{:S(2)}) async-start(s32[16,1,32]{2,1,0:T(1,128)} %sub.101), calls=%async_computation | async-start | bytes 16384 | tf_op jit(solution)/shard_map/all_to_all | solution.py:420
  15.0 22.7 %collective-permute-start.1 = (bf16[48,2816]{1,0:T(8,128)(2,1)}, bf16[48,2816]{1,0:T(8,128)(2,1)S(1)}, u32[]{:S(2)}, u32[]{:S(2)}) collective-permute-start(bf16[48,2816]{1,0:T(8,128)(2,1)} %broadcast_select_fusion.5), channel_id=1, source_target_pairs={{0,1},{1,0},{2,3},{3,2},{4,5},{5,4},{6,7},{7,6},{8,9},{9,8},{10,11... | collective-permute-start | bytes 811016 | tf_op jit(solution)/shard_map/ppermute | solution.py:441
  16.5 64.4 %collective-permute-start.6 = (bf16[384,1536]{1,0:T(8,128)(2,1)}, bf16[384,1536]{1,0:T(8,128)(2,1)}, u32[]{:S(2)}, u32[]{:S(2)}) collective-permute-start(bf16[384,1536]{1,0:T(8,128)(2,1)} %constant_dynamic-slice_fusion), channel_id=1, source_target_pairs={{0,16},{16,0},{1,17},{17,1},{2,18},{18,2},{3,19},{19,3},{4,20},{20... | collective-permute-start | bytes 3538952 | tf_op jit(solution)/shard_map/ppermute | solution.py:490
  18.1 38.2 %collective-permute-start.11 = (bf16[2,48,2816]{2,1,0:T(8,128)(2,1)S(1)}, bf16[2,48,2816]{2,1,0:T(8,128)(2,1)S(1)}, u32[]{:S(2)}, u32[]{:S(2)}) collective-permute-start(bf16[2,48,2816]{2,1,0:T(8,128)(2,1)S(1)} %pad_maximum_fusion.5), channel_id=1, source_target_pairs={{0,16},{16,0},{1,17},{17,1},{2,18},{18,2},{3,19},{19,3},{4,20},{20... | collective-permute-start | bytes 1622024 | tf_op jit(solution)/shard_map/ppermute | solution.py:448
  31.7 56.6 %all-to-all-start.1 = ((bf16[16,32,1536]{2,1,0:T(8,128)(2,1)}), bf16[16,32,1536]{2,1,0:T(8,128)(2,1)}, u32[]{:S(2)}, u32[]{:S(2)}) async-start(bf16[16,32,1536]{2,1,0:T(8,128)(2,1)} %bitcast.4), calls=%async_computation.1 | async-start | bytes 3145728 | tf_op jit(solution)/shard_map/all_to_all | solution.py:474
  37.9 32.0 %collective-permute-start.2 = (bf16[96,2816]{1,0:T(8,128)(2,1)S(1)}, bf16[96,2816]{1,0:T(8,128)(2,1)S(1)}, u32[]{:S(2)}, u32[]{:S(2)}) collective-permute-start(bf16[96,2816]{1,0:T(8,128)(2,1)S(1)} %pad_maximum_fusion.4.refs_0_), channel_id=1, source_target_pairs={{0,4},{4,8},{8,12},{12,14},{14,10},{10,6},{6,2},{2,0},{5,1},{9,5},... | collective-permute-start | bytes 1622024 | tf_op jit(solution)/shard_map/ppermute | solution.py:48
  56.3 1.6 collective-permute-start.12
  58.0 30.3 %copy-start.6 = (bf16[96,2816]{1,0:T(8,128)(2,1)}, bf16[96,2816]{1,0:T(8,128)(2,1)S(1)}, u32[]{:S(2)}) copy-start(bf16[96,2816]{1,0:T(8,128)(2,1)S(1)} %pad_maximum_fusion.6.refs_8_) | copy-start | bytes 1622020
  58.1 22.9 %collective-permute-start.13 = (bf16[96,2816]{1,0:T(8,128)(2,1)S(1)}, bf16[96,2816]{1,0:T(8,128)(2,1)S(1)}, u32[]{:S(2)}, u32[]{:S(2)}) collective-permute-start(bf16[96,2816]{1,0:T(8,128)(2,1)S(1)} %pad_maximum_fusion.6.refs_8_), channel_id=1, source_target_pairs={{0,4},{4,8},{8,12},{12,14},{14,10},{10,6},{6,2},{2,0},{5,1},{9,5},... | collective-permute-start | bytes 1622024 | tf_op jit(solution)/shard_map/ppermute | solution.py:48
  69.9 17.0 %collective-permute-start.3 = (bf16[96,2816]{1,0:T(8,128)(2,1)S(1)}, bf16[96,2816]{1,0:T(8,128)(2,1)S(1)}, u32[]{:S(2)}, u32[]{:S(2)}) collective-permute-start(bf16[96,2816]{1,0:T(8,128)(2,1)S(1)} %collective-permute-done.2.refs_1_), channel_id=1, source_target_pairs={{0,4},{4,8},{8,12},{12,14},{14,10},{10,6},{6,2},{2,0},{5,1},{9,5},... | collective-permute-start | bytes 1622024 | tf_op jit(solution)/shard_map/ppermute | solution.py:48
  80.9 31.4 %collective-permute-start.7 = (bf16[384,1536]{1,0:T(8,128)(2,1)}, bf16[384,1536]{1,0:T(8,128)(2,1)}, u32[]{:S(2)}, u32[]{:S(2)}) collective-permute-start(bf16[384,1536]{1,0:T(8,128)(2,1)} %collective-permute-done.6.w_first_ref), channel_id=1, source_target_pairs={{0,1},{1,0},{2,3},{3,2},{4,5},{5,4},{6,7},{7,6},{8,9},{9,8},{10,11... | collective-permute-start | bytes 3538952 | tf_op jit(solution)/shard_map/ppermute | solution.py:493
  80.9 15.2 %collective-permute-start.14 = (bf16[96,2816]{1,0:T(8,128)(2,1)S(1)}, bf16[96,2816]{1,0:T(8,128)(2,1)}, u32[]{:S(2)}, u32[]{:S(2)}) collective-permute-start(bf16[96,2816]{1,0:T(8,128)(2,1)S(1)} %collective-permute-done.13.refs_9_), channel_id=1, source_target_pairs={{0,4},{4,8},{8,12},{12,14},{14,10},{10,6},{6,2},{2,0},{5,1},{9,5},... | collective-permute-start | bytes 1622024 | tf_op jit(solution)/shard_map/ppermute | solution.py:48
  90.4 39.2 %copy-start.25 = (bf16[256,1536]{1,0:T(8,128)(2,1)}, bf16[256,1536]{1,0:T(8,128)(2,1)S(1)}, u32[]{:S(2)}) copy-start(bf16[256,1536]{1,0:T(8,128)(2,1)S(1)} %convolution_convert_fusion) | copy-start | bytes 2359300
  90.4 21.9 %collective-permute-start = (bf16[256,1536]{1,0:T(8,128)(2,1)S(1)}, bf16[256,1536]{1,0:T(8,128)(2,1)S(1)}, u32[]{:S(2)}, u32[]{:S(2)}) collective-permute-start(bf16[256,1536]{1,0:T(8,128)(2,1)S(1)} %convolution_convert_fusion), channel_id=1, source_target_pairs={{0,16},{16,0},{1,17},{17,1},{2,18},{18,2},{3,19},{19,3},{4,20},{20... | collective-permute-start | bytes 2359304 | tf_op jit(solution)/shard_map/ppermute | solution.py:483
  92.0 11.1 %collective-permute-start.4 = (bf16[96,2816]{1,0:T(8,128)(2,1)S(1)}, bf16[96,2816]{1,0:T(8,128)(2,1)S(1)}, u32[]{:S(2)}, u32[]{:S(2)}) collective-permute-start(bf16[96,2816]{1,0:T(8,128)(2,1)S(1)} %collective-permute-done.3.refs_2_), channel_id=1, source_target_pairs={{0,4},{4,8},{8,12},{12,14},{14,10},{10,6},{6,2},{2,0},{5,1},{9,5},... | collective-permute-start | bytes 1622024 | tf_op jit(solution)/shard_map/ppermute | solution.py:48
  96.2 12.8 %collective-permute-start.15 = (bf16[96,2816]{1,0:T(8,128)(2,1)}, bf16[96,2816]{1,0:T(8,128)(2,1)S(1)}, u32[]{:S(2)}, u32[]{:S(2)}) collective-permute-start(bf16[96,2816]{1,0:T(8,128)(2,1)} %collective-permute-done.14.refs_10_), channel_id=1, source_target_pairs={{0,4},{4,8},{8,12},{12,14},{14,10},{10,6},{6,2},{2,0},{5,1},{9,5},... | collective-permute-start | bytes 1622024 | tf_op jit(solution)/shard_map/ppermute | solution.py:48
  103.0 11.6 %collective-permute-start.5 = (bf16[96,2816]{1,0:T(8,128)(2,1)S(1)}, bf16[96,2816]{1,0:T(8,128)(2,1)S(1)}, u32[]{:S(2)}, u32[]{:S(2)}) collective-permute-start(bf16[96,2816]{1,0:T(8,128)(2,1)S(1)} %collective-permute-done.4.refs_3_), channel_id=1, source_target_pairs={{0,4},{4,8},{8,12},{12,14},{14,10},{10,6},{6,2},{2,0},{5,1},{9,5},... | collective-permute-start | bytes 1622024 | tf_op jit(solution)/shard_map/ppermute | solution.py:48
  108.9 11.5 %collective-permute-start.16 = (bf16[96,2816]{1,0:T(8,128)(2,1)S(1)}, bf16[96,2816]{1,0:T(8,128)(2,1)S(1)}, u32[]{:S(2)}, u32[]{:S(2)}) collective-permute-start(bf16[96,2816]{1,0:T(8,128)(2,1)S(1)} %collective-permute-done.15.refs_11_), channel_id=1, source_target_pairs={{0,4},{4,8},{8,12},{12,14},{14,10},{10,6},{6,2},{2,0},{5,1},{9,5},... | collective-permute-start | bytes 1622024 | tf_op jit(solution)/shard_map/ppermute | solution.py:48
  112.3 34.1 %copy-start.38 = (f32[1536]{0:T(1024)S(1)}, f32[1536]{0:T(1024)}, u32[]{:S(2)}) copy-start(f32[1536]{0:T(1024)} %param.14) | copy-start | bytes 18436
  112.3 33.9 %copy-start.31 = (bf16[256,1536]{1,0:T(8,128)(2,1)}, bf16[256,1536]{1,0:T(8,128)(2,1)S(1)}, u32[]{:S(2)}) copy-start(bf16[256,1536]{1,0:T(8,128)(2,1)S(1)} %collective-permute-done) | copy-start | bytes 2359300
  114.6 19.9 %copy-start.12 = (bf16[96,2816]{1,0:T(8,128)(2,1)}, bf16[96,2816]{1,0:T(8,128)(2,1)S(1)}, u32[]{:S(2)}) copy-start(bf16[96,2816]{1,0:T(8,128)(2,1)S(1)} %collective-permute-done.5.refs_4_) | copy-start | bytes 1622020
  114.6 11.6 %collective-permute-start.8 = (bf16[96,2816]{1,0:T(8,128)(2,1)S(1)}, bf16[96,2816]{1,0:T(8,128)(2,1)S(1)}, u32[]{:S(2)}, u32[]{:S(2)}) collective-permute-start(bf16[96,2816]{1,0:T(8,128)(2,1)S(1)} %collective-permute-done.5.refs_4_), channel_id=1, source_target_pairs={{0,4},{4,8},{8,12},{12,14},{14,10},{10,6},{6,2},{2,0},{5,1},{9,5},... | collective-permute-start | bytes 1622024 | tf_op jit(solution)/shard_map/ppermute | solution.py:48
  120.4 23.2 %copy-start.24 = (bf16[96,2816]{1,0:T(8,128)(2,1)}, bf16[96,2816]{1,0:T(8,128)(2,1)S(1)}, u32[]{:S(2)}) copy-start(bf16[96,2816]{1,0:T(8,128)(2,1)S(1)} %collective-permute-done.16.refs_12_) | copy-start | bytes 1622020
  120.4 11.6 %collective-permute-start.17 = (bf16[96,2816]{1,0:T(8,128)(2,1)S(1)}, bf16[96,2816]{1,0:T(8,128)(2,1)S(1)}, u32[]{:S(2)}, u32[]{:S(2)}) collective-permute-start(bf16[96,2816]{1,0:T(8,128)(2,1)S(1)} %collective-permute-done.16.refs_12_), channel_id=1, source_target_pairs={{0,4},{4,8},{8,12},{12,14},{14,10},{10,6},{6,2},{2,0},{5,1},{9,5},... | collective-permute-start | bytes 1622024 | tf_op jit(solution)/shard_map/ppermute | solution.py:48
  126.2 23.4 %copy-start = (bf16[96,2816]{1,0:T(8,128)(2,1)}, bf16[96,2816]{1,0:T(8,128)(2,1)S(1)}, u32[]{:S(2)}) copy-start(bf16[96,2816]{1,0:T(8,128)(2,1)S(1)} %collective-permute-done.8.refs_5_) | copy-start | bytes 1622020
  126.2 11.6 %collective-permute-start.9 = (bf16[96,2816]{1,0:T(8,128)(2,1)S(1)}, bf16[96,2816]{1,0:T(8,128)(2,1)S(1)}, u32[]{:S(2)}, u32[]{:S(2)}) collective-permute-start(bf16[96,2816]{1,0:T(8,128)(2,1)S(1)} %collective-permute-done.8.refs_5_), channel_id=1, source_target_pairs={{0,4},{4,8},{8,12},{12,14},{14,10},{10,6},{6,2},{2,0},{5,1},{9,5},... | collective-permute-start | bytes 1622024 | tf_op jit(solution)/shard_map/ppermute | solution.py:48
  129.6 31.7 %collective-permute-start.20 = (bf16[5,96,2816]{2,1,0:T(8,128)(2,1)}, bf16[5,96,2816]{2,1,0:T(8,128)(2,1)}, u32[]{:S(2)}, u32[]{:S(2)}) collective-permute-start(bf16[5,96,2816]{2,1,0:T(8,128)(2,1)} %bitcast_dynamic-update-slice_fusion.5), channel_id=1, source_target_pairs={{0,1},{1,0},{2,3},{3,2},{4,5},{5,4},{6,7},{7,6},{8,9},{9,8},{10,11... | collective-permute-start | bytes 8110088 | tf_op jit(solution)/shard_map/ppermute | solution.py:496
  132.0 11.6 %collective-permute-start.18 = (bf16[96,2816]{1,0:T(8,128)(2,1)S(1)}, bf16[96,2816]{1,0:T(8,128)(2,1)}, u32[]{:S(2)}, u32[]{:S(2)}) collective-permute-start(bf16[96,2816]{1,0:T(8,128)(2,1)S(1)} %collective-permute-done.17.refs_13_), channel_id=1, source_target_pairs={{0,4},{4,8},{8,12},{12,14},{14,10},{10,6},{6,2},{2,0},{5,1},{9,5},... | collective-permute-start | bytes 1622024 | tf_op jit(solution)/shard_map/ppermute | solution.py:48
  137.8 11.6 %collective-permute-start.10 = (bf16[96,2816]{1,0:T(8,128)(2,1)S(1)}, bf16[96,2816]{1,0:T(8,128)(2,1)S(1)}, u32[]{:S(2)}, u32[]{:S(2)}) collective-permute-start(bf16[96,2816]{1,0:T(8,128)(2,1)S(1)} %collective-permute-done.9.refs_6_), channel_id=1, source_target_pairs={{0,4},{4,8},{8,12},{12,14},{14,10},{10,6},{6,2},{2,0},{5,1},{9,5},... | collective-permute-start | bytes 1622024 | tf_op jit(solution)/shard_map/ppermute | solution.py:48
  141.1 20.2 %collective-permute-start.22 = (bf16[5,96,2816]{2,1,0:T(8,128)(2,1)}, bf16[5,96,2816]{2,1,0:T(8,128)(2,1)}, u32[]{:S(2)}, u32[]{:S(2)}) collective-permute-start(bf16[5,96,2816]{2,1,0:T(8,128)(2,1)} %bitcast_dynamic-update-slice_fusion), channel_id=1, source_target_pairs={{0,1},{1,0},{2,3},{3,2},{4,5},{5,4},{6,7},{7,6},{8,9},{9,8},{10,11... | collective-permute-start | bytes 8110088 | tf_op jit(solution)/shard_map/ppermute | solution.py:496
  143.6 11.7 %collective-permute-start.19 = (bf16[96,2816]{1,0:T(8,128)(2,1)}, bf16[96,2816]{1,0:T(8,128)(2,1)}, u32[]{:S(2)}, u32[]{:S(2)}) collective-permute-start(bf16[96,2816]{1,0:T(8,128)(2,1)} %collective-permute-done.18.refs_14_), channel_id=1, source_target_pairs={{0,4},{4,8},{8,12},{12,14},{14,10},{10,6},{6,2},{2,0},{5,1},{9,5},... | collective-permute-start | bytes 1622024 | tf_op jit(solution)/shard_map/ppermute | solution.py:48
  150.2 11.1 %collective-permute-start.21 = (bf16[3,96,2816]{2,1,0:T(8,128)(2,1)S(1)}, bf16[3,96,2816]{2,1,0:T(8,128)(2,1)S(1)}, u32[]{:S(2)}, u32[]{:S(2)}) collective-permute-start(bf16[3,96,2816]{2,1,0:T(8,128)(2,1)S(1)} %pad_maximum_fusion), channel_id=1, source_target_pairs={{0,1},{1,0},{2,3},{3,2},{4,5},{5,4},{6,7},{7,6},{8,9},{9,8},{10,11... | collective-permute-start | bytes 4866056 | tf_op jit(solution)/shard_map/ppermute | solution.py:496
  156.8 4.5 %collective-permute-start.23 = (bf16[3,96,2816]{2,1,0:T(8,128)(2,1)S(1)}, bf16[3,96,2816]{2,1,0:T(8,128)(2,1)S(1)}, u32[]{:S(2)}, u32[]{:S(2)}) collective-permute-start(bf16[3,96,2816]{2,1,0:T(8,128)(2,1)S(1)} %pad_maximum_fusion.1), channel_id=1, source_target_pairs={{0,1},{1,0},{2,3},{3,2},{4,5},{5,4},{6,7},{7,6},{8,9},{9,8},{10,11... | collective-permute-start | bytes 4866056 | tf_op jit(solution)/shard_map/ppermute | solution.py:496
  160.0 20.2 %copy-start.17 = (bf16[256,1536]{1,0:T(8,128)(2,1)}, bf16[256,1536]{1,0:T(8,128)(2,1)S(1)}, u32[]{:S(2)}) copy-start(bf16[256,1536]{1,0:T(8,128)(2,1)S(1)} %get-tuple-element.36.emb_ref) | copy-start | bytes 2359300
  160.0 20.2 %copy-start.18 = (bf16[256,1536]{1,0:T(8,128)(2,1)}, bf16[256,1536]{1,0:T(8,128)(2,1)S(1)}, u32[]{:S(2)}) copy-start(bf16[256,1536]{1,0:T(8,128)(2,1)S(1)} %get-tuple-element.37.emb_ref) | copy-start | bytes 2359300
  163.0 32.8 %copy-start.9 = (bf16[96,2816]{1,0:T(8,128)(2,1)S(1)}, bf16[96,2816]{1,0:T(8,128)(2,1)}, u32[]{:S(2)}) copy-start(bf16[96,2816]{1,0:T(8,128)(2,1)} %copy-done.8) | copy-start | bytes 1622020
  180.2 15.6 %copy-start.1 = (bf16[96,2816]{1,0:T(8,128)(2,1)S(1)}, bf16[96,2816]{1,0:T(8,128)(2,1)}, u32[]{:S(2)}) copy-start(bf16[96,2816]{1,0:T(8,128)(2,1)} %copy-done) | copy-start | bytes 1622020
  180.2 15.6 %copy-start.3 = (bf16[96,2816]{1,0:T(8,128)(2,1)S(1)}, bf16[96,2816]{1,0:T(8,128)(2,1)}, u32[]{:S(2)}) copy-start(bf16[96,2816]{1,0:T(8,128)(2,1)} %copy-done.2) | copy-start | bytes 1622020
  180.2 15.6 %copy-start.5 = (bf16[96,2816]{1,0:T(8,128)(2,1)S(1)}, bf16[96,2816]{1,0:T(8,128)(2,1)}, u32[]{:S(2)}) copy-start(bf16[96,2816]{1,0:T(8,128)(2,1)} %copy-done.4) | copy-start | bytes 1622020
  180.3 15.6 %copy-start.7 = (bf16[96,2816]{1,0:T(8,128)(2,1)S(1)}, bf16[96,2816]{1,0:T(8,128)(2,1)}, u32[]{:S(2)}) copy-start(bf16[96,2816]{1,0:T(8,128)(2,1)} %copy-done.6) | copy-start | bytes 1622020
  183.8 12.0 %collective-permute-start.26 = (bf16[256,768]{1,0:T(8,128)(2,1)S(1)}, bf16[256,768]{1,0:T(8,128)(2,1)S(1)}, u32[]{:S(2)}, u32[]{:S(2)}) collective-permute-start(bf16[256,768]{1,0:T(8,128)(2,1)S(1)} %attention_late.1.own_ref), channel_id=1, source_target_pairs={{0,16},{16,0},{1,17},{17,1},{2,18},{18,2},{3,19},{19,3},{4,20},{20... | collective-permute-start | bytes 1179656 | tf_op jit(solution)/shard_map/ppermute | solution.py:538
  184.3 27.3 %collective-permute-start.24 = (bf16[256,768]{1,0:T(8,128)(2,1)S(1)}, bf16[256,768]{1,0:T(8,128)(2,1)S(1)}, u32[]{:S(2)}, u32[]{:S(2)}) collective-permute-start(bf16[256,768]{1,0:T(8,128)(2,1)S(1)} %get-tuple-element.21.own_ref), channel_id=1, source_target_pairs={{0,16},{16,0},{1,17},{17,1},{2,18},{18,2},{3,19},{19,3},{4,20},{20... | collective-permute-start | bytes 1179656 | tf_op jit(solution)/shard_map/ppermute | solution.py:538
  211.0 19.2 %copy-start.29 = (f32[256,1536]{1,0:T(8,128)S(1)}, f32[256,1536]{1,0:T(8,128)}, u32[]{:S(2)}) copy-start(f32[256,1536]{1,0:T(8,128)} %get-tuple-element.27) | copy-start | bytes 4718596
  211.0 19.2 %copy-start.33 = (bf16[256,1536]{1,0:T(8,128)(2,1)S(1)}, bf16[256,1536]{1,0:T(8,128)(2,1)}, u32[]{:S(2)}) copy-start(bf16[256,1536]{1,0:T(8,128)(2,1)} %get-tuple-element.28) | copy-start | bytes 2359300
  211.0 19.2 %collective-permute-start.27 = (bf16[256,1536]{1,0:T(8,128)(2,1)}, bf16[256,1536]{1,0:T(8,128)(2,1)S(1)}, u32[]{:S(2)}, u32[]{:S(2)}) collective-permute-start(bf16[256,1536]{1,0:T(8,128)(2,1)} %get-tuple-element.28), channel_id=1, source_target_pairs={{0,16},{16,0},{1,17},{17,1},{2,18},{18,2},{3,19},{19,3},{4,20},{20... | collective-permute-start | bytes 2359304 | tf_op jit(solution)/shard_map/ppermute | solution.py:547
  226.9 19.0 %collective-permute-start.25 = (bf16[256,1536]{1,0:T(8,128)(2,1)}, bf16[256,1536]{1,0:T(8,128)(2,1)S(1)}, u32[]{:S(2)}, u32[]{:S(2)}) collective-permute-start(bf16[256,1536]{1,0:T(8,128)(2,1)} %get-tuple-element.23), channel_id=1, source_target_pairs={{0,16},{16,0},{1,17},{17,1},{2,18},{18,2},{3,19},{19,3},{4,20},{20... | collective-permute-start | bytes 2359304 | tf_op jit(solution)/shard_map/ppermute | solution.py:547
  230.2 15.7 %copy-start.30 = (f32[256,1536]{1,0:T(8,128)S(1)}, f32[256,1536]{1,0:T(8,128)}, u32[]{:S(2)}) copy-start(f32[256,1536]{1,0:T(8,128)} %get-tuple-element.22) | copy-start | bytes 4718596
  230.2 15.7 %copy-start.34 = (bf16[256,1536]{1,0:T(8,128)(2,1)S(1)}, bf16[256,1536]{1,0:T(8,128)(2,1)}, u32[]{:S(2)}) copy-start(bf16[256,1536]{1,0:T(8,128)(2,1)} %get-tuple-element.23) | copy-start | bytes 2359300
  (23 other events, 110.5 us)

commit v4 on v3

--- a/solution.py
+++ b/solution.py
@@ -18,14 +18,14 @@
 BF = jnp.bfloat16
 F32 = jnp.float32
 PAIR = [(0, 1), (1, 0)]
-VMEM_LIMIT = 48 * 1024 * 1024
-
-
-def token_offsets(starts, row_count):
+
+
+def token_offsets(lengths, row_count):
     positions = jnp.arange(row_count, dtype=jnp.int32)
-    offset = positions
-    for i in range(1, starts.shape[0]):
-        offset = jnp.where(positions >= starts[i], positions - starts[i], offset)
+    offset, start = positions, 0
+    for i in range(1, lengths.shape[0]):
+        start = start + lengths[i - 1]
+        offset = jnp.where(positions >= start, positions - start, offset)
     return offset
 
 
@@ -53,8 +53,8 @@
     return [pl.BlockSpec(memory_space=pltpu.VMEM)] * count
 
 
-def params():
-    return pltpu.CompilerParams(vmem_limit_bytes=VMEM_LIMIT)
+def params(mebibytes):
+    return pltpu.CompilerParams(vmem_limit_bytes=mebibytes * 1024 * 1024)
 
 
 def spread_columns(heads):
@@ -64,20 +64,21 @@
     return (target[:, None] == jnp.arange(heads * LANES, dtype=jnp.int32)[None, :]).astype(BF)
 
 
-def tenant_at(start_ref, tenant_ref, positions):
-    tenant = jnp.full(positions.shape, tenant_ref[0], jnp.int32)
+def tenant_at(length_ref, tenant_ref, positions):
+    tenant, start = jnp.full(positions.shape, tenant_ref[0], jnp.int32), 0
     for i in range(1, tenant_ref.shape[0]):
-        tenant = jnp.where(positions >= start_ref[i], tenant_ref[i], tenant)
+        start = start + length_ref[i - 1]
+        tenant = jnp.where(positions >= start, tenant_ref[i], tenant)
     return tenant
 
 
-def bias_of(start_ref, tenant_ref, first, count, seen):
+def bias_of(length_ref, tenant_ref, first, count, seen):
     row = lax.broadcasted_iota(jnp.int32, (count, seen), 0) + first
     col = lax.broadcasted_iota(jnp.int32, (count, seen), 1)
     query_tenant = tenant_at(
-        start_ref, tenant_ref, lax.broadcasted_iota(jnp.int32, (count, 1), 0) + first
+        length_ref, tenant_ref, lax.broadcasted_iota(jnp.int32, (count, 1), 0) + first
     )
-    key_tenant = tenant_at(start_ref, tenant_ref, lax.broadcasted_iota(jnp.int32, (1, seen), 1))
+    key_tenant = tenant_at(length_ref, tenant_ref, lax.broadcasted_iota(jnp.int32, (1, seen), 1))
     return jnp.where((col <= row) & (query_tenant == key_tenant), 0.0, -1e30)
 
 
@@ -106,79 +107,82 @@
     kv_heads,
     blocks,
     spots_ref,
-    start_ref,
+    length_ref,
     tenant_ref,
-    emb_ref,
+    half_ref,
+    own_ref,
+    other_ref,
     gain_ref,
     cos_ref,
-    sin_ref,
+    low_ref,
+    high_ref,
     spread_ref,
     pack_ref,
     *refs,
 ):
     sources, refs = block_list(refs[:blocks]), refs[blocks:]
-    att_ref, cache_ref, late_ref, keys, values, raw, weight_ref, normed, mixed, bias, sems = refs
-    tokens = emb_ref.shape[0]
-    step = tokens // 2
+    att_ref, cache_ref, late_ref, keys, values, raw, normed, mixed, bias, sems = refs
+    step = own_ref.shape[0]
     group = q_heads // kv_heads
     _, count, rows, cols = raw.shape
     copies = block_copies(spots_ref, sources, raw, sems, pl.ds(0, cols))
     for copy in copies:
         copy.start()
-    for r in range(0, tokens, step):
-        x = emb_ref[r : r + step, :].astype(F32)
+    for half, ref in ((half_ref[0], own_ref), (1 - half_ref[0], other_ref)):
+        x = ref[...].astype(F32)
         scale = lax.rsqrt(jnp.mean(x * x, axis=-1, keepdims=True) + norm_eps)
-        normed[r : r + step, :] = (x * scale * gain_ref[...]).astype(BF)
-    bias[...] = bias_of(start_ref, tenant_ref, 0, step, step)
+        place = pl.ds(pl.multiple_of(half * step, step), step)
+        normed[place, :] = (x * scale * gain_ref[...]).astype(BF)
+    bias[...] = bias_of(length_ref, tenant_ref, 0, step, step)
     for copy in copies:
         copy.wait()
     narrow, wide = spread_ref.shape
-    target = 0
-    for part in range(2):
-        for b in range(cols // narrow):
-            piece = raw[part, :, :, b * narrow : (b + 1) * narrow].reshape(count * rows, narrow)
-            weight_ref[:, target : target + wide] = jnp.dot(
-                piece, spread_ref[...], preferred_element_type=F32
-            ).astype(BF)
-            target += wide
 
     def turned(x):
-        return (x * cos_ref[...] + pltpu.roll(x, 64, 1) * sin_ref[...]).astype(BF)
-
-    def project(first, heads):
+        return (
+            x * cos_ref[...]
+            + pltpu.roll(x, narrow - HALF, 1) * low_ref[...]
+            + pltpu.roll(x, HALF, 1) * high_ref[...]
+        ).astype(BF)
+
+    def spread(x):
+        return jnp.dot(x, spread_ref[...], preferred_element_type=F32).astype(BF)
+
+    def project(part):
         return jnp.dot(
-            normed[...],
-            weight_ref[:, first * LANES : (first + heads) * LANES],
-            preferred_element_type=F32,
-        )
-
-    k_all = project(q_heads, kv_heads)
-    for h in range(kv_heads):
-        keys[:, h * LANES : (h + 1) * LANES] = turned(k_all[:, h * LANES : (h + 1) * LANES])
-    values[...] = project(q_heads + kv_heads, kv_heads).astype(BF)
-    for kv in range(kv_heads):
-        lanes = slice(kv * LANES, (kv + 1) * LANES)
-        q_all = project(kv * group, group)
-        for g in range(group):
-            h = kv * group + g
-            head = slice(h * LANES, (h + 1) * LANES)
-            q = turned(q_all[:, g * LANES : (g + 1) * LANES])
-            late_ref[:, head] = q[step:, :]
-            mixed[:, head] = attend_head(
-                q[:step, :], keys[:step, lanes], values[:step, lanes], bias[...]
+            normed[...], raw[part].reshape(count * rows, cols), preferred_element_type=F32
+        )
+
+    key_value = project(1)
+    key_heads = turned(key_value[:, :narrow])
+    value_heads = key_value[:, narrow:].astype(BF)
+    cache_ref[0] = key_heads
+    cache_ref[1] = value_heads
+    keys[...] = spread(key_heads)
+    values[...] = spread(value_heads)
+    query = project(0)
+    for b in range(cols // narrow):
+        q_wide = spread(turned(query[:, b * narrow : (b + 1) * narrow]))
+        late_ref[:, b * wide : (b + 1) * wide] = q_wide[step:, :]
+        for g in range(wide // LANES):
+            h = b * (wide // LANES) + g
+            lanes = slice(h // group * LANES, (h // group + 1) * LANES)
+            mixed[:, h * LANES : (h + 1) * LANES] = attend_head(
+                q_wide[:step, g * LANES : (g + 1) * LANES],
+                keys[:step, lanes],
+                values[:step, lanes],
+                bias[...],
             )
     att_ref[...] = packed(mixed[...], pack_ref)
-    cache_ref[0] = packed(keys[...], pack_ref)
-    cache_ref[1] = packed(values[...], pack_ref)
 
 
 def late_kernel(
-    q_heads, kv_heads, start_ref, tenant_ref, q_ref, keys, values, pack_ref, att_ref, mixed, bias
+    q_heads, kv_heads, length_ref, tenant_ref, q_ref, keys, values, pack_ref, att_ref, mixed, bias
 ):
     step = q_ref.shape[0]
     seen = keys.shape[0]
     group = q_heads // kv_heads
-    bias[...] = bias_of(start_ref, tenant_ref, seen - step, step, seen)
+    bias[...] = bias_of(length_ref, tenant_ref, seen - step, step, seen)
     for h in range(q_heads):
         head = slice(h * LANES, (h + 1) * LANES)
         lanes = slice(h // group * LANES, (h // group + 1) * LANES)
@@ -203,13 +207,12 @@
 
 
 def attention_early(
-    spots, starts, tenants, embedded, gain, cosine, sine, spread, blocks, cols, q_heads, kv_heads
+    spots, lengths, tenants, half, own, other, gain, tables, spread, blocks, cols, q_heads, kv_heads
 ):
-    tokens, width = embedded.shape
+    step, width = own.shape
+    tokens = 2 * step
     rows = blocks[0].shape[0]
     total = spots.shape[1]
-    wide = 2 * cols // spread.shape[0] * spread.shape[1]
-    step = tokens // 2
     return pl.pallas_call(
         functools.partial(project_kernel, q_heads, kv_heads, len(blocks)),
         out_shape=(
@@ -219,29 +222,28 @@
             jax.ShapeDtypeStruct((tokens, kv_heads * LANES), BF),
             jax.ShapeDtypeStruct((tokens, kv_heads * LANES), BF),
         ),
-        in_specs=[pl.BlockSpec(memory_space=pltpu.SMEM)] * 3
-        + in_vmem(6)
+        in_specs=[pl.BlockSpec(memory_space=pltpu.SMEM)] * 4
+        + in_vmem(8)
         + [pl.BlockSpec(memory_space=pl.ANY)] * len(blocks),
         out_specs=tuple(in_vmem(5)),
         scratch_shapes=[
             pltpu.VMEM((2, total // 2, rows, cols), BF),
-            pltpu.VMEM((width, wide), BF),
             pltpu.VMEM((tokens, width), BF),
             pltpu.VMEM((step, q_heads * LANES), BF),
             pltpu.VMEM((step, step), F32),
             pltpu.SemaphoreType.DMA((total,)),
         ],
-        compiler_params=params(),
+        compiler_params=params(48),
         name="attention_early",
         cost_estimate=pl.CostEstimate(
-            flops=2 * tokens * width * wide + 2 * width * wide * spread.shape[0],
-            bytes_accessed=4 * width * wide + 6 * embedded.size,
+            flops=4 * tokens * width * cols,
+            bytes_accessed=4 * width * cols + 12 * own.size,
             transcendentals=q_heads * step * step,
         ),
-    )(spots, starts, tenants, embedded, gain, cosine, sine, spread, spread.T, *blocks)
-
-
-def attention_late(starts, tenants, queries, keys, values, pack, q_heads, kv_heads):
+    )(spots, lengths, tenants, half, own, other, gain, *tables, spread, spread.T, *blocks)
+
+
+def attention_late(lengths, tenants, queries, keys, values, pack, q_heads, kv_heads):
     step, tokens = queries.shape[0], keys.shape[0]
     return pl.pallas_call(
         functools.partial(late_kernel, q_heads, kv_heads),
@@ -252,22 +254,23 @@
             pltpu.VMEM((step, q_heads * LANES), BF),
             pltpu.VMEM((step, tokens), F32),
         ],
-        compiler_params=params(),
+        compiler_params=params(48),
         name="attention_late",
         cost_estimate=pl.CostEstimate(
             flops=4 * q_heads * step * tokens * LANES,
             bytes_accessed=8 * keys.size,
             transcendentals=q_heads * step * tokens,
         ),
-    )(starts, tenants, queries, keys, values, pack)
+    )(lengths, tenants, queries, keys, values, pack)
 
 
 def ffn_kernel(
     blocks,
     first_col,
     spots_ref,
-    core_ref,
-    emb_ref,
+    side_ref,
+    emb_own_ref,
+    emb_other_ref,
     own_ref,
     other_ref,
     w_own_ref,
@@ -299,11 +302,12 @@
     for copy in pending:
         copy.start()
     depth = w_first_ref.shape[0]
-    core = core_ref[0]
+    core = side_ref[0]
     first = pl.ds(pl.multiple_of(core * depth, LANES), depth)
     second = pl.ds(pl.multiple_of((1 - core) * depth, LANES), depth)
+    embedded = jnp.where(side_ref[1] == 1, emb_own_ref[...], emb_other_ref[...])
     x = (
-        emb_ref[...].astype(F32)
+        embedded.astype(F32)
         + jnp.dot(own_ref[...], w_own_ref[...], preferred_element_type=F32)
         + jnp.dot(other_ref[:, first], w_first_ref[...], preferred_element_type=F32)
         + jnp.dot(other_ref[:, second], w_second_ref[...], preferred_element_type=F32)
@@ -332,9 +336,9 @@
 
 
 def ffn_part(
-    spots, core, embedded, own, other, w_own, w_first, w_second, gain, down, blocks, first_col
+    spots, side, embedded, own, other, w_own, w_first, w_second, gain, down, blocks, first_col
 ):
-    tokens, width = embedded.shape
+    tokens, width = embedded[0].shape
     rows = blocks[0].shape[0]
     total = spots.shape[1]
     ff_half = down.shape[0]
@@ -346,7 +350,7 @@
             jax.ShapeDtypeStruct((tokens, width), BF),
         ),
         in_specs=[pl.BlockSpec(memory_space=pltpu.SMEM)] * 2
-        + in_vmem(7)
+        + in_vmem(8)
         + [pl.BlockSpec(memory_space=pl.ANY)] * (1 + len(blocks)),
         out_specs=tuple(in_vmem(2)),
         scratch_shapes=[
@@ -357,14 +361,14 @@
             pltpu.SemaphoreType.DMA((2, total)),
             pltpu.SemaphoreType.DMA((2,)),
         ],
-        compiler_params=params(),
+        compiler_params=params(48),
         name="ffn_part",
         cost_estimate=pl.CostEstimate(
             flops=2 * tokens * width * (3 * ff_half + 2 * w_own.shape[0]),
             bytes_accessed=6 * width * ff_half + 4 * w_own.size,
             transcendentals=tokens * ff_half,
         ),
-    )(spots, core, embedded, own, other, w_own, w_first, w_second, gain, down, *blocks)
+    )(spots, side, *embedded, own, other, w_own, w_first, w_second, gain, down, *blocks)
 
 
 def per_device(
@@ -408,18 +412,28 @@
     slots = jnp.arange(group_count * capacity, dtype=jnp.int32)
     chosen = place[None, :] == slots[:, None]
     requests = jnp.sum(jnp.where(chosen, row_in_range[None, :] + 1, 0), axis=1) - 1
-    lengths = prompt_lengths[0]
-    starts = jnp.stack([jnp.sum(lengths[:i]) for i in range(lengths.shape[0])]).astype(jnp.int32)
-    offset = token_offsets(starts, tokens)
-    lane = jnp.arange(LANES, dtype=jnp.int32)
-    frequency = rope_base ** (-2.0 * (lane % 64).astype(F32) / HEAD_DIM)
-    angles = offset.astype(F32)[:, None] * frequency[None, :]
-    cosine = jnp.cos(angles)
-    sine = jnp.where(lane < 64, -1.0, 1.0)[None, :] * jnp.sin(angles)
-
     asked = lax.all_to_all(
         requests.reshape(group_count, capacity), "req", split_axis=0, concat_axis=0, tiled=True
     ).reshape(-1)
+
+    pick_rows = (asked[:, None] == jnp.arange(own_rows, dtype=jnp.int32)[None, :]).astype(BF)
+    found_rows = jnp.dot(pick_rows, embed_table, preferred_element_type=F32).astype(BF)
+    returned = lax.all_to_all(
+        found_rows.reshape(group_count, capacity, width),
+        "req",
+        split_axis=0,
+        concat_axis=0,
+        tiled=True,
+    ).reshape(group_count * capacity, width)
+    lengths = prompt_lengths[0]
+    kv_local = kv_half // HEAD_DIM
+    lane = jnp.arange(kv_half, dtype=jnp.int32) % HEAD_DIM
+    frequency = rope_base ** (-2.0 * (lane % HALF).astype(F32) / HEAD_DIM)
+    offset = token_offsets(after(lengths, found_rows), tokens)
+    angles = offset.astype(F32)[:, None] * frequency[None, :]
+    sine = jnp.sin(angles)
+    low = lane < HALF
+    tables = (jnp.cos(angles), jnp.where(low, -sine, 0.0), jnp.where(low, 0.0, sine))
 
     q_parts = ((0, q_half),)
     kv_parts = ((q_full, kv_half), (q_full + kv_full, kv_half))
@@ -434,7 +448,7 @@
                 gate_up_weight, part * ff_full + half * ff_half, ff_half, axis=1
             )
         )
-        return jnp.concatenate([piece.astype(BF) for piece in pieces], axis=1)
+        return after(jnp.concatenate([piece.astype(BF) for piece in pieces], axis=1), *tables)
 
     def chip_block(parts):
         kept = jnp.where(core == 0, parts[0], parts[1])
@@ -468,72 +482,61 @@
         ]
     ).astype(jnp.int32)
 
-    asked = after(asked, cosine, sine)
-    pick_rows = (asked[:, None] == jnp.arange(own_rows, dtype=jnp.int32)[None, :]).astype(BF)
-    found_rows = jnp.dot(pick_rows, embed_table, preferred_element_type=F32).astype(BF)
-    returned = lax.all_to_all(
-        found_rows.reshape(group_count, capacity, width),
-        "req",
-        split_axis=0,
-        concat_axis=0,
-        tiled=True,
-    ).reshape(group_count * capacity, width)
     pick_mine = (place[:, None] == slots[None, :]).astype(BF)
     embedded_own = jnp.dot(pick_mine, returned, preferred_element_type=F32).astype(BF)
     embedded_other = lax.ppermute(embedded_own, "tp", PAIR)
-    embedded = [
-        jnp.where(tp_index == 0, embedded_own, embedded_other),
-        jnp.where(tp_index == 0, embedded_other, embedded_own),
-    ]
 
     out_rows = q_half // 2
     out_first = lax.ppermute(
-        lax.dynamic_slice_in_dim(out_weight, core * out_rows, out_rows), "tp", PAIR
+        after(lax.dynamic_slice_in_dim(out_weight, core * out_rows, out_rows), came), "tp", PAIR
     )
     out_second = lax.ppermute(out_first, "req", core_swap)
 
     def swapped(blocks):
-        return lax.ppermute(jnp.stack(blocks), "req", core_swap)
+        sent = blocks[0] if len(blocks) == 1 else jnp.stack(blocks)
+        return lax.ppermute(sent, "req", core_swap)
 
     cut = (chips + 2) // 2
     for i in range(chips - 1):
-        ready = {2: (embedded_own,), 4: (embedded_other, out_second)}.get(i, ())
-        own_ring = ring_more(own_ring, 1, ring_pairs, *ready)
-        other_ring = ring_more(other_ring, 1, ring_pairs, *ready)
+        ready = {2: (embedded_own,), chips - 3: (embedded_other, out_second)}.get(i, ())
+        own_ring = ring_more(own_ring, 1, ring_pairs, other_ring[max(i - 1, 0)], *ready)
+        other_ring = ring_more(other_ring, 1, ring_pairs, own_ring[i])
     blocks = [
         *own_ring,
         *other_ring,
         swapped(own_ring[:cut]),
-        swapped(own_ring[cut:]),
+        swapped(own_ring[cut:-1]),
+        swapped(own_ring[-1:]),
         swapped(other_ring[:cut]),
-        swapped(other_ring[cut:]),
+        swapped(other_ring[cut:-1]),
+        swapped(other_ring[-1:]),
     ]
 
-    kv_local = kv_half // HEAD_DIM
     spread = spread_columns(kv_local)
     pack = spread.T
     q_local = q_half // HEAD_DIM
     early, kv_cache, queries, keys, values = attention_early(
         spots,
-        starts,
+        lengths,
         tenant_ids[0],
-        jnp.concatenate(embedded, axis=0),
+        tp_index[None],
+        embedded_own,
+        embedded_other,
         attention_gain[None, :],
-        cosine,
-        sine,
+        tables,
         spread,
         blocks,
         q_half,
         q_local,
         kv_local,
     )
-    late = attention_late(starts, tenant_ids[0], queries, keys, values, pack, q_local, kv_local)
+    late = attention_late(lengths, tenant_ids[0], queries, keys, values, pack, q_local, kv_local)
     finals = []
-    for start, attended in zip(embedded, (early, late)):
+    for half, attended in enumerate((early, late)):
         residual, part = ffn_part(
             spots,
-            core[None],
-            start,
+            jnp.stack([core, (tp_index == half).astype(jnp.int32)]),
+            (embedded_own, embedded_other),
             attended,
             lax.ppermute(attended, "tp", PAIR),
             out_weight,

time: 249 us -> 241 us (0.968)
  starting transfers between devices: 70.3 us -> 52.2 us
  waiting for transfers between devices: 83.6 us -> 97.5 us
  Pallas kernels: 51.1 us -> 46.8 us
    ppermute x14, starting transfers between devices: 45.5 us -> 30.6 us  [ring_more(): blocks.append(lax.ppermute(last, 'req', pairs))]
    ppermute x5 -> x7, waiting for transfers between devices: 0.04 us -> 7.92 us  [the longest x1 5.77 us: per_device(): lax.ppermute(after(lax.dynamic_slice_in_dim(out_weight, core * out_rows,...]
    pallas_call x1, Pallas kernels: 17.1 us -> 11.5 us  [attention_early(): pl.pallas_call(functools.partial(project_kernel, q_heads, kv_heads, len(b...]
    ppermute x14, waiting for transfers between devices: 39.3 us -> 44.4 us  [ring_more(): blocks.append(lax.ppermute(last, 'req', pairs))]
    select_n x2 -> x1, other arithmetic: 0.12 us -> 4.01 us  [per_device(): jnp.where(low, 0.0, sine)]
    ppermute x1, waiting for transfers between devices: 16.5 us -> 12.9 us  [per_device(): came = lax.ppermute(away, 'tp', PAIR)]
    all_to_all x1, waiting for transfers between devices: 0.01 us -> 3.56 us  [per_device(): lax.all_to_all(requests.reshape(group_count, capacity), 'req', split_axis...]
    convert_element_type x3, local copies, waits for them, and re-layouts: 3.5 us -> 0.17 us  [columns(): piece.astype(BF)]
  transfers between devices with their start and end apart: 30 -> 32, of which waited for: 17 -> 21; matrix products, arithmetic and copies ran while one was open for 14% -> 11% of each run, Pallas kernels for 12% -> 13%
where the time goes in v4:
time: 241 us
  waiting for transfers between devices  97.5 us (40%)
  starting transfers between devices  52.2 us (22%)
  Pallas kernels  46.8 us (19%)
  local copies, waits for them, and re-layouts  16.2 us (7%)
  other arithmetic  15.6 us (6%)
  matrix products  9.39 us (4%)
  between operations  2.86 us (1%)
    ppermute x14, waiting for transfers between devices, ring_more(): blocks.append(lax.ppermute(last, 'req', pairs))  44.4 us
    pallas_call x2, Pallas kernels, ffn_part(): pl.pallas_call(functools.partial(ffn_kernel, len(blocks), first_col), out...  31 us
    ppermute x14, starting transfers between devices, ring_more(): blocks.append(lax.ppermute(last, 'req', pairs))  30.6 us
    ppermute x2, waiting for transfers between devices, per_device(): total = part.astype(F32) + lax.ppermute(part, 'tp', PAIR).astype(F32)  17.1 us
    ppermute x1, waiting for transfers between devices, per_device(): came = lax.ppermute(away, 'tp', PAIR)  12.9 us
    pallas_call x1, Pallas kernels, attention_early(): pl.pallas_call(functools.partial(project_kernel, q_heads, kv_heads, len(b...  11.5 us
    ppermute x2, waiting for transfers between devices, per_device(): lax.ppermute(attended, 'tp', PAIR)  10.2 us
    unnamed x60, local copies, waits for them, and re-layouts  9.85 us
  transfers between devices with their start and end apart: 32, of which 21 were waited for; matrix products, arithmetic and copies ran while one was open for 11% of the time, Pallas kernels for 13%

profile of v4, /device:TPU:0, one launch (start us, length us, event | category | flops | bytes accessed | tf_op | source)
XLA Modules:
  0.0 240.6 jit_solution(14639656335825045880)
XLA Ops:
  2.6 7.4 %all-to-all-start = ((s32[16,1,32]{2,1,0:T(1,128)}), s32[16,1,32]{2,1,0:T(1,128)S(1)}, u32[]{:S(2)}, u32[]{:S(2)}) async-start(s32[16,1,32]{2,1,0:T(1,128)} %sub.101), calls=%async_computation | async-start | bytes 16384 | tf_op jit(solution)/shard_map/all_to_all | solution.py:415
  10.0 2.4 constant_dynamic-slice_fusion
  12.8 3.6 %all-to-all-done = s32[16,1,32]{2,1,0:T(1,128)S(1)} async-done(((s32[16,1,32]{2,1,0:T(1,128)}), s32[16,1,32]{2,1,0:T(1,128)S(1)}, u32[]{:S(2)}, u32[]{:S(2)}) %all-to-all-start) | async-done | bytes 2080 | tf_op jit(solution)/shard_map/all_to_all | solution.py:415
  17.6 7.4 %fusion.1 = bf16[512,1536]{1,0:T(8,128)(2,1)} fusion(bf16[2000,1536]{1,0:T(8,128)(2,1)} %param.13, s32[512]{0:T(512)S(1)} %eq.123), kind=kOutput, calls=%fused_computation.2 | convolution fusion | flops 3147538432 | bytes 7718912 | tf_op jit(solution)/shard_map/dot_general | solution.py:420
  25.0 4.5 %all-to-all-start.1 = ((bf16[16,32,1536]{2,1,0:T(8,128)(2,1)}), bf16[16,32,1536]{2,1,0:T(8,128)(2,1)}, u32[]{:S(2)}, u32[]{:S(2)}) async-start(bf16[16,32,1536]{2,1,0:T(8,128)(2,1)} %bitcast.4), calls=%async_computation.1 | async-start | bytes 3145728 | tf_op jit(solution)/shard_map/all_to_all | solution.py:421
  32.5 4.0 %fusion.3 = (f32[512,384]{1,0:T(8,128)}, f32[512,384]{1,0:T(8,128)}, f32[512,384]{1,0:T(8,128)}) fusion(f32[384]{0:T(512)S(1)} %fusion.14, f32[512]{0:T(512)S(1)} %select_convert_fusion, pred[384]{0:T(512)(128)(4,1)S(1)} %fusion.18), kind=kLoop, calls=%fused_computation.10 | loop fusion | flops 786432 | bytes 2363264 | tf_op jit(solution)/shard_map/jit(_where)/select_n | solution.py:436
  36.9 1.6 collective-permute-start.2
  38.5 12.9 %collective-permute-done.2 = bf16[2,48,2816]{2,1,0:T(8,128)(2,1)S(1)} collective-permute-done((bf16[2,48,2816]{2,1,0:T(8,128)(2,1)S(1)}, bf16[2,48,2816]{2,1,0:T(8,128)(2,1)S(1)}, u32[]{:S(2)}, u32[]{:S(2)}) %collective-permute-start.2) | collective-permute-done | bytes 540704 | tf_op jit(solution)/shard_map/ppermute | solution.py:462
  51.6 1.5 collective-permute-done.3
  53.2 1.8 collective-permute-start.4
  55.0 1.5 collective-permute-start.6
  57.3 1.5 collective-permute-start.13
  59.7 7.1 %collective-permute-done.4.refs_1_ = bf16[96,2816]{1,0:T(8,128)(2,1)S(1)} collective-permute-done((bf16[96,2816]{1,0:T(8,128)(2,1)S(1)}, bf16[96,2816]{1,0:T(8,128)(2,1)S(1)}, u32[]{:S(2)}, u32[]{:S(2)}) %collective-permute-start.4) | collective-permute-done | bytes 540704 | tf_op jit(solution)/shard_map/ppermute | solution.py:48
  66.8 4.8 %collective-permute-start.5 = (bf16[96,2816]{1,0:T(8,128)(2,1)S(1)}, bf16[96,2816]{1,0:T(8,128)(2,1)S(1)}, u32[]{:S(2)}, u32[]{:S(2)}) collective-permute-start(bf16[96,2816]{1,0:T(8,128)(2,1)S(1)} %collective-permute-done.4.refs_1_), channel_id=1, source_target_pairs={{0,4},{4,8},{8,12},{12,14},{14,10},{10,6},{6,2},{2,0},{5,1},{9,5},... | collective-permute-start | bytes 1622024 | tf_op jit(solution)/shard_map/ppermute | solution.py:48
  72.6 4.8 %collective-permute-start.8 = (bf16[96,2816]{1,0:T(8,128)(2,1)S(1)}, bf16[96,2816]{1,0:T(8,128)(2,1)S(1)}, u32[]{:S(2)}, u32[]{:S(2)}) collective-permute-start(bf16[96,2816]{1,0:T(8,128)(2,1)S(1)} %collective-permute-done.6.refs_9_), channel_id=1, source_target_pairs={{0,4},{4,8},{8,12},{12,14},{14,10},{10,6},{6,2},{2,0},{5,1},{9,5},... | collective-permute-start | bytes 1622024 | tf_op jit(solution)/shard_map/ppermute | solution.py:48
  79.1 5.8 %collective-permute-done.13.w_first_ref = bf16[384,1536]{1,0:T(8,128)(2,1)} collective-permute-done((bf16[384,1536]{1,0:T(8,128)(2,1)S(1)}, bf16[384,1536]{1,0:T(8,128)(2,1)}, u32[]{:S(2)}, u32[]{:S(2)}) %collective-permute-start.13) | collective-permute-done | bytes 1179680 | tf_op jit(solution)/shard_map/ppermute | solution.py:490
  84.9 4.1 %collective-permute-start.10 = (bf16[96,2816]{1,0:T(8,128)(2,1)S(1)}, bf16[96,2816]{1,0:T(8,128)(2,1)}, u32[]{:S(2)}, u32[]{:S(2)}) collective-permute-start(bf16[96,2816]{1,0:T(8,128)(2,1)S(1)} %collective-permute-done.8.refs_10_), channel_id=1, source_target_pairs={{0,4},{4,8},{8,12},{12,14},{14,10},{10,6},{6,2},{2,0},{5,1},{9,5},... | collective-permute-start | bytes 1622024 | tf_op jit(solution)/shard_map/ppermute | solution.py:48
  90.7 2.0 convolution_convert_fusion.own_ref.emb_own_ref
  92.8 2.5 %collective-permute-start.7 = (bf16[96,2816]{1,0:T(8,128)(2,1)S(1)}, bf16[96,2816]{1,0:T(8,128)(2,1)S(1)}, u32[]{:S(2)}, u32[]{:S(2)}) collective-permute-start(bf16[96,2816]{1,0:T(8,128)(2,1)S(1)} %collective-permute-done.5.refs_2_), channel_id=1, source_target_pairs={{0,4},{4,8},{8,12},{12,14},{14,10},{10,6},{6,2},{2,0},{5,1},{9,5},... | collective-permute-start | bytes 1622024 | tf_op jit(solution)/shard_map/ppermute | solution.py:48
  95.9 1.9 bitcast_dynamic-update-slice_fusion.1
  97.8 1.5 collective-permute-start
  99.3 2.9 %collective-permute-done.7.refs_3_ = bf16[96,2816]{1,0:T(8,128)(2,1)S(1)} collective-permute-done((bf16[96,2816]{1,0:T(8,128)(2,1)S(1)}, bf16[96,2816]{1,0:T(8,128)(2,1)S(1)}, u32[]{:S(2)}, u32[]{:S(2)}) %collective-permute-start.7) | collective-permute-done | bytes 540704 | tf_op jit(solution)/shard_map/ppermute | solution.py:48
  102.2 2.5 %collective-permute-start.9 = (bf16[96,2816]{1,0:T(8,128)(2,1)S(1)}, bf16[96,2816]{1,0:T(8,128)(2,1)S(1)}, u32[]{:S(2)}, u32[]{:S(2)}) collective-permute-start(bf16[96,2816]{1,0:T(8,128)(2,1)S(1)} %collective-permute-done.7.refs_3_), channel_id=1, source_target_pairs={{0,4},{4,8},{8,12},{12,14},{14,10},{10,6},{6,2},{2,0},{5,1},{9,5},... | collective-permute-start | bytes 1622024 | tf_op jit(solution)/shard_map/ppermute | solution.py:48
  104.7 2.0 collective-permute-start.12
  107.5 5.4 %collective-permute-done.9.refs_4_ = bf16[96,2816]{1,0:T(8,128)(2,1)S(1)} collective-permute-done((bf16[96,2816]{1,0:T(8,128)(2,1)S(1)}, bf16[96,2816]{1,0:T(8,128)(2,1)S(1)}, u32[]{:S(2)}, u32[]{:S(2)}) %collective-permute-start.9) | collective-permute-done | bytes 540704 | tf_op jit(solution)/shard_map/ppermute | solution.py:48
  113.0 1.1 collective-permute-start.11
  114.9 3.8 %collective-permute-done.12.refs_12_ = bf16[96,2816]{1,0:T(8,128)(2,1)S(1)} collective-permute-done((bf16[96,2816]{1,0:T(8,128)(2,1)}, bf16[96,2816]{1,0:T(8,128)(2,1)S(1)}, u32[]{:S(2)}, u32[]{:S(2)}) %collective-permute-start.12) | collective-permute-done | bytes 540704 | tf_op jit(solution)/shard_map/ppermute | solution.py:48
  119.6 1.1 collective-permute-start.16
  120.7 3.8 %collective-permute-done.11.refs_5_ = bf16[96,2816]{1,0:T(8,128)(2,1)S(1)} collective-permute-done((bf16[96,2816]{1,0:T(8,128)(2,1)S(1)}, bf16[96,2816]{1,0:T(8,128)(2,1)S(1)}, u32[]{:S(2)}, u32[]{:S(2)}) %collective-permute-start.11) | collective-permute-done | bytes 540704 | tf_op jit(solution)/shard_map/ppermute | solution.py:48
  125.6 4.8 %collective-permute-done.16.refs_13_ = bf16[96,2816]{1,0:T(8,128)(2,1)} collective-permute-done((bf16[96,2816]{1,0:T(8,128)(2,1)S(1)}, bf16[96,2816]{1,0:T(8,128)(2,1)}, u32[]{:S(2)}, u32[]{:S(2)}) %collective-permute-start.16) | collective-permute-done | bytes 540704 | tf_op jit(solution)/shard_map/ppermute | solution.py:48
  131.5 4.7 %collective-permute-done.15.refs_6_ = bf16[96,2816]{1,0:T(8,128)(2,1)} collective-permute-done((bf16[96,2816]{1,0:T(8,128)(2,1)S(1)}, bf16[96,2816]{1,0:T(8,128)(2,1)}, u32[]{:S(2)}, u32[]{:S(2)}) %collective-permute-start.15) | collective-permute-done | bytes 540704 | tf_op jit(solution)/shard_map/ppermute | solution.py:48
  136.2 1.1 collective-permute-start.17
  137.3 2.2 pad_maximum_fusion.1
  139.5 2.5 %collective-permute-done.18.refs_14_ = bf16[96,2816]{1,0:T(8,128)(2,1)} collective-permute-done((bf16[96,2816]{1,0:T(8,128)(2,1)}, bf16[96,2816]{1,0:T(8,128)(2,1)}, u32[]{:S(2)}, u32[]{:S(2)}) %collective-permute-start.18) | collective-permute-done | bytes 540704 | tf_op jit(solution)/shard_map/ppermute | solution.py:48
  142.0 1.1 collective-permute-start.19
  143.1 2.3 pad_maximum_fusion.2
  145.4 2.4 %collective-permute-done.17.refs_7_ = bf16[96,2816]{1,0:T(8,128)(2,1)} collective-permute-done((bf16[96,2816]{1,0:T(8,128)(2,1)}, bf16[96,2816]{1,0:T(8,128)(2,1)}, u32[]{:S(2)}, u32[]{:S(2)}) %collective-permute-start.17) | collective-permute-done | bytes 540704 | tf_op jit(solution)/shard_map/ppermute | solution.py:48
  148.2 5.4 %collective-permute-done.19.refs_15_ = bf16[96,2816]{1,0:T(8,128)(2,1)} collective-permute-done((bf16[96,2816]{1,0:T(8,128)(2,1)}, bf16[96,2816]{1,0:T(8,128)(2,1)}, u32[]{:S(2)}, u32[]{:S(2)}) %collective-permute-start.19) | collective-permute-done | bytes 540704 | tf_op jit(solution)/shard_map/ppermute | solution.py:48
  154.4 1.4 collective-permute-done.22.refs_18_
  157.4 11.5 %attention_early.1 = (bf16[256,768]{1,0:T(8,128)(2,1)S(1)}, bf16[2,512,384]{2,1,0:T(8,128)(2,1)}, bf16[256,1024]{1,0:T(8,128)(2,1)S(1)}, bf16[512,512]{1,0:T(8,128)(2,1)S(1)}, bf16[512,512]{1,0:T(8,128)(2,1)S(1)}) custom-call(s32[2,32]{1,0:T(2,128)S(1)} %pad_add_fusion.spots_ref, s32[4]{0:T(128)S(1)} %bitcast.49, s32[4]{0:T(128)S(1)} %bitcast.51, ...), custom_call_target="tpu_custom_call" | custom-call | flops 2415919104 | bytes 9437184 | tf_op jit(solution)/shard_map/attention_early/pallas_call | solution.py:216
  169.6 4.2 %attention_late.1.own_ref = bf16[256,768]{1,0:T(8,128)(2,1)} custom-call(s32[4]{0:T(128)S(1)} %bitcast.50, s32[4]{0:T(128)S(1)} %bitcast.52, bf16[256,1024]{1,0:T(8,128)(2,1)S(1)} %get-tuple-element.54.q_ref, bf16[512,512]{1,0:T(8,128)(2,1)S(1)} %get-tuple-element.55.keys, bf16[512,512]{1,0:T(8,128)(2,1)S(1)} %get-tuple-element.56.values, ...), custom_call_target="tpu_custom_call" | custom-call | flops 536870912 | bytes 2097152 | tf_op jit(solution)/shard_map/attention_late/pallas_call | solution.py:248
  173.9 1.5 collective-permute-start.28
  176.0 10.2 %collective-permute-done.28.other_ref = bf16[256,768]{1,0:T(8,128)(2,1)} collective-permute-done((bf16[256,768]{1,0:T(8,128)(2,1)}, bf16[256,768]{1,0:T(8,128)(2,1)}, u32[]{:S(2)}, u32[]{:S(2)}) %collective-permute-start.28) | collective-permute-done | bytes 393248 | tf_op jit(solution)/shard_map/ppermute | solution.py:541
  188.2 15.6 %ffn_part.3 = (f32[256,1536]{1,0:T(8,128)}, bf16[256,1536]{1,0:T(8,128)(2,1)}) custom-call(s32[2,32]{1,0:T(2,128)S(1)} %pad_add_fusion.spots_ref, s32[2]{0:T(128)S(1)} %pad_add_fusion.3.side_ref, bf16[256,1536]{1,0:T(8,128)(2,1)} %copy-done.12, bf16[256,1536]{1,0:T(8,128)(2,1)} %copy-done.15, bf16[256,768]{1,0:T(8,128)(2,1)} %attention_late.1.own_ref, ...), custom_call_target="tpu_custom_call" | custom-call | flops 6039797760 | bytes 23592960 | tf_op jit(solution)/shard_map/ffn_part/pallas_call | solution.py:346
  203.9 1.6 collective-permute-start.29
  205.6 15.4 %ffn_part.2 = (f32[256,1536]{1,0:T(8,128)}, bf16[256,1536]{1,0:T(8,128)(2,1)}) custom-call(s32[2,32]{1,0:T(2,128)S(1)} %pad_add_fusion.spots_ref, s32[2]{0:T(128)S(1)} %pad_add_fusion.2.side_ref, bf16[256,1536]{1,0:T(8,128)(2,1)} %copy-done.12, bf16[256,1536]{1,0:T(8,128)(2,1)} %copy-done.15, bf16[256,768]{1,0:T(8,128)(2,1)S(1)} %copy-done.9, ...), custom_call_target="tpu_custom_call" | custom-call | flops 6039797760 | bytes 23592960 | tf_op jit(solution)/shard_map/ffn_part/pallas_call | solution.py:346
  222.6 16.4 %collective-permute-done.27 = bf16[256,1536]{1,0:T(8,128)(2,1)S(1)} collective-permute-done((bf16[256,1536]{1,0:T(8,128)(2,1)}, bf16[256,1536]{1,0:T(8,128)(2,1)S(1)}, u32[]{:S(2)}, u32[]{:S(2)}) %collective-permute-start.27) | collective-permute-done | bytes 786464 | tf_op jit(solution)/shard_map/ppermute | solution.py:550
  239.3 1.2 pad_maximum_fusion
  (132 shorter events, 25.1 us)
Async XLA Ops:
  0.6 11.9 %copy-start.23 = (f32[48,8192]{1,0:T(8,128)S(1)}, f32[48,8192]{1,0:T(8,128)}, u32[]{:S(2)}) copy-start(f32[48,8192]{1,0:T(8,128)} %param.18) | copy-start | bytes 4718596
  2.6 13.7 %all-to-all-start = ((s32[16,1,32]{2,1,0:T(1,128)}), s32[16,1,32]{2,1,0:T(1,128)S(1)}, u32[]{:S(2)}, u32[]{:S(2)}) async-start(s32[16,1,32]{2,1,0:T(1,128)} %sub.101), calls=%async_computation | async-start | bytes 16384 | tf_op jit(solution)/shard_map/all_to_all | solution.py:415
  25.0 65.8 %all-to-all-start.1 = ((bf16[16,32,1536]{2,1,0:T(8,128)(2,1)}), bf16[16,32,1536]{2,1,0:T(8,128)(2,1)}, u32[]{:S(2)}, u32[]{:S(2)}) async-start(bf16[16,32,1536]{2,1,0:T(8,128)(2,1)} %bitcast.4), calls=%async_computation.1 | async-start | bytes 3145728 | tf_op jit(solution)/shard_map/all_to_all | solution.py:421
  36.5 1.9 collective-permute-start.1
  36.9 14.5 %collective-permute-start.2 = (bf16[2,48,2816]{2,1,0:T(8,128)(2,1)S(1)}, bf16[2,48,2816]{2,1,0:T(8,128)(2,1)S(1)}, u32[]{:S(2)}, u32[]{:S(2)}) collective-permute-start(bf16[2,48,2816]{2,1,0:T(8,128)(2,1)S(1)} %pad_maximum_fusion.4), channel_id=1, source_target_pairs={{0,16},{16,0},{1,17},{17,1},{2,18},{18,2},{3,19},{19,3},{4,20},{20... | collective-permute-start | bytes 1622024 | tf_op jit(solution)/shard_map/ppermute | solution.py:462
  51.5 1.6 collective-permute-start.3
  53.2 25.1 %copy-start = (bf16[96,2816]{1,0:T(8,128)(2,1)}, bf16[96,2816]{1,0:T(8,128)(2,1)S(1)}, u32[]{:S(2)}) copy-start(bf16[96,2816]{1,0:T(8,128)(2,1)S(1)} %pad_maximum_fusion.5.refs_8_) | copy-start | bytes 1622020
  53.2 13.6 %collective-permute-start.4 = (bf16[96,2816]{1,0:T(8,128)(2,1)S(1)}, bf16[96,2816]{1,0:T(8,128)(2,1)S(1)}, u32[]{:S(2)}, u32[]{:S(2)}) collective-permute-start(bf16[96,2816]{1,0:T(8,128)(2,1)S(1)} %pad_maximum_fusion.3.refs_0_), channel_id=1, source_target_pairs={{0,4},{4,8},{8,12},{12,14},{14,10},{10,6},{6,2},{2,0},{5,1},{9,5},... | collective-permute-start | bytes 1622024 | tf_op jit(solution)/shard_map/ppermute | solution.py:48
  55.0 17.6 %collective-permute-start.6 = (bf16[96,2816]{1,0:T(8,128)(2,1)S(1)}, bf16[96,2816]{1,0:T(8,128)(2,1)S(1)}, u32[]{:S(2)}, u32[]{:S(2)}) collective-permute-start(bf16[96,2816]{1,0:T(8,128)(2,1)S(1)} %pad_maximum_fusion.5.refs_8_), channel_id=1, source_target_pairs={{0,4},{4,8},{8,12},{12,14},{14,10},{10,6},{6,2},{2,0},{5,1},{9,5},... | collective-permute-start | bytes 1622024 | tf_op jit(solution)/shard_map/ppermute | solution.py:48
  57.3 27.5 %collective-permute-start.13 = (bf16[384,1536]{1,0:T(8,128)(2,1)S(1)}, bf16[384,1536]{1,0:T(8,128)(2,1)}, u32[]{:S(2)}, u32[]{:S(2)}) collective-permute-start(bf16[384,1536]{1,0:T(8,128)(2,1)S(1)} %copy-done.20), channel_id=1, source_target_pairs={{0,16},{16,0},{1,17},{17,1},{2,18},{18,2},{3,19},{19,3},{4,20},{20... | collective-permute-start | bytes 3538952 | tf_op jit(solution)/shard_map/ppermute | solution.py:490
  66.8 18.1 %collective-permute-start.5 = (bf16[96,2816]{1,0:T(8,128)(2,1)S(1)}, bf16[96,2816]{1,0:T(8,128)(2,1)S(1)}, u32[]{:S(2)}, u32[]{:S(2)}) collective-permute-start(bf16[96,2816]{1,0:T(8,128)(2,1)S(1)} %collective-permute-done.4.refs_1_), channel_id=1, source_target_pairs={{0,4},{4,8},{8,12},{12,14},{14,10},{10,6},{6,2},{2,0},{5,1},{9,5},... | collective-permute-start | bytes 1622024 | tf_op jit(solution)/shard_map/ppermute | solution.py:48
  72.6 17.3 %copy-start.2 = (bf16[96,2816]{1,0:T(8,128)(2,1)}, bf16[96,2816]{1,0:T(8,128)(2,1)S(1)}, u32[]{:S(2)}) copy-start(bf16[96,2816]{1,0:T(8,128)(2,1)S(1)} %collective-permute-done.6.refs_9_) | copy-start | bytes 1622020
  72.6 12.3 %collective-permute-start.8 = (bf16[96,2816]{1,0:T(8,128)(2,1)S(1)}, bf16[96,2816]{1,0:T(8,128)(2,1)S(1)}, u32[]{:S(2)}, u32[]{:S(2)}) collective-permute-start(bf16[96,2816]{1,0:T(8,128)(2,1)S(1)} %collective-permute-done.6.refs_9_), channel_id=1, source_target_pairs={{0,4},{4,8},{8,12},{12,14},{14,10},{10,6},{6,2},{2,0},{5,1},{9,5},... | collective-permute-start | bytes 1622024 | tf_op jit(solution)/shard_map/ppermute | solution.py:48
  84.9 34.7 %collective-permute-start.14 = (bf16[384,1536]{1,0:T(8,128)(2,1)}, bf16[384,1536]{1,0:T(8,128)(2,1)}, u32[]{:S(2)}, u32[]{:S(2)}) collective-permute-start(bf16[384,1536]{1,0:T(8,128)(2,1)} %collective-permute-done.13.w_first_ref), channel_id=1, source_target_pairs={{0,1},{1,0},{2,3},{3,2},{4,5},{5,4},{6,7},{7,6},{8,9},{9,8},{10,11... | collective-permute-start | bytes 3538952 | tf_op jit(solution)/shard_map/ppermute | solution.py:493
  84.9 11.0 %collective-permute-start.10 = (bf16[96,2816]{1,0:T(8,128)(2,1)S(1)}, bf16[96,2816]{1,0:T(8,128)(2,1)}, u32[]{:S(2)}, u32[]{:S(2)}) collective-permute-start(bf16[96,2816]{1,0:T(8,128)(2,1)S(1)} %collective-permute-done.8.refs_10_), channel_id=1, source_target_pairs={{0,4},{4,8},{8,12},{12,14},{14,10},{10,6},{6,2},{2,0},{5,1},{9,5},... | collective-permute-start | bytes 1622024 | tf_op jit(solution)/shard_map/ppermute | solution.py:48
  92.8 22.1 %copy-start.12 = (bf16[256,1536]{1,0:T(8,128)(2,1)}, bf16[256,1536]{1,0:T(8,128)(2,1)S(1)}, u32[]{:S(2)}) copy-start(bf16[256,1536]{1,0:T(8,128)(2,1)S(1)} %convolution_convert_fusion.own_ref.emb_own_ref) | copy-start | bytes 2359300
  92.8 9.4 %collective-permute-start.7 = (bf16[96,2816]{1,0:T(8,128)(2,1)S(1)}, bf16[96,2816]{1,0:T(8,128)(2,1)S(1)}, u32[]{:S(2)}, u32[]{:S(2)}) collective-permute-start(bf16[96,2816]{1,0:T(8,128)(2,1)S(1)} %collective-permute-done.5.refs_2_), channel_id=1, source_target_pairs={{0,4},{4,8},{8,12},{12,14},{14,10},{10,6},{6,2},{2,0},{5,1},{9,5},... | collective-permute-start | bytes 1622024 | tf_op jit(solution)/shard_map/ppermute | solution.py:48
  97.8 22.9 %collective-permute-start = (bf16[256,1536]{1,0:T(8,128)(2,1)S(1)}, bf16[256,1536]{1,0:T(8,128)(2,1)S(1)}, u32[]{:S(2)}, u32[]{:S(2)}) collective-permute-start(bf16[256,1536]{1,0:T(8,128)(2,1)S(1)} %convolution_convert_fusion.own_ref.emb_own_ref), channel_id=1, source_target_pairs={{0,16},{16,0},{1,17},{17,1},{2,18},{18,2},{3,19},{19,3},{4,20},{20... | collective-permute-start | bytes 2359304 | tf_op jit(solution)/shard_map/ppermute | solution.py:487
  102.2 10.8 %collective-permute-start.9 = (bf16[96,2816]{1,0:T(8,128)(2,1)S(1)}, bf16[96,2816]{1,0:T(8,128)(2,1)S(1)}, u32[]{:S(2)}, u32[]{:S(2)}) collective-permute-start(bf16[96,2816]{1,0:T(8,128)(2,1)S(1)} %collective-permute-done.7.refs_3_), channel_id=1, source_target_pairs={{0,4},{4,8},{8,12},{12,14},{14,10},{10,6},{6,2},{2,0},{5,1},{9,5},... | collective-permute-start | bytes 1622024 | tf_op jit(solution)/shard_map/ppermute | solution.py:48
  104.7 14.1 %collective-permute-start.12 = (bf16[96,2816]{1,0:T(8,128)(2,1)}, bf16[96,2816]{1,0:T(8,128)(2,1)S(1)}, u32[]{:S(2)}, u32[]{:S(2)}) collective-permute-start(bf16[96,2816]{1,0:T(8,128)(2,1)} %collective-permute-done.10.refs_11_), channel_id=1, source_target_pairs={{0,4},{4,8},{8,12},{12,14},{14,10},{10,6},{6,2},{2,0},{5,1},{9,5},... | collective-permute-start | bytes 1622024 | tf_op jit(solution)/shard_map/ppermute | solution.py:48
  113.0 43.6 %copy-start.4 = (bf16[96,2816]{1,0:T(8,128)(2,1)}, bf16[96,2816]{1,0:T(8,128)(2,1)S(1)}, u32[]{:S(2)}) copy-start(bf16[96,2816]{1,0:T(8,128)(2,1)S(1)} %collective-permute-done.9.refs_4_) | copy-start | bytes 1622020
  113.0 11.6 %collective-permute-start.11 = (bf16[96,2816]{1,0:T(8,128)(2,1)S(1)}, bf16[96,2816]{1,0:T(8,128)(2,1)S(1)}, u32[]{:S(2)}, u32[]{:S(2)}) collective-permute-start(bf16[96,2816]{1,0:T(8,128)(2,1)S(1)} %collective-permute-done.9.refs_4_), channel_id=1, source_target_pairs={{0,4},{4,8},{8,12},{12,14},{14,10},{10,6},{6,2},{2,0},{5,1},{9,5},... | collective-permute-start | bytes 1622024 | tf_op jit(solution)/shard_map/ppermute | solution.py:48
  114.9 41.6 %collective-permute-start.20 = (bf16[5,96,2816]{2,1,0:T(8,128)(2,1)}, bf16[5,96,2816]{2,1,0:T(8,128)(2,1)}, u32[]{:S(2)}, u32[]{:S(2)}) collective-permute-start(bf16[5,96,2816]{2,1,0:T(8,128)(2,1)} %bitcast_dynamic-update-slice_fusion.5), channel_id=1, source_target_pairs={{0,1},{1,0},{2,3},{3,2},{4,5},{5,4},{6,7},{7,6},{8,9},{9,8},{10,11... | collective-permute-start | bytes 8110088 | tf_op jit(solution)/shard_map/ppermute | solution.py:497
  118.7 17.5 %copy-start.14 = (bf16[96,2816]{1,0:T(8,128)(2,1)}, bf16[96,2816]{1,0:T(8,128)(2,1)S(1)}, u32[]{:S(2)}) copy-start(bf16[96,2816]{1,0:T(8,128)(2,1)S(1)} %collective-permute-done.12.refs_12_) | copy-start | bytes 1622020
  119.6 36.9 %collective-permute-start.23 = (bf16[5,96,2816]{2,1,0:T(8,128)(2,1)}, bf16[5,96,2816]{2,1,0:T(8,128)(2,1)}, u32[]{:S(2)}, u32[]{:S(2)}) collective-permute-start(bf16[5,96,2816]{2,1,0:T(8,128)(2,1)} %bitcast_dynamic-update-slice_fusion), channel_id=1, source_target_pairs={{0,1},{1,0},{2,3},{3,2},{4,5},{5,4},{6,7},{7,6},{8,9},{9,8},{10,11... | collective-permute-start | bytes 8110088 | tf_op jit(solution)/shard_map/ppermute | solution.py:497
  119.6 10.8 %collective-permute-start.16 = (bf16[96,2816]{1,0:T(8,128)(2,1)S(1)}, bf16[96,2816]{1,0:T(8,128)(2,1)}, u32[]{:S(2)}, u32[]{:S(2)}) collective-permute-start(bf16[96,2816]{1,0:T(8,128)(2,1)S(1)} %collective-permute-done.12.refs_12_), channel_id=1, source_target_pairs={{0,4},{4,8},{8,12},{12,14},{14,10},{10,6},{6,2},{2,0},{5,1},{9,5},... | collective-permute-start | bytes 1622024 | tf_op jit(solution)/shard_map/ppermute | solution.py:48
  120.7 16.6 %copy-start.15 = (bf16[256,1536]{1,0:T(8,128)(2,1)}, bf16[256,1536]{1,0:T(8,128)(2,1)S(1)}, u32[]{:S(2)}) copy-start(bf16[256,1536]{1,0:T(8,128)(2,1)S(1)} %collective-permute-done.other_ref.emb_other_ref) | copy-start | bytes 2359300
  124.5 32.0 %copy-start.6 = (bf16[96,2816]{1,0:T(8,128)(2,1)}, bf16[96,2816]{1,0:T(8,128)(2,1)S(1)}, u32[]{:S(2)}) copy-start(bf16[96,2816]{1,0:T(8,128)(2,1)S(1)} %collective-permute-done.11.refs_5_) | copy-start | bytes 1622020
  124.5 11.7 %collective-permute-start.15 = (bf16[96,2816]{1,0:T(8,128)(2,1)S(1)}, bf16[96,2816]{1,0:T(8,128)(2,1)}, u32[]{:S(2)}, u32[]{:S(2)}) collective-permute-start(bf16[96,2816]{1,0:T(8,128)(2,1)S(1)} %collective-permute-done.11.refs_5_), channel_id=1, source_target_pairs={{0,4},{4,8},{8,12},{12,14},{14,10},{10,6},{6,2},{2,0},{5,1},{9,5},... | collective-permute-start | bytes 1622024 | tf_op jit(solution)/shard_map/ppermute | solution.py:48
  130.4 11.6 %collective-permute-start.18 = (bf16[96,2816]{1,0:T(8,128)(2,1)}, bf16[96,2816]{1,0:T(8,128)(2,1)}, u32[]{:S(2)}, u32[]{:S(2)}) collective-permute-start(bf16[96,2816]{1,0:T(8,128)(2,1)} %collective-permute-done.16.refs_13_), channel_id=1, source_target_pairs={{0,4},{4,8},{8,12},{12,14},{14,10},{10,6},{6,2},{2,0},{5,1},{9,5},... | collective-permute-start | bytes 1622024 | tf_op jit(solution)/shard_map/ppermute | solution.py:48
  136.2 11.6 %collective-permute-start.17 = (bf16[96,2816]{1,0:T(8,128)(2,1)}, bf16[96,2816]{1,0:T(8,128)(2,1)}, u32[]{:S(2)}, u32[]{:S(2)}) collective-permute-start(bf16[96,2816]{1,0:T(8,128)(2,1)} %collective-permute-done.15.refs_6_), channel_id=1, source_target_pairs={{0,4},{4,8},{8,12},{12,14},{14,10},{10,6},{6,2},{2,0},{5,1},{9,5},... | collective-permute-start | bytes 1622024 | tf_op jit(solution)/shard_map/ppermute | solution.py:48
  139.5 17.9 %copy-start.11 = (s32[1,4]{1,0:T(1,128)S(1)}, s32[1,4]{1,0:T(1,128)}, u32[]{:S(2)}) copy-start(s32[1,4]{1,0:T(1,128)} %param.12) | copy-start | bytes 52
  139.5 14.1 %collective-permute-start.21 = (bf16[2,96,2816]{2,1,0:T(8,128)(2,1)}, bf16[2,96,2816]{2,1,0:T(8,128)(2,1)}, u32[]{:S(2)}, u32[]{:S(2)}) collective-permute-start(bf16[2,96,2816]{2,1,0:T(8,128)(2,1)} %pad_maximum_fusion.1), channel_id=1, source_target_pairs={{0,1},{1,0},{2,3},{3,2},{4,5},{5,4},{6,7},{7,6},{8,9},{9,8},{10,11... | collective-permute-start | bytes 3244040 | tf_op jit(solution)/shard_map/ppermute | solution.py:497
  142.0 11.6 %collective-permute-start.19 = (bf16[96,2816]{1,0:T(8,128)(2,1)}, bf16[96,2816]{1,0:T(8,128)(2,1)}, u32[]{:S(2)}, u32[]{:S(2)}) collective-permute-start(bf16[96,2816]{1,0:T(8,128)(2,1)} %collective-permute-done.18.refs_14_), channel_id=1, source_target_pairs={{0,4},{4,8},{8,12},{12,14},{14,10},{10,6},{6,2},{2,0},{5,1},{9,5},... | collective-permute-start | bytes 1622024 | tf_op jit(solution)/shard_map/ppermute | solution.py:48
  147.8 7.9 %collective-permute-start.24 = (bf16[2,96,2816]{2,1,0:T(8,128)(2,1)}, bf16[2,96,2816]{2,1,0:T(8,128)(2,1)}, u32[]{:S(2)}, u32[]{:S(2)}) collective-permute-start(bf16[2,96,2816]{2,1,0:T(8,128)(2,1)} %pad_maximum_fusion.2), channel_id=1, source_target_pairs={{0,1},{1,0},{2,3},{3,2},{4,5},{5,4},{6,7},{7,6},{8,9},{9,8},{10,11... | collective-permute-start | bytes 3244040 | tf_op jit(solution)/shard_map/ppermute | solution.py:497
  153.6 2.1 collective-permute-start.22
  153.6 2.9 %collective-permute-start.25 = (bf16[96,2816]{1,0:T(8,128)(2,1)}, bf16[96,2816]{1,0:T(8,128)(2,1)S(1)}, u32[]{:S(2)}, u32[]{:S(2)}) collective-permute-start(bf16[96,2816]{1,0:T(8,128)(2,1)} %collective-permute-done.19.refs_15_), channel_id=1, source_target_pairs={{0,1},{1,0},{2,3},{3,2},{4,5},{5,4},{6,7},{7,6},{8,9},{9,8},{10,11... | collective-permute-start | bytes 1622024 | tf_op jit(solution)/shard_map/ppermute | solution.py:497
  169.6 16.5 %copy-start.1 = (bf16[96,2816]{1,0:T(8,128)(2,1)S(1)}, bf16[96,2816]{1,0:T(8,128)(2,1)}, u32[]{:S(2)}) copy-start(bf16[96,2816]{1,0:T(8,128)(2,1)} %copy-done) | copy-start | bytes 1622020
  169.6 16.5 %copy-start.3 = (bf16[96,2816]{1,0:T(8,128)(2,1)S(1)}, bf16[96,2816]{1,0:T(8,128)(2,1)}, u32[]{:S(2)}) copy-start(bf16[96,2816]{1,0:T(8,128)(2,1)} %copy-done.2) | copy-start | bytes 1622020
  173.9 12.3 %collective-permute-start.28 = (bf16[256,768]{1,0:T(8,128)(2,1)}, bf16[256,768]{1,0:T(8,128)(2,1)}, u32[]{:S(2)}, u32[]{:S(2)}) collective-permute-start(bf16[256,768]{1,0:T(8,128)(2,1)} %attention_late.1.own_ref), channel_id=1, source_target_pairs={{0,16},{16,0},{1,17},{17,1},{2,18},{18,2},{3,19},{19,3},{4,20},{20... | collective-permute-start | bytes 1179656 | tf_op jit(solution)/shard_map/ppermute | solution.py:541
  175.5 30.1 %collective-permute-start.26 = (bf16[256,768]{1,0:T(8,128)(2,1)}, bf16[256,768]{1,0:T(8,128)(2,1)S(1)}, u32[]{:S(2)}, u32[]{:S(2)}) collective-permute-start(bf16[256,768]{1,0:T(8,128)(2,1)} %copy-done.8), channel_id=1, source_target_pairs={{0,16},{16,0},{1,17},{17,1},{2,18},{18,2},{3,19},{19,3},{4,20},{20... | collective-permute-start | bytes 1179656 | tf_op jit(solution)/shard_map/ppermute | solution.py:541
  188.2 17.3 %copy-start.9 = (bf16[256,768]{1,0:T(8,128)(2,1)S(1)}, bf16[256,768]{1,0:T(8,128)(2,1)}, u32[]{:S(2)}) copy-start(bf16[256,768]{1,0:T(8,128)(2,1)} %copy-done.8) | copy-start | bytes 1179652
  203.9 18.4 %collective-permute-start.29 = (bf16[256,1536]{1,0:T(8,128)(2,1)}, bf16[256,1536]{1,0:T(8,128)(2,1)S(1)}, u32[]{:S(2)}, u32[]{:S(2)}) collective-permute-start(bf16[256,1536]{1,0:T(8,128)(2,1)} %get-tuple-element.58), channel_id=1, source_target_pairs={{0,16},{16,0},{1,17},{17,1},{2,18},{18,2},{3,19},{19,3},{4,20},{20... | collective-permute-start | bytes 2359304 | tf_op jit(solution)/shard_map/ppermute | solution.py:550
  205.6 16.7 %copy-start.18 = (f32[256,1536]{1,0:T(8,128)S(1)}, f32[256,1536]{1,0:T(8,128)}, u32[]{:S(2)}) copy-start(f32[256,1536]{1,0:T(8,128)} %get-tuple-element.57) | copy-start | bytes 4718596
  205.6 16.7 %copy-start.21 = (bf16[256,1536]{1,0:T(8,128)(2,1)S(1)}, bf16[256,1536]{1,0:T(8,128)(2,1)}, u32[]{:S(2)}) copy-start(bf16[256,1536]{1,0:T(8,128)(2,1)} %get-tuple-element.58) | copy-start | bytes 2359300
  221.0 18.0 %collective-permute-start.27 = (bf16[256,1536]{1,0:T(8,128)(2,1)}, bf16[256,1536]{1,0:T(8,128)(2,1)S(1)}, u32[]{:S(2)}, u32[]{:S(2)}) collective-permute-start(bf16[256,1536]{1,0:T(8,128)(2,1)} %get-tuple-element.53), channel_id=1, source_target_pairs={{0,16},{16,0},{1,17},{17,1},{2,18},{18,2},{3,19},{19,3},{4,20},{20... | collective-permute-start | bytes 2359304 | tf_op jit(solution)/shard_map/ppermute | solution.py:550
  222.3 16.7 %copy-start.19 = (f32[256,1536]{1,0:T(8,128)S(1)}, f32[256,1536]{1,0:T(8,128)}, u32[]{:S(2)}) copy-start(f32[256,1536]{1,0:T(8,128)} %get-tuple-element.52) | copy-start | bytes 4718596
  222.3 16.7 %copy-start.22 = (bf16[256,1536]{1,0:T(8,128)(2,1)S(1)}, bf16[256,1536]{1,0:T(8,128)(2,1)}, u32[]{:S(2)}) copy-start(bf16[256,1536]{1,0:T(8,128)(2,1)} %get-tuple-element.53) | copy-start | bytes 2359300
  (11 other events, 48.8 us)

commit v5 on v4

--- a/solution.py
+++ b/solution.py
@@ -233,7 +233,7 @@
             pltpu.VMEM((step, step), F32),
             pltpu.SemaphoreType.DMA((total,)),
         ],
-        compiler_params=params(48),
+        compiler_params=params(52),
         name="attention_early",
         cost_estimate=pl.CostEstimate(
             flops=4 * tokens * width * cols,
@@ -269,11 +269,8 @@
     first_col,
     spots_ref,
     side_ref,
-    emb_own_ref,
-    emb_other_ref,
-    own_ref,
+    base_ref,
     other_ref,
-    w_own_ref,
     w_first_ref,
     w_second_ref,
     gain_ref,
@@ -305,10 +302,8 @@
     core = side_ref[0]
     first = pl.ds(pl.multiple_of(core * depth, LANES), depth)
     second = pl.ds(pl.multiple_of((1 - core) * depth, LANES), depth)
-    embedded = jnp.where(side_ref[1] == 1, emb_own_ref[...], emb_other_ref[...])
     x = (
-        embedded.astype(F32)
-        + jnp.dot(own_ref[...], w_own_ref[...], preferred_element_type=F32)
+        base_ref[...]
         + jnp.dot(other_ref[:, first], w_first_ref[...], preferred_element_type=F32)
         + jnp.dot(other_ref[:, second], w_second_ref[...], preferred_element_type=F32)
     )
@@ -335,10 +330,8 @@
             part_ref[...] = (total[...] + term).astype(BF)
 
 
-def ffn_part(
-    spots, side, embedded, own, other, w_own, w_first, w_second, gain, down, blocks, first_col
-):
-    tokens, width = embedded[0].shape
+def ffn_part(spots, side, base, other, w_first, w_second, gain, down, blocks, first_col):
+    tokens, width = base.shape
     rows = blocks[0].shape[0]
     total = spots.shape[1]
     ff_half = down.shape[0]
@@ -350,7 +343,7 @@
             jax.ShapeDtypeStruct((tokens, width), BF),
         ),
         in_specs=[pl.BlockSpec(memory_space=pltpu.SMEM)] * 2
-        + in_vmem(8)
+        + in_vmem(5)
         + [pl.BlockSpec(memory_space=pl.ANY)] * (1 + len(blocks)),
         out_specs=tuple(in_vmem(2)),
         scratch_shapes=[
@@ -364,11 +357,11 @@
         compiler_params=params(48),
         name="ffn_part",
         cost_estimate=pl.CostEstimate(
-            flops=2 * tokens * width * (3 * ff_half + 2 * w_own.shape[0]),
-            bytes_accessed=6 * width * ff_half + 4 * w_own.size,
+            flops=2 * tokens * width * (3 * ff_half + 2 * w_first.shape[0]),
+            bytes_accessed=6 * width * ff_half + 4 * w_first.size,
             transcendentals=tokens * ff_half,
         ),
-    )(spots, side, *embedded, own, other, w_own, w_first, w_second, gain, down, *blocks)
+    )(spots, side, base, other, w_first, w_second, gain, down, *blocks)
 
 
 def per_device(
@@ -490,17 +483,16 @@
     out_first = lax.ppermute(
         after(lax.dynamic_slice_in_dim(out_weight, core * out_rows, out_rows), came), "tp", PAIR
     )
-    out_second = lax.ppermute(out_first, "req", core_swap)
-
     def swapped(blocks):
         sent = blocks[0] if len(blocks) == 1 else jnp.stack(blocks)
         return lax.ppermute(sent, "req", core_swap)
 
     cut = (chips + 2) // 2
     for i in range(chips - 1):
-        ready = {2: (embedded_own,), chips - 3: (embedded_other, out_second)}.get(i, ())
+        ready = {2: (embedded_own,), chips - 3: (embedded_other,)}.get(i, ())
         own_ring = ring_more(own_ring, 1, ring_pairs, other_ring[max(i - 1, 0)], *ready)
         other_ring = ring_more(other_ring, 1, ring_pairs, own_ring[i])
+    out_second = lax.ppermute(after(out_first, own_ring[chips - 2]), "req", core_swap)
     blocks = [
         *own_ring,
         *other_ring,
@@ -533,13 +525,12 @@
     late = attention_late(lengths, tenant_ids[0], queries, keys, values, pack, q_local, kv_local)
     finals = []
     for half, attended in enumerate((early, late)):
+        start = jnp.where(tp_index == half, embedded_own, embedded_other).astype(F32)
         residual, part = ffn_part(
             spots,
-            jnp.stack([core, (tp_index == half).astype(jnp.int32)]),
-            (embedded_own, embedded_other),
-            attended,
+            core[None],
+            start + jnp.dot(attended, out_weight, preferred_element_type=F32),
             lax.ppermute(attended, "tp", PAIR),
-            out_weight,
             out_first,
             out_second,
             ffn_gain[None, :],

time: 241 us -> 240 us (level)
  matrix products: 9.39 us -> 14.7 us
  waiting for transfers between devices: 97.5 us -> 94 us
  Pallas kernels: 46.8 us -> 43.4 us
  starting transfers between devices: 52.2 us -> 54.9 us
    ppermute x14, waiting for transfers between devices: 44.4 us -> 50.5 us  [ring_more(): blocks.append(lax.ppermute(last, 'req', pairs))]
    ppermute x1, waiting for transfers between devices: 5.77 us -> 0.01 us  [per_device(): lax.ppermute(after(lax.dynamic_slice_in_dim(out_weight, core * out_rows,...]
    dot_general x0 -> x2, matrix products: none -> 5.32 us  [per_device(): jnp.dot(attended, out_weight, preferred_element_type=F32)]
    ppermute x2, waiting for transfers between devices: 10.2 us -> 5.71 us  [per_device(): lax.ppermute(attended, 'tp', PAIR)]
    pallas_call x2, Pallas kernels: 31 us -> 28.2 us  [ffn_part(): pl.pallas_call(functools.partial(ffn_kernel, len(blocks), first_col), out...]
    unnamed x60 -> x80, local copies, waits for them, and re-layouts: 9.85 us -> 9.83 us
  transfers between devices with their start and end apart: 32 -> 32, of which waited for: 21 -> 20; matrix products, arithmetic and copies ran while one was open for 11% -> 12% of each run, Pallas kernels for 13% -> 18%
where the time goes in v5:
time: 240 us
  waiting for transfers between devices  94 us (39%)
  starting transfers between devices  54.9 us (23%)
  Pallas kernels  43.4 us (18%)
  local copies, waits for them, and re-layouts  15.6 us (6%)
  matrix products  14.7 us (6%)
  other arithmetic  14.2 us (6%)
  between operations  3 us (1%)
    ppermute x14, waiting for transfers between devices, ring_more(): blocks.append(lax.ppermute(last, 'req', pairs))  50.5 us
    ppermute x14, starting transfers between devices, ring_more(): blocks.append(lax.ppermute(last, 'req', pairs))  31.3 us
    pallas_call x2, Pallas kernels, ffn_part(): pl.pallas_call(functools.partial(ffn_kernel, len(blocks), first_col), out...  28.2 us
    ppermute x2, waiting for transfers between devices, per_device(): total = part.astype(F32) + lax.ppermute(part, 'tp', PAIR).astype(F32)  16 us
    ppermute x1, waiting for transfers between devices, per_device(): came = lax.ppermute(away, 'tp', PAIR)  12.9 us
    pallas_call x1, Pallas kernels, attention_early(): pl.pallas_call(functools.partial(project_kernel, q_heads, kv_heads, len(b...  11.6 us
    unnamed x80, local copies, waits for them, and re-layouts  9.83 us
    dot_general x1, matrix products, per_device(): jnp.dot(pick_rows, embed_table, preferred_element_type=F32).astype(BF)  7.37 us
  transfers between devices with their start and end apart: 32, of which 20 were waited for; matrix products, arithmetic and copies ran while one was open for 12% of the time, Pallas kernels for 18%

profile of v5, /device:TPU:0, one launch (start us, length us, event | category | flops | bytes accessed | tf_op | source)
XLA Modules:
  0.0 239.7 jit_solution(10982610065611361411)
XLA Ops:
  2.6 7.4 %all-to-all-start = ((s32[16,1,32]{2,1,0:T(1,128)}), s32[16,1,32]{2,1,0:T(1,128)S(1)}, u32[]{:S(2)}, u32[]{:S(2)}) async-start(s32[16,1,32]{2,1,0:T(1,128)} %sub.101), calls=%async_computation | async-start | bytes 16384 | tf_op jit(solution)/shard_map/all_to_all | solution.py:408
  12.1 4.2 %all-to-all-done = s32[16,1,32]{2,1,0:T(1,128)S(1)} async-done(((s32[16,1,32]{2,1,0:T(1,128)}), s32[16,1,32]{2,1,0:T(1,128)S(1)}, u32[]{:S(2)}, u32[]{:S(2)}) %all-to-all-start) | async-done | bytes 2080 | tf_op jit(solution)/shard_map/all_to_all | solution.py:408
  17.6 7.4 %fusion.1 = bf16[512,1536]{1,0:T(8,128)(2,1)} fusion(bf16[2000,1536]{1,0:T(8,128)(2,1)} %param.13, s32[512]{0:T(512)S(1)} %eq.123), kind=kOutput, calls=%fused_computation.2 | convolution fusion | flops 3147538432 | bytes 7718912 | tf_op jit(solution)/shard_map/dot_general | solution.py:413
  25.0 4.5 %all-to-all-start.1 = ((bf16[16,32,1536]{2,1,0:T(8,128)(2,1)}), bf16[16,32,1536]{2,1,0:T(8,128)(2,1)}, u32[]{:S(2)}, u32[]{:S(2)}) async-start(bf16[16,32,1536]{2,1,0:T(8,128)(2,1)} %bitcast.57), calls=%async_computation.1 | async-start | bytes 3145728 | tf_op jit(solution)/shard_map/all_to_all | solution.py:414
  32.5 4.0 %fusion.3 = (f32[512,384]{1,0:T(8,128)}, f32[512,384]{1,0:T(8,128)}, f32[512,384]{1,0:T(8,128)}) fusion(f32[384]{0:T(512)S(1)} %fusion.14, f32[512]{0:T(512)S(1)} %select_convert_fusion, pred[384]{0:T(512)(128)(4,1)S(1)} %fusion.18), kind=kLoop, calls=%fused_computation.12 | loop fusion | flops 786432 | bytes 2363264 | tf_op jit(solution)/shard_map/jit(_where)/select_n | solution.py:429
  37.0 1.6 collective-permute-start.2
  38.6 12.9 %collective-permute-done.2 = bf16[2,48,2816]{2,1,0:T(8,128)(2,1)S(1)} collective-permute-done((bf16[2,48,2816]{2,1,0:T(8,128)(2,1)S(1)}, bf16[2,48,2816]{2,1,0:T(8,128)(2,1)S(1)}, u32[]{:S(2)}, u32[]{:S(2)}) %collective-permute-start.2) | collective-permute-done | bytes 540704 | tf_op jit(solution)/shard_map/ppermute | solution.py:455
  51.6 1.5 collective-permute-done.3
  53.2 1.8 collective-permute-start.4
  55.0 1.5 collective-permute-start.6
  57.4 1.5 collective-permute-start.25
  59.8 7.1 %collective-permute-done.4.refs_1_ = bf16[96,2816]{1,0:T(8,128)(2,1)S(1)} collective-permute-done((bf16[96,2816]{1,0:T(8,128)(2,1)S(1)}, bf16[96,2816]{1,0:T(8,128)(2,1)S(1)}, u32[]{:S(2)}, u32[]{:S(2)}) %collective-permute-start.4) | collective-permute-done | bytes 540704 | tf_op jit(solution)/shard_map/ppermute | solution.py:48
  66.9 4.8 %collective-permute-start.5 = (bf16[96,2816]{1,0:T(8,128)(2,1)S(1)}, bf16[96,2816]{1,0:T(8,128)(2,1)S(1)}, u32[]{:S(2)}, u32[]{:S(2)}) collective-permute-start(bf16[96,2816]{1,0:T(8,128)(2,1)S(1)} %collective-permute-done.4.refs_1_), channel_id=1, source_target_pairs={{0,4},{4,8},{8,12},{12,14},{14,10},{10,6},{6,2},{2,0},{5,1},{9,5},... | collective-permute-start | bytes 1622024 | tf_op jit(solution)/shard_map/ppermute | solution.py:48
  72.6 4.8 %collective-permute-start.8 = (bf16[96,2816]{1,0:T(8,128)(2,1)S(1)}, bf16[96,2816]{1,0:T(8,128)(2,1)S(1)}, u32[]{:S(2)}, u32[]{:S(2)}) collective-permute-start(bf16[96,2816]{1,0:T(8,128)(2,1)S(1)} %collective-permute-done.6.refs_9_), channel_id=1, source_target_pairs={{0,4},{4,8},{8,12},{12,14},{14,10},{10,6},{6,2},{2,0},{5,1},{9,5},... | collective-permute-start | bytes 1622024 | tf_op jit(solution)/shard_map/ppermute | solution.py:48
  79.1 5.2 %collective-permute-done.8.refs_10_ = bf16[96,2816]{1,0:T(8,128)(2,1)S(1)} collective-permute-done((bf16[96,2816]{1,0:T(8,128)(2,1)S(1)}, bf16[96,2816]{1,0:T(8,128)(2,1)S(1)}, u32[]{:S(2)}, u32[]{:S(2)}) %collective-permute-start.8) | collective-permute-done | bytes 540704 | tf_op jit(solution)/shard_map/ppermute | solution.py:48
  84.3 4.7 %collective-permute-start.10 = (bf16[96,2816]{1,0:T(8,128)(2,1)S(1)}, bf16[96,2816]{1,0:T(8,128)(2,1)}, u32[]{:S(2)}, u32[]{:S(2)}) collective-permute-start(bf16[96,2816]{1,0:T(8,128)(2,1)S(1)} %collective-permute-done.8.refs_10_), channel_id=1, source_target_pairs={{0,4},{4,8},{8,12},{12,14},{14,10},{10,6},{6,2},{2,0},{5,1},{9,5},... | collective-permute-start | bytes 1622024 | tf_op jit(solution)/shard_map/ppermute | solution.py:48
  90.8 2.0 convolution_convert_fusion.own_ref
  92.8 2.5 %collective-permute-start.7 = (bf16[96,2816]{1,0:T(8,128)(2,1)S(1)}, bf16[96,2816]{1,0:T(8,128)(2,1)S(1)}, u32[]{:S(2)}, u32[]{:S(2)}) collective-permute-start(bf16[96,2816]{1,0:T(8,128)(2,1)S(1)} %collective-permute-done.5.refs_2_), channel_id=1, source_target_pairs={{0,4},{4,8},{8,12},{12,14},{14,10},{10,6},{6,2},{2,0},{5,1},{9,5},... | collective-permute-start | bytes 1622024 | tf_op jit(solution)/shard_map/ppermute | solution.py:48
  95.9 1.9 bitcast_dynamic-update-slice_fusion.1
  97.8 1.5 collective-permute-start
  99.3 2.9 %collective-permute-done.7.refs_3_ = bf16[96,2816]{1,0:T(8,128)(2,1)S(1)} collective-permute-done((bf16[96,2816]{1,0:T(8,128)(2,1)S(1)}, bf16[96,2816]{1,0:T(8,128)(2,1)S(1)}, u32[]{:S(2)}, u32[]{:S(2)}) %collective-permute-start.7) | collective-permute-done | bytes 540704 | tf_op jit(solution)/shard_map/ppermute | solution.py:48
  102.2 2.5 %collective-permute-start.9 = (bf16[96,2816]{1,0:T(8,128)(2,1)S(1)}, bf16[96,2816]{1,0:T(8,128)(2,1)S(1)}, u32[]{:S(2)}, u32[]{:S(2)}) collective-permute-start(bf16[96,2816]{1,0:T(8,128)(2,1)S(1)} %collective-permute-done.7.refs_3_), channel_id=1, source_target_pairs={{0,4},{4,8},{8,12},{12,14},{14,10},{10,6},{6,2},{2,0},{5,1},{9,5},... | collective-permute-start | bytes 1622024 | tf_op jit(solution)/shard_map/ppermute | solution.py:48
  104.7 2.0 collective-permute-start.12
  107.6 5.4 %collective-permute-done.9.refs_4_ = bf16[96,2816]{1,0:T(8,128)(2,1)S(1)} collective-permute-done((bf16[96,2816]{1,0:T(8,128)(2,1)S(1)}, bf16[96,2816]{1,0:T(8,128)(2,1)S(1)}, u32[]{:S(2)}, u32[]{:S(2)}) %collective-permute-start.9) | collective-permute-done | bytes 540704 | tf_op jit(solution)/shard_map/ppermute | solution.py:48
  114.1 4.7 %collective-permute-done.12.refs_12_ = bf16[96,2816]{1,0:T(8,128)(2,1)S(1)} collective-permute-done((bf16[96,2816]{1,0:T(8,128)(2,1)}, bf16[96,2816]{1,0:T(8,128)(2,1)S(1)}, u32[]{:S(2)}, u32[]{:S(2)}) %collective-permute-start.12) | collective-permute-done | bytes 540704 | tf_op jit(solution)/shard_map/ppermute | solution.py:48
  122.1 2.4 %collective-permute-done.11.refs_5_ = bf16[96,2816]{1,0:T(8,128)(2,1)S(1)} collective-permute-done((bf16[96,2816]{1,0:T(8,128)(2,1)S(1)}, bf16[96,2816]{1,0:T(8,128)(2,1)S(1)}, u32[]{:S(2)}, u32[]{:S(2)}) %collective-permute-start.11) | collective-permute-done | bytes 540704 | tf_op jit(solution)/shard_map/ppermute | solution.py:48
  125.7 4.7 %collective-permute-done.14.refs_13_ = bf16[96,2816]{1,0:T(8,128)(2,1)S(1)} collective-permute-done((bf16[96,2816]{1,0:T(8,128)(2,1)S(1)}, bf16[96,2816]{1,0:T(8,128)(2,1)S(1)}, u32[]{:S(2)}, u32[]{:S(2)}) %collective-permute-start.14) | collective-permute-done | bytes 540704 | tf_op jit(solution)/shard_map/ppermute | solution.py:48
  131.5 4.7 %collective-permute-done.13.refs_6_ = bf16[96,2816]{1,0:T(8,128)(2,1)S(1)} collective-permute-done((bf16[96,2816]{1,0:T(8,128)(2,1)S(1)}, bf16[96,2816]{1,0:T(8,128)(2,1)S(1)}, u32[]{:S(2)}, u32[]{:S(2)}) %collective-permute-start.13) | collective-permute-done | bytes 540704 | tf_op jit(solution)/shard_map/ppermute | solution.py:48
  136.1 1.1 collective-permute-start.15
  137.2 4.8 %collective-permute-done.16.refs_14_ = bf16[96,2816]{1,0:T(8,128)(2,1)} collective-permute-done((bf16[96,2816]{1,0:T(8,128)(2,1)S(1)}, bf16[96,2816]{1,0:T(8,128)(2,1)}, u32[]{:S(2)}, u32[]{:S(2)}) %collective-permute-start.16) | collective-permute-done | bytes 540704 | tf_op jit(solution)/shard_map/ppermute | solution.py:48
  142.0 1.1 collective-permute-start.17
  144.3 2.1 pad_maximum_fusion.2
  146.5 1.3 collective-permute-done.15.refs_7_
  147.8 5.8 %collective-permute-done.17.refs_15_ = bf16[96,2816]{1,0:T(8,128)(2,1)} collective-permute-done((bf16[96,2816]{1,0:T(8,128)(2,1)}, bf16[96,2816]{1,0:T(8,128)(2,1)}, u32[]{:S(2)}, u32[]{:S(2)}) %collective-permute-start.17) | collective-permute-done | bytes 540704 | tf_op jit(solution)/shard_map/ppermute | solution.py:48
  154.6 1.3 collective-permute-done.20.refs_18_
  156.3 1.9 collective-permute-done.23.refs_21_
  159.0 11.6 %attention_early.1 = (bf16[256,768]{1,0:T(8,128)(2,1)S(1)}, bf16[2,512,384]{2,1,0:T(8,128)(2,1)}, bf16[256,1024]{1,0:T(8,128)(2,1)S(1)}, bf16[512,512]{1,0:T(8,128)(2,1)}, bf16[512,512]{1,0:T(8,128)(2,1)}) custom-call(s32[2,32]{1,0:T(2,128)S(1)} %pad_add_fusion.spots_ref, s32[4]{0:T(128)S(1)} %bitcast.52, s32[4]{0:T(128)S(1)} %bitcast.54, ...), custom_call_target="tpu_custom_call" | custom-call | flops 2415919104 | bytes 9437184 | tf_op jit(solution)/shard_map/attention_early/pallas_call | solution.py:216
  172.8 3.5 %attention_late.1 = bf16[256,768]{1,0:T(8,128)(2,1)S(1)} custom-call(s32[4]{0:T(128)S(1)} %bitcast.53, s32[4]{0:T(128)S(1)} %bitcast.55, bf16[256,1024]{1,0:T(8,128)(2,1)S(1)} %get-tuple-element.56.q_ref, bf16[512,512]{1,0:T(8,128)(2,1)S(1)} %copy-done.19, bf16[512,512]{1,0:T(8,128)(2,1)S(1)} %copy-done.20, bf16[512,384]{1,0:T(8,128)(2,1)S(1)} %fusion.7.pack_ref), custom_call_target="tpu_custom_call" | custom-call | flops 536870912 | bytes 2097152 | tf_op jit(solution)/shard_map/attention_late/pallas_call | solution.py:248
  176.2 1.6 collective-permute-start.28
  179.2 3.4 %convolution_add_fusion.base_ref = f32[256,1536]{1,0:T(8,128)} fusion(bf16[256,768]{1,0:T(8,128)(2,1)S(1)} %attention_late.1, bf16[768,1536]{1,0:T(8,128)(2,1)S(1)} %copy-done, bf16[256,1536]{1,0:T(8,128)(2,1)} %copy-done.23, bf16[256,1536]{1,0:T(8,128)(2,1)} %collective-permute-done.other_ref, pred[]{:T(512)S(6)} %eq.133), kind=kOutput, calls=%fused_computation.3 | convolution fusion | flops 605159424 | bytes 5898241 | tf_op jit(solution)/shard_map/dot_general | solution.py:532
  182.6 5.7 %collective-permute-done.28.other_ref = bf16[256,768]{1,0:T(8,128)(2,1)S(1)} collective-permute-done((bf16[256,768]{1,0:T(8,128)(2,1)S(1)}, bf16[256,768]{1,0:T(8,128)(2,1)S(1)}, u32[]{:S(2)}, u32[]{:S(2)}) %collective-permute-start.28) | collective-permute-done | bytes 393248 | tf_op jit(solution)/shard_map/ppermute | solution.py:533
  188.3 14.1 %ffn_part.3 = (f32[256,1536]{1,0:T(8,128)}, bf16[256,1536]{1,0:T(8,128)(2,1)}) custom-call(s32[2,32]{1,0:T(2,128)S(1)} %pad_add_fusion.spots_ref, s32[1]{0:T(128)} %bitcast.side_ref, f32[256,1536]{1,0:T(8,128)} %convolution_add_fusion.base_ref, bf16[256,768]{1,0:T(8,128)(2,1)S(1)} %collective-permute-done.28.other_ref, ...), custom_call_target="tpu_custom_call" | custom-call | flops 5435817984 | bytes 21233664 | tf_op jit(solution)/shard_map/ffn_part/pallas_call | solution.py:339
  202.4 1.6 collective-permute-start.29
  204.0 1.9 convolution_add_fusion.1.base_ref
  205.9 14.2 %ffn_part.2 = (f32[256,1536]{1,0:T(8,128)}, bf16[256,1536]{1,0:T(8,128)(2,1)}) custom-call(s32[2,32]{1,0:T(2,128)S(1)} %pad_add_fusion.spots_ref, s32[1]{0:T(128)} %bitcast.side_ref, f32[256,1536]{1,0:T(8,128)} %convolution_add_fusion.1.base_ref, bf16[256,768]{1,0:T(8,128)(2,1)S(1)} %collective-permute-done.24.other_ref, ...), custom_call_target="tpu_custom_call" | custom-call | flops 5435817984 | bytes 21233664 | tf_op jit(solution)/shard_map/ffn_part/pallas_call | solution.py:339
  220.1 1.7 collective-permute-start.27
  222.2 16.0 %collective-permute-done.27 = bf16[256,1536]{1,0:T(8,128)(2,1)S(1)} collective-permute-done((bf16[256,1536]{1,0:T(8,128)(2,1)}, bf16[256,1536]{1,0:T(8,128)(2,1)S(1)}, u32[]{:S(2)}, u32[]{:S(2)}) %collective-permute-start.27) | collective-permute-done | bytes 786464 | tf_op jit(solution)/shard_map/ppermute | solution.py:541
  238.5 1.2 pad_maximum_fusion
  (152 shorter events, 28.7 us)
Async XLA Ops:
  2.6 13.7 %all-to-all-start = ((s32[16,1,32]{2,1,0:T(1,128)}), s32[16,1,32]{2,1,0:T(1,128)S(1)}, u32[]{:S(2)}, u32[]{:S(2)}) async-start(s32[16,1,32]{2,1,0:T(1,128)} %sub.101), calls=%async_computation | async-start | bytes 16384 | tf_op jit(solution)/shard_map/all_to_all | solution.py:408
  25.0 65.8 %all-to-all-start.1 = ((bf16[16,32,1536]{2,1,0:T(8,128)(2,1)}), bf16[16,32,1536]{2,1,0:T(8,128)(2,1)}, u32[]{:S(2)}, u32[]{:S(2)}) async-start(bf16[16,32,1536]{2,1,0:T(8,128)(2,1)} %bitcast.57), calls=%async_computation.1 | async-start | bytes 3145728 | tf_op jit(solution)/shard_map/all_to_all | solution.py:414
  36.6 1.9 collective-permute-start.1
  37.0 14.5 %collective-permute-start.2 = (bf16[2,48,2816]{2,1,0:T(8,128)(2,1)S(1)}, bf16[2,48,2816]{2,1,0:T(8,128)(2,1)S(1)}, u32[]{:S(2)}, u32[]{:S(2)}) collective-permute-start(bf16[2,48,2816]{2,1,0:T(8,128)(2,1)S(1)} %pad_maximum_fusion.4), channel_id=1, source_target_pairs={{0,16},{16,0},{1,17},{17,1},{2,18},{18,2},{3,19},{19,3},{4,20},{20... | collective-permute-start | bytes 1622024 | tf_op jit(solution)/shard_map/ppermute | solution.py:455
  51.5 1.6 collective-permute-start.3
  53.2 25.1 %copy-start.3 = (bf16[96,2816]{1,0:T(8,128)(2,1)}, bf16[96,2816]{1,0:T(8,128)(2,1)S(1)}, u32[]{:S(2)}) copy-start(bf16[96,2816]{1,0:T(8,128)(2,1)S(1)} %pad_maximum_fusion.5.refs_8_) | copy-start | bytes 1622020
  53.2 13.6 %collective-permute-start.4 = (bf16[96,2816]{1,0:T(8,128)(2,1)S(1)}, bf16[96,2816]{1,0:T(8,128)(2,1)S(1)}, u32[]{:S(2)}, u32[]{:S(2)}) collective-permute-start(bf16[96,2816]{1,0:T(8,128)(2,1)S(1)} %pad_maximum_fusion.3.refs_0_), channel_id=1, source_target_pairs={{0,4},{4,8},{8,12},{12,14},{14,10},{10,6},{6,2},{2,0},{5,1},{9,5},... | collective-permute-start | bytes 1622024 | tf_op jit(solution)/shard_map/ppermute | solution.py:48
  55.0 17.6 %collective-permute-start.6 = (bf16[96,2816]{1,0:T(8,128)(2,1)S(1)}, bf16[96,2816]{1,0:T(8,128)(2,1)S(1)}, u32[]{:S(2)}, u32[]{:S(2)}) collective-permute-start(bf16[96,2816]{1,0:T(8,128)(2,1)S(1)} %pad_maximum_fusion.5.refs_8_), channel_id=1, source_target_pairs={{0,4},{4,8},{8,12},{12,14},{14,10},{10,6},{6,2},{2,0},{5,1},{9,5},... | collective-permute-start | bytes 1622024 | tf_op jit(solution)/shard_map/ppermute | solution.py:48
  57.4 86.8 %collective-permute-start.25 = (bf16[384,1536]{1,0:T(8,128)(2,1)}, bf16[384,1536]{1,0:T(8,128)(2,1)}, u32[]{:S(2)}, u32[]{:S(2)}) collective-permute-start(bf16[384,1536]{1,0:T(8,128)(2,1)} %constant_dynamic-slice_fusion), channel_id=1, source_target_pairs={{0,16},{16,0},{1,17},{17,1},{2,18},{18,2},{3,19},{19,3},{4,20},{20... | collective-permute-start | bytes 3538952 | tf_op jit(solution)/shard_map/ppermute | solution.py:483
  66.8 23.0 %copy-start.5 = (bf16[96,2816]{1,0:T(8,128)(2,1)}, bf16[96,2816]{1,0:T(8,128)(2,1)S(1)}, u32[]{:S(2)}) copy-start(bf16[96,2816]{1,0:T(8,128)(2,1)S(1)} %collective-permute-done.4.refs_1_) | copy-start | bytes 1622020
  66.9 12.3 %collective-permute-start.5 = (bf16[96,2816]{1,0:T(8,128)(2,1)S(1)}, bf16[96,2816]{1,0:T(8,128)(2,1)S(1)}, u32[]{:S(2)}, u32[]{:S(2)}) collective-permute-start(bf16[96,2816]{1,0:T(8,128)(2,1)S(1)} %collective-permute-done.4.refs_1_), channel_id=1, source_target_pairs={{0,4},{4,8},{8,12},{12,14},{14,10},{10,6},{6,2},{2,0},{5,1},{9,5},... | collective-permute-start | bytes 1622024 | tf_op jit(solution)/shard_map/ppermute | solution.py:48
  72.6 17.2 %copy-start.7 = (bf16[96,2816]{1,0:T(8,128)(2,1)}, bf16[96,2816]{1,0:T(8,128)(2,1)S(1)}, u32[]{:S(2)}) copy-start(bf16[96,2816]{1,0:T(8,128)(2,1)S(1)} %collective-permute-done.6.refs_9_) | copy-start | bytes 1622020
  72.6 11.7 %collective-permute-start.8 = (bf16[96,2816]{1,0:T(8,128)(2,1)S(1)}, bf16[96,2816]{1,0:T(8,128)(2,1)S(1)}, u32[]{:S(2)}, u32[]{:S(2)}) collective-permute-start(bf16[96,2816]{1,0:T(8,128)(2,1)S(1)} %collective-permute-done.6.refs_9_), channel_id=1, source_target_pairs={{0,4},{4,8},{8,12},{12,14},{14,10},{10,6},{6,2},{2,0},{5,1},{9,5},... | collective-permute-start | bytes 1622024 | tf_op jit(solution)/shard_map/ppermute | solution.py:48
  79.1 13.7 %copy-start.9 = (bf16[96,2816]{1,0:T(8,128)(2,1)}, bf16[96,2816]{1,0:T(8,128)(2,1)S(1)}, u32[]{:S(2)}) copy-start(bf16[96,2816]{1,0:T(8,128)(2,1)S(1)} %collective-permute-done.5.refs_2_) | copy-start | bytes 1622020
  84.3 11.6 %collective-permute-start.10 = (bf16[96,2816]{1,0:T(8,128)(2,1)S(1)}, bf16[96,2816]{1,0:T(8,128)(2,1)}, u32[]{:S(2)}, u32[]{:S(2)}) collective-permute-start(bf16[96,2816]{1,0:T(8,128)(2,1)S(1)} %collective-permute-done.8.refs_10_), channel_id=1, source_target_pairs={{0,4},{4,8},{8,12},{12,14},{14,10},{10,6},{6,2},{2,0},{5,1},{9,5},... | collective-permute-start | bytes 1622024 | tf_op jit(solution)/shard_map/ppermute | solution.py:48
  92.8 28.0 %copy-start.23 = (bf16[256,1536]{1,0:T(8,128)(2,1)}, bf16[256,1536]{1,0:T(8,128)(2,1)S(1)}, u32[]{:S(2)}) copy-start(bf16[256,1536]{1,0:T(8,128)(2,1)S(1)} %convolution_convert_fusion.own_ref) | copy-start | bytes 2359300
  92.8 9.4 %collective-permute-start.7 = (bf16[96,2816]{1,0:T(8,128)(2,1)S(1)}, bf16[96,2816]{1,0:T(8,128)(2,1)S(1)}, u32[]{:S(2)}, u32[]{:S(2)}) collective-permute-start(bf16[96,2816]{1,0:T(8,128)(2,1)S(1)} %collective-permute-done.5.refs_2_), channel_id=1, source_target_pairs={{0,4},{4,8},{8,12},{12,14},{14,10},{10,6},{6,2},{2,0},{5,1},{9,5},... | collective-permute-start | bytes 1622024 | tf_op jit(solution)/shard_map/ppermute | solution.py:48
  97.8 23.8 %collective-permute-start = (bf16[256,1536]{1,0:T(8,128)(2,1)S(1)}, bf16[256,1536]{1,0:T(8,128)(2,1)}, u32[]{:S(2)}, u32[]{:S(2)}) collective-permute-start(bf16[256,1536]{1,0:T(8,128)(2,1)S(1)} %convolution_convert_fusion.own_ref), channel_id=1, source_target_pairs={{0,16},{16,0},{1,17},{17,1},{2,18},{18,2},{3,19},{19,3},{4,20},{20... | collective-permute-start | bytes 2359304 | tf_op jit(solution)/shard_map/ppermute | solution.py:480
  102.2 19.4 %copy-start.11 = (bf16[96,2816]{1,0:T(8,128)(2,1)}, bf16[96,2816]{1,0:T(8,128)(2,1)S(1)}, u32[]{:S(2)}) copy-start(bf16[96,2816]{1,0:T(8,128)(2,1)S(1)} %collective-permute-done.7.refs_3_) | copy-start | bytes 1622020
  102.2 10.7 %collective-permute-start.9 = (bf16[96,2816]{1,0:T(8,128)(2,1)S(1)}, bf16[96,2816]{1,0:T(8,128)(2,1)S(1)}, u32[]{:S(2)}, u32[]{:S(2)}) collective-permute-start(bf16[96,2816]{1,0:T(8,128)(2,1)S(1)} %collective-permute-done.7.refs_3_), channel_id=1, source_target_pairs={{0,4},{4,8},{8,12},{12,14},{14,10},{10,6},{6,2},{2,0},{5,1},{9,5},... | collective-permute-start | bytes 1622024 | tf_op jit(solution)/shard_map/ppermute | solution.py:48
  104.7 14.0 %collective-permute-start.12 = (bf16[96,2816]{1,0:T(8,128)(2,1)}, bf16[96,2816]{1,0:T(8,128)(2,1)S(1)}, u32[]{:S(2)}, u32[]{:S(2)}) collective-permute-start(bf16[96,2816]{1,0:T(8,128)(2,1)} %collective-permute-done.10.refs_11_), channel_id=1, source_target_pairs={{0,4},{4,8},{8,12},{12,14},{14,10},{10,6},{6,2},{2,0},{5,1},{9,5},... | collective-permute-start | bytes 1622024 | tf_op jit(solution)/shard_map/ppermute | solution.py:48
  113.0 31.3 %copy-start.13 = (bf16[96,2816]{1,0:T(8,128)(2,1)}, bf16[96,2816]{1,0:T(8,128)(2,1)S(1)}, u32[]{:S(2)}) copy-start(bf16[96,2816]{1,0:T(8,128)(2,1)S(1)} %collective-permute-done.9.refs_4_) | copy-start | bytes 1622020
  113.0 11.6 %collective-permute-start.11 = (bf16[96,2816]{1,0:T(8,128)(2,1)S(1)}, bf16[96,2816]{1,0:T(8,128)(2,1)S(1)}, u32[]{:S(2)}, u32[]{:S(2)}) collective-permute-start(bf16[96,2816]{1,0:T(8,128)(2,1)S(1)} %collective-permute-done.9.refs_4_), channel_id=1, source_target_pairs={{0,4},{4,8},{8,12},{12,14},{14,10},{10,6},{6,2},{2,0},{5,1},{9,5},... | collective-permute-start | bytes 1622024 | tf_op jit(solution)/shard_map/ppermute | solution.py:48
  118.7 17.4 %copy-start.27 = (bf16[96,2816]{1,0:T(8,128)(2,1)}, bf16[96,2816]{1,0:T(8,128)(2,1)S(1)}, u32[]{:S(2)}) copy-start(bf16[96,2816]{1,0:T(8,128)(2,1)S(1)} %collective-permute-done.12.refs_12_) | copy-start | bytes 1622020
  118.8 11.6 %collective-permute-start.14 = (bf16[96,2816]{1,0:T(8,128)(2,1)S(1)}, bf16[96,2816]{1,0:T(8,128)(2,1)S(1)}, u32[]{:S(2)}, u32[]{:S(2)}) collective-permute-start(bf16[96,2816]{1,0:T(8,128)(2,1)S(1)} %collective-permute-done.12.refs_12_), channel_id=1, source_target_pairs={{0,4},{4,8},{8,12},{12,14},{14,10},{10,6},{6,2},{2,0},{5,1},{9,5},... | collective-permute-start | bytes 1622024 | tf_op jit(solution)/shard_map/ppermute | solution.py:48
  120.8 37.5 %collective-permute-start.18 = (bf16[5,96,2816]{2,1,0:T(8,128)(2,1)}, bf16[5,96,2816]{2,1,0:T(8,128)(2,1)}, u32[]{:S(2)}, u32[]{:S(2)}) collective-permute-start(bf16[5,96,2816]{2,1,0:T(8,128)(2,1)} %bitcast_dynamic-update-slice_fusion.5), channel_id=1, source_target_pairs={{0,1},{1,0},{2,3},{3,2},{4,5},{5,4},{6,7},{7,6},{8,9},{9,8},{10,11... | collective-permute-start | bytes 8110088 | tf_op jit(solution)/shard_map/ppermute | solution.py:488
  121.6 36.6 %collective-permute-start.21 = (bf16[5,96,2816]{2,1,0:T(8,128)(2,1)}, bf16[5,96,2816]{2,1,0:T(8,128)(2,1)}, u32[]{:S(2)}, u32[]{:S(2)}) collective-permute-start(bf16[5,96,2816]{2,1,0:T(8,128)(2,1)} %bitcast_dynamic-update-slice_fusion), channel_id=1, source_target_pairs={{0,1},{1,0},{2,3},{3,2},{4,5},{5,4},{6,7},{7,6},{8,9},{9,8},{10,11... | collective-permute-start | bytes 8110088 | tf_op jit(solution)/shard_map/ppermute | solution.py:488
  124.5 19.7 %copy-start.15 = (bf16[96,2816]{1,0:T(8,128)(2,1)}, bf16[96,2816]{1,0:T(8,128)(2,1)S(1)}, u32[]{:S(2)}) copy-start(bf16[96,2816]{1,0:T(8,128)(2,1)S(1)} %collective-permute-done.11.refs_5_) | copy-start | bytes 1622020
  124.5 11.6 %collective-permute-start.13 = (bf16[96,2816]{1,0:T(8,128)(2,1)S(1)}, bf16[96,2816]{1,0:T(8,128)(2,1)S(1)}, u32[]{:S(2)}, u32[]{:S(2)}) collective-permute-start(bf16[96,2816]{1,0:T(8,128)(2,1)S(1)} %collective-permute-done.11.refs_5_), channel_id=1, source_target_pairs={{0,4},{4,8},{8,12},{12,14},{14,10},{10,6},{6,2},{2,0},{5,1},{9,5},... | collective-permute-start | bytes 1622024 | tf_op jit(solution)/shard_map/ppermute | solution.py:48
  130.3 16.1 %copy-start.28 = (bf16[96,2816]{1,0:T(8,128)(2,1)}, bf16[96,2816]{1,0:T(8,128)(2,1)S(1)}, u32[]{:S(2)}) copy-start(bf16[96,2816]{1,0:T(8,128)(2,1)S(1)} %collective-permute-done.14.refs_13_) | copy-start | bytes 1622020
  130.3 11.7 %collective-permute-start.16 = (bf16[96,2816]{1,0:T(8,128)(2,1)S(1)}, bf16[96,2816]{1,0:T(8,128)(2,1)}, u32[]{:S(2)}, u32[]{:S(2)}) collective-permute-start(bf16[96,2816]{1,0:T(8,128)(2,1)S(1)} %collective-permute-done.14.refs_13_), channel_id=1, source_target_pairs={{0,4},{4,8},{8,12},{12,14},{14,10},{10,6},{6,2},{2,0},{5,1},{9,5},... | collective-permute-start | bytes 1622024 | tf_op jit(solution)/shard_map/ppermute | solution.py:48
  136.1 11.7 %collective-permute-start.15 = (bf16[96,2816]{1,0:T(8,128)(2,1)S(1)}, bf16[96,2816]{1,0:T(8,128)(2,1)}, u32[]{:S(2)}, u32[]{:S(2)}) collective-permute-start(bf16[96,2816]{1,0:T(8,128)(2,1)S(1)} %collective-permute-done.13.refs_6_), channel_id=1, source_target_pairs={{0,4},{4,8},{8,12},{12,14},{14,10},{10,6},{6,2},{2,0},{5,1},{9,5},... | collective-permute-start | bytes 1622024 | tf_op jit(solution)/shard_map/ppermute | solution.py:48
  142.0 11.6 %collective-permute-start.17 = (bf16[96,2816]{1,0:T(8,128)(2,1)}, bf16[96,2816]{1,0:T(8,128)(2,1)}, u32[]{:S(2)}, u32[]{:S(2)}) collective-permute-start(bf16[96,2816]{1,0:T(8,128)(2,1)} %collective-permute-done.16.refs_14_), channel_id=1, source_target_pairs={{0,4},{4,8},{8,12},{12,14},{14,10},{10,6},{6,2},{2,0},{5,1},{9,5},... | collective-permute-start | bytes 1622024 | tf_op jit(solution)/shard_map/ppermute | solution.py:48
  144.2 14.8 %copy-start.22 = (s32[1,4]{1,0:T(1,128)S(1)}, s32[1,4]{1,0:T(1,128)}, u32[]{:S(2)}) copy-start(s32[1,4]{1,0:T(1,128)} %param.12) | copy-start | bytes 52
  144.2 9.7 %collective-permute-start.19 = (bf16[2,96,2816]{2,1,0:T(8,128)(2,1)}, bf16[2,96,2816]{2,1,0:T(8,128)(2,1)}, u32[]{:S(2)}, u32[]{:S(2)}) collective-permute-start(bf16[2,96,2816]{2,1,0:T(8,128)(2,1)} %pad_maximum_fusion.1), channel_id=1, source_target_pairs={{0,1},{1,0},{2,3},{3,2},{4,5},{5,4},{6,7},{7,6},{8,9},{9,8},{10,11... | collective-permute-start | bytes 3244040 | tf_op jit(solution)/shard_map/ppermute | solution.py:488
  147.8 8.5 %collective-permute-start.22 = (bf16[2,96,2816]{2,1,0:T(8,128)(2,1)}, bf16[2,96,2816]{2,1,0:T(8,128)(2,1)S(1)}, u32[]{:S(2)}, u32[]{:S(2)}) collective-permute-start(bf16[2,96,2816]{2,1,0:T(8,128)(2,1)} %pad_maximum_fusion.2), channel_id=1, source_target_pairs={{0,1},{1,0},{2,3},{3,2},{4,5},{5,4},{6,7},{7,6},{8,9},{9,8},{10,11... | collective-permute-start | bytes 3244040 | tf_op jit(solution)/shard_map/ppermute | solution.py:488
  153.6 2.3 collective-permute-start.20
  154.0 28.6 %collective-permute-start.26 = (bf16[384,1536]{1,0:T(8,128)(2,1)}, bf16[384,1536]{1,0:T(8,128)(2,1)}, u32[]{:S(2)}, u32[]{:S(2)}) collective-permute-start(bf16[384,1536]{1,0:T(8,128)(2,1)} %collective-permute-done.25.w_first_ref), channel_id=1, source_target_pairs={{0,1},{1,0},{2,3},{3,2},{4,5},{5,4},{6,7},{7,6},{8,9},{9,8},{10,11... | collective-permute-start | bytes 3538952 | tf_op jit(solution)/shard_map/ppermute | solution.py:495
  155.9 2.3 collective-permute-start.23
  176.2 12.0 %collective-permute-start.28 = (bf16[256,768]{1,0:T(8,128)(2,1)S(1)}, bf16[256,768]{1,0:T(8,128)(2,1)S(1)}, u32[]{:S(2)}, u32[]{:S(2)}) collective-permute-start(bf16[256,768]{1,0:T(8,128)(2,1)S(1)} %attention_late.1), channel_id=1, source_target_pairs={{0,16},{16,0},{1,17},{17,1},{2,18},{18,2},{3,19},{19,3},{4,20},{20... | collective-permute-start | bytes 1179656 | tf_op jit(solution)/shard_map/ppermute | solution.py:533
  178.6 27.3 %collective-permute-start.24 = (bf16[256,768]{1,0:T(8,128)(2,1)S(1)}, bf16[256,768]{1,0:T(8,128)(2,1)S(1)}, u32[]{:S(2)}, u32[]{:S(2)}) collective-permute-start(bf16[256,768]{1,0:T(8,128)(2,1)S(1)} %get-tuple-element.51), channel_id=1, source_target_pairs={{0,16},{16,0},{1,17},{17,1},{2,18},{18,2},{3,19},{19,3},{4,20},{20... | collective-permute-start | bytes 1179656 | tf_op jit(solution)/shard_map/ppermute | solution.py:533
  182.6 21.4 %copy-start.24 = (bf16[256,1536]{1,0:T(8,128)(2,1)S(1)}, bf16[256,1536]{1,0:T(8,128)(2,1)}, u32[]{:S(2)}) copy-start(bf16[256,1536]{1,0:T(8,128)(2,1)} %copy-done.23) | copy-start | bytes 2359300
  202.4 19.4 %collective-permute-start.29 = (bf16[256,1536]{1,0:T(8,128)(2,1)}, bf16[256,1536]{1,0:T(8,128)(2,1)S(1)}, u32[]{:S(2)}, u32[]{:S(2)}) collective-permute-start(bf16[256,1536]{1,0:T(8,128)(2,1)} %get-tuple-element.60), channel_id=1, source_target_pairs={{0,16},{16,0},{1,17},{17,1},{2,18},{18,2},{3,19},{19,3},{4,20},{20... | collective-permute-start | bytes 2359304 | tf_op jit(solution)/shard_map/ppermute | solution.py:541
  205.9 15.9 %copy-start.30 = (f32[256,1536]{1,0:T(8,128)S(1)}, f32[256,1536]{1,0:T(8,128)}, u32[]{:S(2)}) copy-start(f32[256,1536]{1,0:T(8,128)} %get-tuple-element.59) | copy-start | bytes 4718596
  205.9 15.9 %copy-start.32 = (bf16[256,1536]{1,0:T(8,128)(2,1)S(1)}, bf16[256,1536]{1,0:T(8,128)(2,1)}, u32[]{:S(2)}) copy-start(bf16[256,1536]{1,0:T(8,128)(2,1)} %get-tuple-element.60) | copy-start | bytes 2359300
  220.1 18.0 %collective-permute-start.27 = (bf16[256,1536]{1,0:T(8,128)(2,1)}, bf16[256,1536]{1,0:T(8,128)(2,1)S(1)}, u32[]{:S(2)}, u32[]{:S(2)}) collective-permute-start(bf16[256,1536]{1,0:T(8,128)(2,1)} %get-tuple-element.55), channel_id=1, source_target_pairs={{0,16},{16,0},{1,17},{17,1},{2,18},{18,2},{3,19},{19,3},{4,20},{20... | collective-permute-start | bytes 2359304 | tf_op jit(solution)/shard_map/ppermute | solution.py:541
  221.9 16.3 %copy-start.31 = (f32[256,1536]{1,0:T(8,128)S(1)}, f32[256,1536]{1,0:T(8,128)}, u32[]{:S(2)}) copy-start(f32[256,1536]{1,0:T(8,128)} %get-tuple-element.54) | copy-start | bytes 4718596
  221.9 16.3 %copy-start.33 = (bf16[256,1536]{1,0:T(8,128)(2,1)S(1)}, bf16[256,1536]{1,0:T(8,128)(2,1)}, u32[]{:S(2)}) copy-start(bf16[256,1536]{1,0:T(8,128)(2,1)} %get-tuple-element.55) | copy-start | bytes 2359300
  (21 other events, 155.0 us)

commit v6 on v5

--- a/solution.py
+++ b/solution.py
@@ -522,15 +522,19 @@
         q_local,
         kv_local,
     )
+    early_other = lax.ppermute(early, "tp", PAIR)
+    queries = after(queries, early_other)
     late = attention_late(lengths, tenant_ids[0], queries, keys, values, pack, q_local, kv_local)
     finals = []
-    for half, attended in enumerate((early, late)):
+    late_other = lax.ppermute(late, "tp", PAIR)
+    sides = ((early, early_other), (late, late_other))
+    for half, (attended, came_over) in enumerate(sides):
         start = jnp.where(tp_index == half, embedded_own, embedded_other).astype(F32)
         residual, part = ffn_part(
             spots,
             core[None],
             start + jnp.dot(attended, out_weight, preferred_element_type=F32),
-            lax.ppermute(attended, "tp", PAIR),
+            came_over,
             out_first,
             out_second,
             ffn_gain[None, :],

time: 240 us -> 241 us (level)
    unnamed x80 -> x86, local copies, waits for them, and re-layouts: 9.83 us -> 8.53 us
  transfers between devices with their start and end apart: 32 -> 32, of which waited for: 20 -> 21; matrix products, arithmetic and copies ran while one was open for 12% -> 12% of each run, Pallas kernels for 18% -> 18%
where the time goes in v6:
time: 241 us; the launch traced here: 240 us
  waiting for transfers between devices  95.7 us (40%)
  starting transfers between devices  54.6 us (23%)
  Pallas kernels  44.2 us (18%)
  matrix products  14.7 us (6%)
  other arithmetic  14.3 us (6%)
  local copies, waits for them, and re-layouts  13.6 us (6%)
  between operations  3 us (1%)
    ppermute x14, waiting for transfers between devices, ring_more(): blocks.append(lax.ppermute(last, 'req', pairs))  50.6 us
    ppermute x14, starting transfers between devices, ring_more(): blocks.append(lax.ppermute(last, 'req', pairs))  31 us
    pallas_call x2, Pallas kernels, ffn_part(): pl.pallas_call(functools.partial(ffn_kernel, len(blocks), first_col), out...  28.3 us
    ppermute x2, waiting for transfers between devices, per_device(): total = part.astype(F32) + lax.ppermute(part, 'tp', PAIR).astype(F32)  17 us
    ppermute x1, waiting for transfers between devices, per_device(): came = lax.ppermute(away, 'tp', PAIR)  12.9 us
    pallas_call x1, Pallas kernels, attention_early(): pl.pallas_call(functools.partial(project_kernel, q_heads, kv_heads, len(b...  12.4 us
    unnamed x86, local copies, waits for them, and re-layouts  8.53 us
    dot_general x1, matrix products, per_device(): jnp.dot(pick_rows, embed_table, preferred_element_type=F32).astype(BF)  7.37 us
  transfers between devices with their start and end apart: 32, of which 21 were waited for; matrix products, arithmetic and copies ran while one was open for 12% of the time, Pallas kernels for 18%

profile of v6, /device:TPU:0, one launch (start us, length us, event | category | flops | bytes accessed | tf_op | source)
XLA Modules:
  0.0 240.0 jit_solution(17326120859473235422)
XLA Ops:
  2.6 7.4 %all-to-all-start = ((s32[16,1,32]{2,1,0:T(1,128)}), s32[16,1,32]{2,1,0:T(1,128)S(1)}, u32[]{:S(2)}, u32[]{:S(2)}) async-start(s32[16,1,32]{2,1,0:T(1,128)} %sub.101), calls=%async_computation | async-start | bytes 16384 | tf_op jit(solution)/shard_map/all_to_all | solution.py:408
  12.1 4.2 %all-to-all-done = s32[16,1,32]{2,1,0:T(1,128)S(1)} async-done(((s32[16,1,32]{2,1,0:T(1,128)}), s32[16,1,32]{2,1,0:T(1,128)S(1)}, u32[]{:S(2)}, u32[]{:S(2)}) %all-to-all-start) | async-done | bytes 2080 | tf_op jit(solution)/shard_map/all_to_all | solution.py:408
  17.6 7.4 %fusion.1 = bf16[512,1536]{1,0:T(8,128)(2,1)} fusion(bf16[2000,1536]{1,0:T(8,128)(2,1)} %param.13, s32[512]{0:T(512)S(1)} %eq.123), kind=kOutput, calls=%fused_computation.2 | convolution fusion | flops 3147538432 | bytes 7718912 | tf_op jit(solution)/shard_map/dot_general | solution.py:413
  25.0 4.5 %all-to-all-start.1 = ((bf16[16,32,1536]{2,1,0:T(8,128)(2,1)}), bf16[16,32,1536]{2,1,0:T(8,128)(2,1)}, u32[]{:S(2)}, u32[]{:S(2)}) async-start(bf16[16,32,1536]{2,1,0:T(8,128)(2,1)} %bitcast.57), calls=%async_computation.1 | async-start | bytes 3145728 | tf_op jit(solution)/shard_map/all_to_all | solution.py:414
  32.6 4.0 %fusion.3 = (f32[512,384]{1,0:T(8,128)}, f32[512,384]{1,0:T(8,128)}, f32[512,384]{1,0:T(8,128)}) fusion(f32[384]{0:T(512)S(1)} %fusion.14, f32[512]{0:T(512)S(1)} %select_convert_fusion, pred[384]{0:T(512)(128)(4,1)S(1)} %fusion.18), kind=kLoop, calls=%fused_computation.12 | loop fusion | flops 786432 | bytes 2363264 | tf_op jit(solution)/shard_map/jit(_where)/select_n | solution.py:429
  37.1 1.6 collective-permute-start.2
  38.7 12.9 %collective-permute-done.2 = bf16[2,48,2816]{2,1,0:T(8,128)(2,1)S(1)} collective-permute-done((bf16[2,48,2816]{2,1,0:T(8,128)(2,1)S(1)}, bf16[2,48,2816]{2,1,0:T(8,128)(2,1)S(1)}, u32[]{:S(2)}, u32[]{:S(2)}) %collective-permute-start.2) | collective-permute-done | bytes 540704 | tf_op jit(solution)/shard_map/ppermute | solution.py:455
  51.8 1.5 collective-permute-done.3
  53.3 1.8 collective-permute-start.4
  55.2 1.5 collective-permute-start.6
  57.5 1.5 collective-permute-start.25
  59.9 7.1 %collective-permute-done.4.refs_1_ = bf16[96,2816]{1,0:T(8,128)(2,1)S(1)} collective-permute-done((bf16[96,2816]{1,0:T(8,128)(2,1)S(1)}, bf16[96,2816]{1,0:T(8,128)(2,1)S(1)}, u32[]{:S(2)}, u32[]{:S(2)}) %collective-permute-start.4) | collective-permute-done | bytes 540704 | tf_op jit(solution)/shard_map/ppermute | solution.py:48
  67.0 4.7 %collective-permute-start.5 = (bf16[96,2816]{1,0:T(8,128)(2,1)S(1)}, bf16[96,2816]{1,0:T(8,128)(2,1)S(1)}, u32[]{:S(2)}, u32[]{:S(2)}) collective-permute-start(bf16[96,2816]{1,0:T(8,128)(2,1)S(1)} %collective-permute-done.4.refs_1_), channel_id=1, source_target_pairs={{0,4},{4,8},{8,12},{12,14},{14,10},{10,6},{6,2},{2,0},{5,1},{9,5},... | collective-permute-start | bytes 1622024 | tf_op jit(solution)/shard_map/ppermute | solution.py:48
  72.8 4.7 %collective-permute-start.8 = (bf16[96,2816]{1,0:T(8,128)(2,1)S(1)}, bf16[96,2816]{1,0:T(8,128)(2,1)S(1)}, u32[]{:S(2)}, u32[]{:S(2)}) collective-permute-start(bf16[96,2816]{1,0:T(8,128)(2,1)S(1)} %collective-permute-done.6.refs_9_), channel_id=1, source_target_pairs={{0,4},{4,8},{8,12},{12,14},{14,10},{10,6},{6,2},{2,0},{5,1},{9,5},... | collective-permute-start | bytes 1622024 | tf_op jit(solution)/shard_map/ppermute | solution.py:48
  79.1 5.2 %collective-permute-done.8.refs_10_ = bf16[96,2816]{1,0:T(8,128)(2,1)S(1)} collective-permute-done((bf16[96,2816]{1,0:T(8,128)(2,1)S(1)}, bf16[96,2816]{1,0:T(8,128)(2,1)S(1)}, u32[]{:S(2)}, u32[]{:S(2)}) %collective-permute-start.8) | collective-permute-done | bytes 540704 | tf_op jit(solution)/shard_map/ppermute | solution.py:48
  84.3 4.7 %collective-permute-start.10 = (bf16[96,2816]{1,0:T(8,128)(2,1)S(1)}, bf16[96,2816]{1,0:T(8,128)(2,1)}, u32[]{:S(2)}, u32[]{:S(2)}) collective-permute-start(bf16[96,2816]{1,0:T(8,128)(2,1)S(1)} %collective-permute-done.8.refs_10_), channel_id=1, source_target_pairs={{0,4},{4,8},{8,12},{12,14},{14,10},{10,6},{6,2},{2,0},{5,1},{9,5},... | collective-permute-start | bytes 1622024 | tf_op jit(solution)/shard_map/ppermute | solution.py:48
  90.8 2.0 convolution_convert_fusion.own_ref
  92.8 2.5 %collective-permute-start.7 = (bf16[96,2816]{1,0:T(8,128)(2,1)S(1)}, bf16[96,2816]{1,0:T(8,128)(2,1)S(1)}, u32[]{:S(2)}, u32[]{:S(2)}) collective-permute-start(bf16[96,2816]{1,0:T(8,128)(2,1)S(1)} %collective-permute-done.5.refs_2_), channel_id=1, source_target_pairs={{0,4},{4,8},{8,12},{12,14},{14,10},{10,6},{6,2},{2,0},{5,1},{9,5},... | collective-permute-start | bytes 1622024 | tf_op jit(solution)/shard_map/ppermute | solution.py:48
  95.9 1.9 bitcast_dynamic-update-slice_fusion.1
  97.8 1.5 collective-permute-start
  99.3 2.9 %collective-permute-done.7.refs_3_ = bf16[96,2816]{1,0:T(8,128)(2,1)S(1)} collective-permute-done((bf16[96,2816]{1,0:T(8,128)(2,1)S(1)}, bf16[96,2816]{1,0:T(8,128)(2,1)S(1)}, u32[]{:S(2)}, u32[]{:S(2)}) %collective-permute-start.7) | collective-permute-done | bytes 540704 | tf_op jit(solution)/shard_map/ppermute | solution.py:48
  102.2 2.5 %collective-permute-start.9 = (bf16[96,2816]{1,0:T(8,128)(2,1)S(1)}, bf16[96,2816]{1,0:T(8,128)(2,1)S(1)}, u32[]{:S(2)}, u32[]{:S(2)}) collective-permute-start(bf16[96,2816]{1,0:T(8,128)(2,1)S(1)} %collective-permute-done.7.refs_3_), channel_id=1, source_target_pairs={{0,4},{4,8},{8,12},{12,14},{14,10},{10,6},{6,2},{2,0},{5,1},{9,5},... | collective-permute-start | bytes 1622024 | tf_op jit(solution)/shard_map/ppermute | solution.py:48
  104.7 2.0 collective-permute-start.12
  107.6 5.4 %collective-permute-done.9.refs_4_ = bf16[96,2816]{1,0:T(8,128)(2,1)S(1)} collective-permute-done((bf16[96,2816]{1,0:T(8,128)(2,1)S(1)}, bf16[96,2816]{1,0:T(8,128)(2,1)S(1)}, u32[]{:S(2)}, u32[]{:S(2)}) %collective-permute-start.9) | collective-permute-done | bytes 540704 | tf_op jit(solution)/shard_map/ppermute | solution.py:48
  114.1 4.7 %collective-permute-done.12.refs_12_ = bf16[96,2816]{1,0:T(8,128)(2,1)S(1)} collective-permute-done((bf16[96,2816]{1,0:T(8,128)(2,1)}, bf16[96,2816]{1,0:T(8,128)(2,1)S(1)}, u32[]{:S(2)}, u32[]{:S(2)}) %collective-permute-start.12) | collective-permute-done | bytes 540704 | tf_op jit(solution)/shard_map/ppermute | solution.py:48
  122.2 2.4 collective-permute-done.11.refs_5_
  125.7 4.7 %collective-permute-done.14.refs_13_ = bf16[96,2816]{1,0:T(8,128)(2,1)S(1)} collective-permute-done((bf16[96,2816]{1,0:T(8,128)(2,1)S(1)}, bf16[96,2816]{1,0:T(8,128)(2,1)S(1)}, u32[]{:S(2)}, u32[]{:S(2)}) %collective-permute-start.14) | collective-permute-done | bytes 540704 | tf_op jit(solution)/shard_map/ppermute | solution.py:48
  131.5 4.7 %collective-permute-done.13.refs_6_ = bf16[96,2816]{1,0:T(8,128)(2,1)S(1)} collective-permute-done((bf16[96,2816]{1,0:T(8,128)(2,1)S(1)}, bf16[96,2816]{1,0:T(8,128)(2,1)S(1)}, u32[]{:S(2)}, u32[]{:S(2)}) %collective-permute-start.13) | collective-permute-done | bytes 540704 | tf_op jit(solution)/shard_map/ppermute | solution.py:48
  136.1 1.1 collective-permute-start.15
  137.3 4.8 %collective-permute-done.16.refs_14_ = bf16[96,2816]{1,0:T(8,128)(2,1)} collective-permute-done((bf16[96,2816]{1,0:T(8,128)(2,1)S(1)}, bf16[96,2816]{1,0:T(8,128)(2,1)}, u32[]{:S(2)}, u32[]{:S(2)}) %collective-permute-start.16) | collective-permute-done | bytes 540704 | tf_op jit(solution)/shard_map/ppermute | solution.py:48
  142.0 1.1 collective-permute-start.17
  144.3 2.1 pad_maximum_fusion.2
  146.5 1.4 collective-permute-done.15.refs_7_
  147.8 5.8 %collective-permute-done.17.refs_15_ = bf16[96,2816]{1,0:T(8,128)(2,1)} collective-permute-done((bf16[96,2816]{1,0:T(8,128)(2,1)}, bf16[96,2816]{1,0:T(8,128)(2,1)}, u32[]{:S(2)}, u32[]{:S(2)}) %collective-permute-start.17) | collective-permute-done | bytes 540704 | tf_op jit(solution)/shard_map/ppermute | solution.py:48
  154.6 1.2 collective-permute-done.20.refs_18_
  157.0 1.7 collective-permute-done.23.refs_21_
  159.5 12.4 %attention_early.1 = (bf16[256,768]{1,0:T(8,128)(2,1)}, bf16[2,512,384]{2,1,0:T(8,128)(2,1)}, bf16[256,1024]{1,0:T(8,128)(2,1)S(1)}, bf16[512,512]{1,0:T(8,128)(2,1)}, bf16[512,512]{1,0:T(8,128)(2,1)}) custom-call(s32[2,32]{1,0:T(2,128)S(1)} %pad_add_fusion.spots_ref, s32[4]{0:T(128)S(1)} %bitcast.52, s32[4]{0:T(128)S(1)} %bitcast.54, s32[1]{0:T(128)} %bitcast.7.half_ref, ...), custom_call_target="tpu_custom_call" | custom-call | flops 2415919104 | bytes 9437184 | tf_op jit(solution)/shard_map/attention_early/pallas_call | solution.py:216
  171.9 1.6 collective-permute-start.24
  173.6 3.3 %convolution_add_fusion.1.base_ref = f32[256,1536]{1,0:T(8,128)} fusion(bf16[256,768]{1,0:T(8,128)(2,1)} %get-tuple-element.52, bf16[768,1536]{1,0:T(8,128)(2,1)S(1)} %copy-done, bf16[256,1536]{1,0:T(8,128)(2,1)} %copy-done.23, bf16[256,1536]{1,0:T(8,128)(2,1)} %copy-done.28, pred[]{:T(512)S(6)} %eq.113), kind=kOutput, calls=%fused_computation.4 | convolution fusion | flops 605159424 | bytes 5898241 | tf_op jit(solution)/shard_map/dot_general | solution.py:536
  176.9 6.5 %collective-permute-done.24.other_ref = bf16[256,768]{1,0:T(8,128)(2,1)} collective-permute-done((bf16[256,768]{1,0:T(8,128)(2,1)}, bf16[256,768]{1,0:T(8,128)(2,1)}, u32[]{:S(2)}, u32[]{:S(2)}) %collective-permute-start.24) | collective-permute-done | bytes 393248 | tf_op jit(solution)/shard_map/ppermute | solution.py:525
  183.5 3.5 %attention_late.1 = bf16[256,768]{1,0:T(8,128)(2,1)S(1)} custom-call(s32[4]{0:T(128)S(1)} %bitcast.53, s32[4]{0:T(128)S(1)} %bitcast.55, bf16[256,1024]{1,0:T(8,128)(2,1)S(1)} %get-tuple-element.58.q_ref, bf16[512,512]{1,0:T(8,128)(2,1)S(1)} %copy-done.19, bf16[512,512]{1,0:T(8,128)(2,1)S(1)} %copy-done.20, bf16[512,384]{1,0:T(8,128)(2,1)S(1)} %fusion.7.pack_ref), custom_call_target="tpu_custom_call" | custom-call | flops 536870912 | bytes 2097152 | tf_op jit(solution)/shard_map/attention_late/pallas_call | solution.py:248
  187.0 1.6 collective-permute-start.28
  188.7 14.2 %ffn_part.2 = (f32[256,1536]{1,0:T(8,128)}, bf16[256,1536]{1,0:T(8,128)(2,1)}) custom-call(s32[2,32]{1,0:T(2,128)S(1)} %pad_add_fusion.spots_ref, s32[1]{0:T(128)} %bitcast.side_ref, f32[256,1536]{1,0:T(8,128)} %convolution_add_fusion.1.base_ref, bf16[256,768]{1,0:T(8,128)(2,1)} %collective-permute-done.24.other_ref, ...), custom_call_target="tpu_custom_call" | custom-call | flops 5435817984 | bytes 21233664 | tf_op jit(solution)/shard_map/ffn_part/pallas_call | solution.py:339
  203.4 1.9 convolution_add_fusion.base_ref
  205.4 14.2 %ffn_part.3 = (f32[256,1536]{1,0:T(8,128)}, bf16[256,1536]{1,0:T(8,128)(2,1)}) custom-call(s32[2,32]{1,0:T(2,128)S(1)} %pad_add_fusion.spots_ref, s32[1]{0:T(128)} %bitcast.side_ref, f32[256,1536]{1,0:T(8,128)} %convolution_add_fusion.base_ref, bf16[256,768]{1,0:T(8,128)(2,1)S(1)} %collective-permute-done.28.other_ref, ...), custom_call_target="tpu_custom_call" | custom-call | flops 5435817984 | bytes 21233664 | tf_op jit(solution)/shard_map/ffn_part/pallas_call | solution.py:339
  219.5 1.6 collective-permute-start.29
  222.2 16.2 %collective-permute-done.29 = bf16[256,1536]{1,0:T(8,128)(2,1)S(1)} collective-permute-done((bf16[256,1536]{1,0:T(8,128)(2,1)}, bf16[256,1536]{1,0:T(8,128)(2,1)S(1)}, u32[]{:S(2)}, u32[]{:S(2)}) %collective-permute-start.29) | collective-permute-done | bytes 786464 | tf_op jit(solution)/shard_map/ppermute | solution.py:545
  238.8 1.2 pad_maximum_fusion
  (158 shorter events, 27.8 us)
Async XLA Ops:
  2.6 13.7 %all-to-all-start = ((s32[16,1,32]{2,1,0:T(1,128)}), s32[16,1,32]{2,1,0:T(1,128)S(1)}, u32[]{:S(2)}, u32[]{:S(2)}) async-start(s32[16,1,32]{2,1,0:T(1,128)} %sub.101), calls=%async_computation | async-start | bytes 16384 | tf_op jit(solution)/shard_map/all_to_all | solution.py:408
  25.0 65.8 %all-to-all-start.1 = ((bf16[16,32,1536]{2,1,0:T(8,128)(2,1)}), bf16[16,32,1536]{2,1,0:T(8,128)(2,1)}, u32[]{:S(2)}, u32[]{:S(2)}) async-start(bf16[16,32,1536]{2,1,0:T(8,128)(2,1)} %bitcast.57), calls=%async_computation.1 | async-start | bytes 3145728 | tf_op jit(solution)/shard_map/all_to_all | solution.py:414
  36.7 1.9 collective-permute-start.1
  37.1 14.5 %collective-permute-start.2 = (bf16[2,48,2816]{2,1,0:T(8,128)(2,1)S(1)}, bf16[2,48,2816]{2,1,0:T(8,128)(2,1)S(1)}, u32[]{:S(2)}, u32[]{:S(2)}) collective-permute-start(bf16[2,48,2816]{2,1,0:T(8,128)(2,1)S(1)} %pad_maximum_fusion.4), channel_id=1, source_target_pairs={{0,16},{16,0},{1,17},{17,1},{2,18},{18,2},{3,19},{19,3},{4,20},{20... | collective-permute-start | bytes 1622024 | tf_op jit(solution)/shard_map/ppermute | solution.py:455
  51.6 1.6 collective-permute-start.3
  53.3 25.0 %copy-start.3 = (bf16[96,2816]{1,0:T(8,128)(2,1)}, bf16[96,2816]{1,0:T(8,128)(2,1)S(1)}, u32[]{:S(2)}) copy-start(bf16[96,2816]{1,0:T(8,128)(2,1)S(1)} %pad_maximum_fusion.5.refs_8_) | copy-start | bytes 1622020
  53.3 13.6 %collective-permute-start.4 = (bf16[96,2816]{1,0:T(8,128)(2,1)S(1)}, bf16[96,2816]{1,0:T(8,128)(2,1)S(1)}, u32[]{:S(2)}, u32[]{:S(2)}) collective-permute-start(bf16[96,2816]{1,0:T(8,128)(2,1)S(1)} %pad_maximum_fusion.3.refs_0_), channel_id=1, source_target_pairs={{0,4},{4,8},{8,12},{12,14},{14,10},{10,6},{6,2},{2,0},{5,1},{9,5},... | collective-permute-start | bytes 1622024 | tf_op jit(solution)/shard_map/ppermute | solution.py:48
  55.2 17.6 %collective-permute-start.6 = (bf16[96,2816]{1,0:T(8,128)(2,1)S(1)}, bf16[96,2816]{1,0:T(8,128)(2,1)S(1)}, u32[]{:S(2)}, u32[]{:S(2)}) collective-permute-start(bf16[96,2816]{1,0:T(8,128)(2,1)S(1)} %pad_maximum_fusion.5.refs_8_), channel_id=1, source_target_pairs={{0,4},{4,8},{8,12},{12,14},{14,10},{10,6},{6,2},{2,0},{5,1},{9,5},... | collective-permute-start | bytes 1622024 | tf_op jit(solution)/shard_map/ppermute | solution.py:48
  57.5 86.7 %collective-permute-start.25 = (bf16[384,1536]{1,0:T(8,128)(2,1)}, bf16[384,1536]{1,0:T(8,128)(2,1)}, u32[]{:S(2)}, u32[]{:S(2)}) collective-permute-start(bf16[384,1536]{1,0:T(8,128)(2,1)} %constant_dynamic-slice_fusion), channel_id=1, source_target_pairs={{0,16},{16,0},{1,17},{17,1},{2,18},{18,2},{3,19},{19,3},{4,20},{20... | collective-permute-start | bytes 3538952 | tf_op jit(solution)/shard_map/ppermute | solution.py:483
  67.0 22.9 %copy-start.5 = (bf16[96,2816]{1,0:T(8,128)(2,1)}, bf16[96,2816]{1,0:T(8,128)(2,1)S(1)}, u32[]{:S(2)}) copy-start(bf16[96,2816]{1,0:T(8,128)(2,1)S(1)} %collective-permute-done.4.refs_1_) | copy-start | bytes 1622020
  67.0 12.2 %collective-permute-start.5 = (bf16[96,2816]{1,0:T(8,128)(2,1)S(1)}, bf16[96,2816]{1,0:T(8,128)(2,1)S(1)}, u32[]{:S(2)}, u32[]{:S(2)}) collective-permute-start(bf16[96,2816]{1,0:T(8,128)(2,1)S(1)} %collective-permute-done.4.refs_1_), channel_id=1, source_target_pairs={{0,4},{4,8},{8,12},{12,14},{14,10},{10,6},{6,2},{2,0},{5,1},{9,5},... | collective-permute-start | bytes 1622024 | tf_op jit(solution)/shard_map/ppermute | solution.py:48
  72.8 17.1 %copy-start.7 = (bf16[96,2816]{1,0:T(8,128)(2,1)}, bf16[96,2816]{1,0:T(8,128)(2,1)S(1)}, u32[]{:S(2)}) copy-start(bf16[96,2816]{1,0:T(8,128)(2,1)S(1)} %collective-permute-done.6.refs_9_) | copy-start | bytes 1622020
  72.8 11.6 %collective-permute-start.8 = (bf16[96,2816]{1,0:T(8,128)(2,1)S(1)}, bf16[96,2816]{1,0:T(8,128)(2,1)S(1)}, u32[]{:S(2)}, u32[]{:S(2)}) collective-permute-start(bf16[96,2816]{1,0:T(8,128)(2,1)S(1)} %collective-permute-done.6.refs_9_), channel_id=1, source_target_pairs={{0,4},{4,8},{8,12},{12,14},{14,10},{10,6},{6,2},{2,0},{5,1},{9,5},... | collective-permute-start | bytes 1622024 | tf_op jit(solution)/shard_map/ppermute | solution.py:48
  84.3 11.6 %collective-permute-start.10 = (bf16[96,2816]{1,0:T(8,128)(2,1)S(1)}, bf16[96,2816]{1,0:T(8,128)(2,1)}, u32[]{:S(2)}, u32[]{:S(2)}) collective-permute-start(bf16[96,2816]{1,0:T(8,128)(2,1)S(1)} %collective-permute-done.8.refs_10_), channel_id=1, source_target_pairs={{0,4},{4,8},{8,12},{12,14},{14,10},{10,6},{6,2},{2,0},{5,1},{9,5},... | collective-permute-start | bytes 1622024 | tf_op jit(solution)/shard_map/ppermute | solution.py:48
  92.8 28.0 %copy-start.23 = (bf16[256,1536]{1,0:T(8,128)(2,1)}, bf16[256,1536]{1,0:T(8,128)(2,1)S(1)}, u32[]{:S(2)}) copy-start(bf16[256,1536]{1,0:T(8,128)(2,1)S(1)} %convolution_convert_fusion.own_ref) | copy-start | bytes 2359300
  92.8 9.4 %collective-permute-start.7 = (bf16[96,2816]{1,0:T(8,128)(2,1)S(1)}, bf16[96,2816]{1,0:T(8,128)(2,1)S(1)}, u32[]{:S(2)}, u32[]{:S(2)}) collective-permute-start(bf16[96,2816]{1,0:T(8,128)(2,1)S(1)} %collective-permute-done.5.refs_2_), channel_id=1, source_target_pairs={{0,4},{4,8},{8,12},{12,14},{14,10},{10,6},{6,2},{2,0},{5,1},{9,5},... | collective-permute-start | bytes 1622024 | tf_op jit(solution)/shard_map/ppermute | solution.py:48
  97.8 23.8 %collective-permute-start = (bf16[256,1536]{1,0:T(8,128)(2,1)S(1)}, bf16[256,1536]{1,0:T(8,128)(2,1)S(1)}, u32[]{:S(2)}, u32[]{:S(2)}) collective-permute-start(bf16[256,1536]{1,0:T(8,128)(2,1)S(1)} %convolution_convert_fusion.own_ref), channel_id=1, source_target_pairs={{0,16},{16,0},{1,17},{17,1},{2,18},{18,2},{3,19},{19,3},{4,20},{20... | collective-permute-start | bytes 2359304 | tf_op jit(solution)/shard_map/ppermute | solution.py:480
  102.2 19.4 %copy-start.11 = (bf16[96,2816]{1,0:T(8,128)(2,1)}, bf16[96,2816]{1,0:T(8,128)(2,1)S(1)}, u32[]{:S(2)}) copy-start(bf16[96,2816]{1,0:T(8,128)(2,1)S(1)} %collective-permute-done.7.refs_3_) | copy-start | bytes 1622020
  102.2 10.7 %collective-permute-start.9 = (bf16[96,2816]{1,0:T(8,128)(2,1)S(1)}, bf16[96,2816]{1,0:T(8,128)(2,1)S(1)}, u32[]{:S(2)}, u32[]{:S(2)}) collective-permute-start(bf16[96,2816]{1,0:T(8,128)(2,1)S(1)} %collective-permute-done.7.refs_3_), channel_id=1, source_target_pairs={{0,4},{4,8},{8,12},{12,14},{14,10},{10,6},{6,2},{2,0},{5,1},{9,5},... | collective-permute-start | bytes 1622024 | tf_op jit(solution)/shard_map/ppermute | solution.py:48
  104.7 14.0 %collective-permute-start.12 = (bf16[96,2816]{1,0:T(8,128)(2,1)}, bf16[96,2816]{1,0:T(8,128)(2,1)S(1)}, u32[]{:S(2)}, u32[]{:S(2)}) collective-permute-start(bf16[96,2816]{1,0:T(8,128)(2,1)} %collective-permute-done.10.refs_11_), channel_id=1, source_target_pairs={{0,4},{4,8},{8,12},{12,14},{14,10},{10,6},{6,2},{2,0},{5,1},{9,5},... | collective-permute-start | bytes 1622024 | tf_op jit(solution)/shard_map/ppermute | solution.py:48
  113.0 31.3 %copy-start.13 = (bf16[96,2816]{1,0:T(8,128)(2,1)}, bf16[96,2816]{1,0:T(8,128)(2,1)S(1)}, u32[]{:S(2)}) copy-start(bf16[96,2816]{1,0:T(8,128)(2,1)S(1)} %collective-permute-done.9.refs_4_) | copy-start | bytes 1622020
  113.0 11.6 %collective-permute-start.11 = (bf16[96,2816]{1,0:T(8,128)(2,1)S(1)}, bf16[96,2816]{1,0:T(8,128)(2,1)S(1)}, u32[]{:S(2)}, u32[]{:S(2)}) collective-permute-start(bf16[96,2816]{1,0:T(8,128)(2,1)S(1)} %collective-permute-done.9.refs_4_), channel_id=1, source_target_pairs={{0,4},{4,8},{8,12},{12,14},{14,10},{10,6},{6,2},{2,0},{5,1},{9,5},... | collective-permute-start | bytes 1622024 | tf_op jit(solution)/shard_map/ppermute | solution.py:48
  118.8 17.4 %copy-start.26 = (bf16[96,2816]{1,0:T(8,128)(2,1)}, bf16[96,2816]{1,0:T(8,128)(2,1)S(1)}, u32[]{:S(2)}) copy-start(bf16[96,2816]{1,0:T(8,128)(2,1)S(1)} %collective-permute-done.12.refs_12_) | copy-start | bytes 1622020
  118.8 11.6 %collective-permute-start.14 = (bf16[96,2816]{1,0:T(8,128)(2,1)S(1)}, bf16[96,2816]{1,0:T(8,128)(2,1)S(1)}, u32[]{:S(2)}, u32[]{:S(2)}) collective-permute-start(bf16[96,2816]{1,0:T(8,128)(2,1)S(1)} %collective-permute-done.12.refs_12_), channel_id=1, source_target_pairs={{0,4},{4,8},{8,12},{12,14},{14,10},{10,6},{6,2},{2,0},{5,1},{9,5},... | collective-permute-start | bytes 1622024 | tf_op jit(solution)/shard_map/ppermute | solution.py:48
  120.8 37.9 %collective-permute-start.18 = (bf16[5,96,2816]{2,1,0:T(8,128)(2,1)}, bf16[5,96,2816]{2,1,0:T(8,128)(2,1)}, u32[]{:S(2)}, u32[]{:S(2)}) collective-permute-start(bf16[5,96,2816]{2,1,0:T(8,128)(2,1)} %bitcast_dynamic-update-slice_fusion.5), channel_id=1, source_target_pairs={{0,1},{1,0},{2,3},{3,2},{4,5},{5,4},{6,7},{7,6},{8,9},{9,8},{10,11... | collective-permute-start | bytes 8110088 | tf_op jit(solution)/shard_map/ppermute | solution.py:488
  121.6 20.4 %copy-start.28 = (bf16[256,1536]{1,0:T(8,128)(2,1)}, bf16[256,1536]{1,0:T(8,128)(2,1)S(1)}, u32[]{:S(2)}) copy-start(bf16[256,1536]{1,0:T(8,128)(2,1)S(1)} %collective-permute-done.other_ref) | copy-start | bytes 2359300
  121.6 37.1 %collective-permute-start.21 = (bf16[5,96,2816]{2,1,0:T(8,128)(2,1)}, bf16[5,96,2816]{2,1,0:T(8,128)(2,1)}, u32[]{:S(2)}, u32[]{:S(2)}) collective-permute-start(bf16[5,96,2816]{2,1,0:T(8,128)(2,1)} %bitcast_dynamic-update-slice_fusion), channel_id=1, source_target_pairs={{0,1},{1,0},{2,3},{3,2},{4,5},{5,4},{6,7},{7,6},{8,9},{9,8},{10,11... | collective-permute-start | bytes 8110088 | tf_op jit(solution)/shard_map/ppermute | solution.py:488
  124.6 19.7 %copy-start.15 = (bf16[96,2816]{1,0:T(8,128)(2,1)}, bf16[96,2816]{1,0:T(8,128)(2,1)S(1)}, u32[]{:S(2)}) copy-start(bf16[96,2816]{1,0:T(8,128)(2,1)S(1)} %collective-permute-done.11.refs_5_) | copy-start | bytes 1622020
  124.6 11.6 %collective-permute-start.13 = (bf16[96,2816]{1,0:T(8,128)(2,1)S(1)}, bf16[96,2816]{1,0:T(8,128)(2,1)S(1)}, u32[]{:S(2)}, u32[]{:S(2)}) collective-permute-start(bf16[96,2816]{1,0:T(8,128)(2,1)S(1)} %collective-permute-done.11.refs_5_), channel_id=1, source_target_pairs={{0,4},{4,8},{8,12},{12,14},{14,10},{10,6},{6,2},{2,0},{5,1},{9,5},... | collective-permute-start | bytes 1622024 | tf_op jit(solution)/shard_map/ppermute | solution.py:48
  130.3 16.1 %copy-start.27 = (bf16[96,2816]{1,0:T(8,128)(2,1)}, bf16[96,2816]{1,0:T(8,128)(2,1)S(1)}, u32[]{:S(2)}) copy-start(bf16[96,2816]{1,0:T(8,128)(2,1)S(1)} %collective-permute-done.14.refs_13_) | copy-start | bytes 1622020
  130.4 11.7 %collective-permute-start.16 = (bf16[96,2816]{1,0:T(8,128)(2,1)S(1)}, bf16[96,2816]{1,0:T(8,128)(2,1)}, u32[]{:S(2)}, u32[]{:S(2)}) collective-permute-start(bf16[96,2816]{1,0:T(8,128)(2,1)S(1)} %collective-permute-done.14.refs_13_), channel_id=1, source_target_pairs={{0,4},{4,8},{8,12},{12,14},{14,10},{10,6},{6,2},{2,0},{5,1},{9,5},... | collective-permute-start | bytes 1622024 | tf_op jit(solution)/shard_map/ppermute | solution.py:48
  136.1 11.7 %collective-permute-start.15 = (bf16[96,2816]{1,0:T(8,128)(2,1)S(1)}, bf16[96,2816]{1,0:T(8,128)(2,1)}, u32[]{:S(2)}, u32[]{:S(2)}) collective-permute-start(bf16[96,2816]{1,0:T(8,128)(2,1)S(1)} %collective-permute-done.13.refs_6_), channel_id=1, source_target_pairs={{0,4},{4,8},{8,12},{12,14},{14,10},{10,6},{6,2},{2,0},{5,1},{9,5},... | collective-permute-start | bytes 1622024 | tf_op jit(solution)/shard_map/ppermute | solution.py:48
  142.0 11.6 %collective-permute-start.17 = (bf16[96,2816]{1,0:T(8,128)(2,1)}, bf16[96,2816]{1,0:T(8,128)(2,1)}, u32[]{:S(2)}, u32[]{:S(2)}) collective-permute-start(bf16[96,2816]{1,0:T(8,128)(2,1)} %collective-permute-done.16.refs_14_), channel_id=1, source_target_pairs={{0,4},{4,8},{8,12},{12,14},{14,10},{10,6},{6,2},{2,0},{5,1},{9,5},... | collective-permute-start | bytes 1622024 | tf_op jit(solution)/shard_map/ppermute | solution.py:48
  144.2 9.8 %collective-permute-start.19 = (bf16[2,96,2816]{2,1,0:T(8,128)(2,1)}, bf16[2,96,2816]{2,1,0:T(8,128)(2,1)}, u32[]{:S(2)}, u32[]{:S(2)}) collective-permute-start(bf16[2,96,2816]{2,1,0:T(8,128)(2,1)} %pad_maximum_fusion.1), channel_id=1, source_target_pairs={{0,1},{1,0},{2,3},{3,2},{4,5},{5,4},{6,7},{7,6},{8,9},{9,8},{10,11... | collective-permute-start | bytes 3244040 | tf_op jit(solution)/shard_map/ppermute | solution.py:488
  147.8 9.1 %collective-permute-start.22 = (bf16[2,96,2816]{2,1,0:T(8,128)(2,1)}, bf16[2,96,2816]{2,1,0:T(8,128)(2,1)}, u32[]{:S(2)}, u32[]{:S(2)}) collective-permute-start(bf16[2,96,2816]{2,1,0:T(8,128)(2,1)} %pad_maximum_fusion.2), channel_id=1, source_target_pairs={{0,1},{1,0},{2,3},{3,2},{4,5},{5,4},{6,7},{7,6},{8,9},{9,8},{10,11... | collective-permute-start | bytes 3244040 | tf_op jit(solution)/shard_map/ppermute | solution.py:488
  153.6 2.1 collective-permute-start.20
  154.0 34.6 %collective-permute-start.26 = (bf16[384,1536]{1,0:T(8,128)(2,1)}, bf16[384,1536]{1,0:T(8,128)(2,1)}, u32[]{:S(2)}, u32[]{:S(2)}) collective-permute-start(bf16[384,1536]{1,0:T(8,128)(2,1)} %collective-permute-done.25.w_first_ref), channel_id=1, source_target_pairs={{0,1},{1,0},{2,3},{3,2},{4,5},{5,4},{6,7},{7,6},{8,9},{9,8},{10,11... | collective-permute-start | bytes 3538952 | tf_op jit(solution)/shard_map/ppermute | solution.py:495
  156.6 2.1 collective-permute-start.23
  171.9 11.5 %collective-permute-start.24 = (bf16[256,768]{1,0:T(8,128)(2,1)}, bf16[256,768]{1,0:T(8,128)(2,1)}, u32[]{:S(2)}, u32[]{:S(2)}) collective-permute-start(bf16[256,768]{1,0:T(8,128)(2,1)} %get-tuple-element.52), channel_id=1, source_target_pairs={{0,16},{16,0},{1,17},{17,1},{2,18},{18,2},{3,19},{19,3},{4,20},{20... | collective-permute-start | bytes 1179656 | tf_op jit(solution)/shard_map/ppermute | solution.py:525
  187.0 16.5 %copy-start.24 = (bf16[256,1536]{1,0:T(8,128)(2,1)S(1)}, bf16[256,1536]{1,0:T(8,128)(2,1)}, u32[]{:S(2)}) copy-start(bf16[256,1536]{1,0:T(8,128)(2,1)} %copy-done.23) | copy-start | bytes 2359300
  187.0 16.4 %copy-start.29 = (bf16[256,1536]{1,0:T(8,128)(2,1)S(1)}, bf16[256,1536]{1,0:T(8,128)(2,1)}, u32[]{:S(2)}) copy-start(bf16[256,1536]{1,0:T(8,128)(2,1)} %copy-done.28) | copy-start | bytes 2359300
  187.0 18.4 %collective-permute-start.28 = (bf16[256,768]{1,0:T(8,128)(2,1)S(1)}, bf16[256,768]{1,0:T(8,128)(2,1)S(1)}, u32[]{:S(2)}, u32[]{:S(2)}) collective-permute-start(bf16[256,768]{1,0:T(8,128)(2,1)S(1)} %attention_late.1), channel_id=1, source_target_pairs={{0,16},{16,0},{1,17},{17,1},{2,18},{18,2},{3,19},{19,3},{4,20},{20... | collective-permute-start | bytes 1179656 | tf_op jit(solution)/shard_map/ppermute | solution.py:529
  202.8 19.1 %collective-permute-start.27 = (bf16[256,1536]{1,0:T(8,128)(2,1)}, bf16[256,1536]{1,0:T(8,128)(2,1)S(1)}, u32[]{:S(2)}, u32[]{:S(2)}) collective-permute-start(bf16[256,1536]{1,0:T(8,128)(2,1)} %get-tuple-element.56), channel_id=1, source_target_pairs={{0,16},{16,0},{1,17},{17,1},{2,18},{18,2},{3,19},{19,3},{4,20},{20... | collective-permute-start | bytes 2359304 | tf_op jit(solution)/shard_map/ppermute | solution.py:545
  205.4 16.6 %copy-start.32 = (f32[256,1536]{1,0:T(8,128)S(1)}, f32[256,1536]{1,0:T(8,128)}, u32[]{:S(2)}) copy-start(f32[256,1536]{1,0:T(8,128)} %get-tuple-element.55) | copy-start | bytes 4718596
  205.4 16.6 %copy-start.34 = (bf16[256,1536]{1,0:T(8,128)(2,1)S(1)}, bf16[256,1536]{1,0:T(8,128)(2,1)}, u32[]{:S(2)}) copy-start(bf16[256,1536]{1,0:T(8,128)(2,1)} %get-tuple-element.56) | copy-start | bytes 2359300
  219.5 18.9 %collective-permute-start.29 = (bf16[256,1536]{1,0:T(8,128)(2,1)}, bf16[256,1536]{1,0:T(8,128)(2,1)S(1)}, u32[]{:S(2)}, u32[]{:S(2)}) collective-permute-start(bf16[256,1536]{1,0:T(8,128)(2,1)} %get-tuple-element.62), channel_id=1, source_target_pairs={{0,16},{16,0},{1,17},{17,1},{2,18},{18,2},{3,19},{19,3},{4,20},{20... | collective-permute-start | bytes 2359304 | tf_op jit(solution)/shard_map/ppermute | solution.py:545
  221.9 16.5 %copy-start.33 = (f32[256,1536]{1,0:T(8,128)S(1)}, f32[256,1536]{1,0:T(8,128)}, u32[]{:S(2)}) copy-start(f32[256,1536]{1,0:T(8,128)} %get-tuple-element.61) | copy-start | bytes 4718596
  221.9 16.5 %copy-start.35 = (bf16[256,1536]{1,0:T(8,128)(2,1)S(1)}, bf16[256,1536]{1,0:T(8,128)(2,1)}, u32[]{:S(2)}) copy-start(bf16[256,1536]{1,0:T(8,128)(2,1)} %get-tuple-element.62) | copy-start | bytes 2359300
  (24 other events, 249.6 us)

commit v7 on v6

--- a/solution.py
+++ b/solution.py
@@ -295,9 +295,10 @@
         )
         return made
 
-    pending = copies(0)
-    for copy in pending:
-        copy.start()
+    pending = [copies(j) for j in range(min(2, steps))]
+    for made in pending:
+        for copy in made:
+            copy.start()
     depth = w_first_ref.shape[0]
     core = side_ref[0]
     first = pl.ds(pl.multiple_of(core * depth, LANES), depth)
@@ -311,12 +312,8 @@
     scale = lax.rsqrt(jnp.mean(x * x, axis=-1, keepdims=True) + norm_eps)
     normed[...] = (x * scale * gain_ref[...]).astype(BF)
     for j in range(steps):
-        current, slot = pending, j % 2
-        if j + 1 < steps:
-            pending = copies(j + 1)
-            for copy in pending:
-                copy.start()
-        for copy in current:
+        slot = j % 2
+        for copy in pending[j]:
             copy.wait()
         gate = jnp.dot(normed[...], buf[slot, 0].reshape(width, wide), preferred_element_type=F32)
         up = jnp.dot(normed[...], buf[slot, 1].reshape(width, wide), preferred_element_type=F32)
@@ -328,6 +325,10 @@
             total[...] += term
         else:
             part_ref[...] = (total[...] + term).astype(BF)
+        if j + 2 < steps:
+            pending.append(copies(j + 2))
+            for copy in pending[-1]:
+                copy.start()
 
 
 def ffn_part(spots, side, base, other, w_first, w_second, gain, down, blocks, first_col):

time: 241 us -> 240 us (level)
  no operation moved by 1% of the time
where the time goes in v7:
time: 240 us; the launch traced here: 239 us
  waiting for transfers between devices  96.5 us (40%)
  starting transfers between devices  54.6 us (23%)
  Pallas kernels  42.6 us (18%)
  matrix products  14.7 us (6%)
  other arithmetic  14.3 us (6%)
  local copies, waits for them, and re-layouts  13.6 us (6%)
  between operations  3 us (1%)
    ppermute x14, waiting for transfers between devices, ring_more(): blocks.append(lax.ppermute(last, 'req', pairs))  50.6 us
    ppermute x14, starting transfers between devices, ring_more(): blocks.append(lax.ppermute(last, 'req', pairs))  31 us
    pallas_call x2, Pallas kernels, ffn_part(): pl.pallas_call(functools.partial(ffn_kernel, len(blocks), first_col), out...  26.7 us
    ppermute x2, waiting for transfers between devices, per_device(): total = part.astype(F32) + lax.ppermute(part, 'tp', PAIR).astype(F32)  17.8 us
    ppermute x1, waiting for transfers between devices, per_device(): came = lax.ppermute(away, 'tp', PAIR)  12.9 us
    pallas_call x1, Pallas kernels, attention_early(): pl.pallas_call(functools.partial(project_kernel, q_heads, kv_heads, len(b...  12.4 us
    unnamed x86, local copies, waits for them, and re-layouts  8.53 us
    dot_general x1, matrix products, per_device(): jnp.dot(pick_rows, embed_table, preferred_element_type=F32).astype(BF)  7.37 us
  transfers between devices with their start and end apart: 32, of which 21 were waited for; matrix products, arithmetic and copies ran while one was open for 12% of the time, Pallas kernels for 18%

profile of v7, /device:TPU:0, one launch (start us, length us, event | category | flops | bytes accessed | tf_op | source)
XLA Modules:
  0.0 239.2 jit_solution(6468169083429978451)
XLA Ops:
  2.6 7.4 %all-to-all-start = ((s32[16,1,32]{2,1,0:T(1,128)}), s32[16,1,32]{2,1,0:T(1,128)S(1)}, u32[]{:S(2)}, u32[]{:S(2)}) async-start(s32[16,1,32]{2,1,0:T(1,128)} %sub.101), calls=%async_computation | async-start | bytes 16384 | tf_op jit(solution)/shard_map/all_to_all | solution.py:409
  12.1 4.2 %all-to-all-done = s32[16,1,32]{2,1,0:T(1,128)S(1)} async-done(((s32[16,1,32]{2,1,0:T(1,128)}), s32[16,1,32]{2,1,0:T(1,128)S(1)}, u32[]{:S(2)}, u32[]{:S(2)}) %all-to-all-start) | async-done | bytes 2080 | tf_op jit(solution)/shard_map/all_to_all | solution.py:409
  17.6 7.4 %fusion.1 = bf16[512,1536]{1,0:T(8,128)(2,1)} fusion(bf16[2000,1536]{1,0:T(8,128)(2,1)} %param.13, s32[512]{0:T(512)S(1)} %eq.123), kind=kOutput, calls=%fused_computation.2 | convolution fusion | flops 3147538432 | bytes 7718912 | tf_op jit(solution)/shard_map/dot_general | solution.py:414
  25.0 4.5 %all-to-all-start.1 = ((bf16[16,32,1536]{2,1,0:T(8,128)(2,1)}), bf16[16,32,1536]{2,1,0:T(8,128)(2,1)}, u32[]{:S(2)}, u32[]{:S(2)}) async-start(bf16[16,32,1536]{2,1,0:T(8,128)(2,1)} %bitcast.57), calls=%async_computation.1 | async-start | bytes 3145728 | tf_op jit(solution)/shard_map/all_to_all | solution.py:415
  32.6 4.0 %fusion.3 = (f32[512,384]{1,0:T(8,128)}, f32[512,384]{1,0:T(8,128)}, f32[512,384]{1,0:T(8,128)}) fusion(f32[384]{0:T(512)S(1)} %fusion.14, f32[512]{0:T(512)S(1)} %select_convert_fusion, pred[384]{0:T(512)(128)(4,1)S(1)} %fusion.18), kind=kLoop, calls=%fused_computation.12 | loop fusion | flops 786432 | bytes 2363264 | tf_op jit(solution)/shard_map/jit(_where)/select_n | solution.py:430
  37.1 1.6 collective-permute-start.2
  38.7 12.9 %collective-permute-done.2 = bf16[2,48,2816]{2,1,0:T(8,128)(2,1)S(1)} collective-permute-done((bf16[2,48,2816]{2,1,0:T(8,128)(2,1)S(1)}, bf16[2,48,2816]{2,1,0:T(8,128)(2,1)S(1)}, u32[]{:S(2)}, u32[]{:S(2)}) %collective-permute-start.2) | collective-permute-done | bytes 540704 | tf_op jit(solution)/shard_map/ppermute | solution.py:456
  51.8 1.5 collective-permute-done.3
  53.3 1.8 collective-permute-start.4
  55.2 1.5 collective-permute-start.6
  57.5 1.5 collective-permute-start.25
  59.9 7.1 %collective-permute-done.4.refs_1_ = bf16[96,2816]{1,0:T(8,128)(2,1)S(1)} collective-permute-done((bf16[96,2816]{1,0:T(8,128)(2,1)S(1)}, bf16[96,2816]{1,0:T(8,128)(2,1)S(1)}, u32[]{:S(2)}, u32[]{:S(2)}) %collective-permute-start.4) | collective-permute-done | bytes 540704 | tf_op jit(solution)/shard_map/ppermute | solution.py:48
  67.0 4.7 %collective-permute-start.5 = (bf16[96,2816]{1,0:T(8,128)(2,1)S(1)}, bf16[96,2816]{1,0:T(8,128)(2,1)S(1)}, u32[]{:S(2)}, u32[]{:S(2)}) collective-permute-start(bf16[96,2816]{1,0:T(8,128)(2,1)S(1)} %collective-permute-done.4.refs_1_), channel_id=1, source_target_pairs={{0,4},{4,8},{8,12},{12,14},{14,10},{10,6},{6,2},{2,0},{5,1},{9,5},... | collective-permute-start | bytes 1622024 | tf_op jit(solution)/shard_map/ppermute | solution.py:48
  72.8 4.7 %collective-permute-start.8 = (bf16[96,2816]{1,0:T(8,128)(2,1)S(1)}, bf16[96,2816]{1,0:T(8,128)(2,1)S(1)}, u32[]{:S(2)}, u32[]{:S(2)}) collective-permute-start(bf16[96,2816]{1,0:T(8,128)(2,1)S(1)} %collective-permute-done.6.refs_9_), channel_id=1, source_target_pairs={{0,4},{4,8},{8,12},{12,14},{14,10},{10,6},{6,2},{2,0},{5,1},{9,5},... | collective-permute-start | bytes 1622024 | tf_op jit(solution)/shard_map/ppermute | solution.py:48
  79.1 5.2 %collective-permute-done.8.refs_10_ = bf16[96,2816]{1,0:T(8,128)(2,1)S(1)} collective-permute-done((bf16[96,2816]{1,0:T(8,128)(2,1)S(1)}, bf16[96,2816]{1,0:T(8,128)(2,1)S(1)}, u32[]{:S(2)}, u32[]{:S(2)}) %collective-permute-start.8) | collective-permute-done | bytes 540704 | tf_op jit(solution)/shard_map/ppermute | solution.py:48
  84.3 4.7 %collective-permute-start.10 = (bf16[96,2816]{1,0:T(8,128)(2,1)S(1)}, bf16[96,2816]{1,0:T(8,128)(2,1)}, u32[]{:S(2)}, u32[]{:S(2)}) collective-permute-start(bf16[96,2816]{1,0:T(8,128)(2,1)S(1)} %collective-permute-done.8.refs_10_), channel_id=1, source_target_pairs={{0,4},{4,8},{8,12},{12,14},{14,10},{10,6},{6,2},{2,0},{5,1},{9,5},... | collective-permute-start | bytes 1622024 | tf_op jit(solution)/shard_map/ppermute | solution.py:48
  90.8 2.0 convolution_convert_fusion.own_ref
  92.8 2.5 %collective-permute-start.7 = (bf16[96,2816]{1,0:T(8,128)(2,1)S(1)}, bf16[96,2816]{1,0:T(8,128)(2,1)S(1)}, u32[]{:S(2)}, u32[]{:S(2)}) collective-permute-start(bf16[96,2816]{1,0:T(8,128)(2,1)S(1)} %collective-permute-done.5.refs_2_), channel_id=1, source_target_pairs={{0,4},{4,8},{8,12},{12,14},{14,10},{10,6},{6,2},{2,0},{5,1},{9,5},... | collective-permute-start | bytes 1622024 | tf_op jit(solution)/shard_map/ppermute | solution.py:48
  95.9 1.9 bitcast_dynamic-update-slice_fusion.1
  97.8 1.5 collective-permute-start
  99.3 2.9 %collective-permute-done.7.refs_3_ = bf16[96,2816]{1,0:T(8,128)(2,1)S(1)} collective-permute-done((bf16[96,2816]{1,0:T(8,128)(2,1)S(1)}, bf16[96,2816]{1,0:T(8,128)(2,1)S(1)}, u32[]{:S(2)}, u32[]{:S(2)}) %collective-permute-start.7) | collective-permute-done | bytes 540704 | tf_op jit(solution)/shard_map/ppermute | solution.py:48
  102.2 2.5 %collective-permute-start.9 = (bf16[96,2816]{1,0:T(8,128)(2,1)S(1)}, bf16[96,2816]{1,0:T(8,128)(2,1)S(1)}, u32[]{:S(2)}, u32[]{:S(2)}) collective-permute-start(bf16[96,2816]{1,0:T(8,128)(2,1)S(1)} %collective-permute-done.7.refs_3_), channel_id=1, source_target_pairs={{0,4},{4,8},{8,12},{12,14},{14,10},{10,6},{6,2},{2,0},{5,1},{9,5},... | collective-permute-start | bytes 1622024 | tf_op jit(solution)/shard_map/ppermute | solution.py:48
  104.7 2.0 collective-permute-start.12
  107.6 5.4 %collective-permute-done.9.refs_4_ = bf16[96,2816]{1,0:T(8,128)(2,1)S(1)} collective-permute-done((bf16[96,2816]{1,0:T(8,128)(2,1)S(1)}, bf16[96,2816]{1,0:T(8,128)(2,1)S(1)}, u32[]{:S(2)}, u32[]{:S(2)}) %collective-permute-start.9) | collective-permute-done | bytes 540704 | tf_op jit(solution)/shard_map/ppermute | solution.py:48
  114.1 4.7 %collective-permute-done.12.refs_12_ = bf16[96,2816]{1,0:T(8,128)(2,1)S(1)} collective-permute-done((bf16[96,2816]{1,0:T(8,128)(2,1)}, bf16[96,2816]{1,0:T(8,128)(2,1)S(1)}, u32[]{:S(2)}, u32[]{:S(2)}) %collective-permute-start.12) | collective-permute-done | bytes 540704 | tf_op jit(solution)/shard_map/ppermute | solution.py:48
  122.2 2.4 collective-permute-done.11.refs_5_
  125.7 4.7 %collective-permute-done.14.refs_13_ = bf16[96,2816]{1,0:T(8,128)(2,1)S(1)} collective-permute-done((bf16[96,2816]{1,0:T(8,128)(2,1)S(1)}, bf16[96,2816]{1,0:T(8,128)(2,1)S(1)}, u32[]{:S(2)}, u32[]{:S(2)}) %collective-permute-start.14) | collective-permute-done | bytes 540704 | tf_op jit(solution)/shard_map/ppermute | solution.py:48
  131.5 4.7 %collective-permute-done.13.refs_6_ = bf16[96,2816]{1,0:T(8,128)(2,1)S(1)} collective-permute-done((bf16[96,2816]{1,0:T(8,128)(2,1)S(1)}, bf16[96,2816]{1,0:T(8,128)(2,1)S(1)}, u32[]{:S(2)}, u32[]{:S(2)}) %collective-permute-start.13) | collective-permute-done | bytes 540704 | tf_op jit(solution)/shard_map/ppermute | solution.py:48
  137.3 4.8 %collective-permute-done.16.refs_14_ = bf16[96,2816]{1,0:T(8,128)(2,1)} collective-permute-done((bf16[96,2816]{1,0:T(8,128)(2,1)S(1)}, bf16[96,2816]{1,0:T(8,128)(2,1)}, u32[]{:S(2)}, u32[]{:S(2)}) %collective-permute-start.16) | collective-permute-done | bytes 540704 | tf_op jit(solution)/shard_map/ppermute | solution.py:48
  142.0 1.1 collective-permute-start.17
  144.3 2.1 pad_maximum_fusion.2
  146.5 1.4 collective-permute-done.15.refs_7_
  147.8 5.8 %collective-permute-done.17.refs_15_ = bf16[96,2816]{1,0:T(8,128)(2,1)} collective-permute-done((bf16[96,2816]{1,0:T(8,128)(2,1)}, bf16[96,2816]{1,0:T(8,128)(2,1)}, u32[]{:S(2)}, u32[]{:S(2)}) %collective-permute-start.17) | collective-permute-done | bytes 540704 | tf_op jit(solution)/shard_map/ppermute | solution.py:48
  154.6 1.2 collective-permute-done.20.refs_18_
  157.0 1.7 collective-permute-done.23.refs_21_
  159.5 12.4 %attention_early.1 = (bf16[256,768]{1,0:T(8,128)(2,1)}, bf16[2,512,384]{2,1,0:T(8,128)(2,1)}, bf16[256,1024]{1,0:T(8,128)(2,1)S(1)}, bf16[512,512]{1,0:T(8,128)(2,1)}, bf16[512,512]{1,0:T(8,128)(2,1)}) custom-call(s32[2,32]{1,0:T(2,128)S(1)} %pad_add_fusion.spots_ref, s32[4]{0:T(128)S(1)} %bitcast.52, s32[4]{0:T(128)S(1)} %bitcast.54, s32[1]{0:T(128)} %bitcast.7.half_ref, ...), custom_call_target="tpu_custom_call" | custom-call | flops 2415919104 | bytes 9437184 | tf_op jit(solution)/shard_map/attention_early/pallas_call | solution.py:216
  171.9 1.6 collective-permute-start.24
  173.6 3.3 %convolution_add_fusion.1.base_ref = f32[256,1536]{1,0:T(8,128)} fusion(bf16[256,768]{1,0:T(8,128)(2,1)} %get-tuple-element.52, bf16[768,1536]{1,0:T(8,128)(2,1)S(1)} %copy-done, bf16[256,1536]{1,0:T(8,128)(2,1)} %copy-done.23, bf16[256,1536]{1,0:T(8,128)(2,1)} %copy-done.28, pred[]{:T(512)S(6)} %eq.113), kind=kOutput, calls=%fused_computation.4 | convolution fusion | flops 605159424 | bytes 5898241 | tf_op jit(solution)/shard_map/dot_general | solution.py:537
  176.9 6.5 %collective-permute-done.24.other_ref = bf16[256,768]{1,0:T(8,128)(2,1)} collective-permute-done((bf16[256,768]{1,0:T(8,128)(2,1)}, bf16[256,768]{1,0:T(8,128)(2,1)}, u32[]{:S(2)}, u32[]{:S(2)}) %collective-permute-start.24) | collective-permute-done | bytes 393248 | tf_op jit(solution)/shard_map/ppermute | solution.py:526
  183.5 3.5 %attention_late.1 = bf16[256,768]{1,0:T(8,128)(2,1)S(1)} custom-call(s32[4]{0:T(128)S(1)} %bitcast.53, s32[4]{0:T(128)S(1)} %bitcast.55, bf16[256,1024]{1,0:T(8,128)(2,1)S(1)} %get-tuple-element.58.q_ref, bf16[512,512]{1,0:T(8,128)(2,1)S(1)} %copy-done.19, bf16[512,512]{1,0:T(8,128)(2,1)S(1)} %copy-done.20, bf16[512,384]{1,0:T(8,128)(2,1)S(1)} %fusion.7.pack_ref), custom_call_target="tpu_custom_call" | custom-call | flops 536870912 | bytes 2097152 | tf_op jit(solution)/shard_map/attention_late/pallas_call | solution.py:248
  187.0 1.6 collective-permute-start.28
  188.7 13.4 %ffn_part.2 = (f32[256,1536]{1,0:T(8,128)}, bf16[256,1536]{1,0:T(8,128)(2,1)}) custom-call(s32[2,32]{1,0:T(2,128)S(1)} %pad_add_fusion.spots_ref, s32[1]{0:T(128)} %bitcast.side_ref, f32[256,1536]{1,0:T(8,128)} %convolution_add_fusion.1.base_ref, bf16[256,768]{1,0:T(8,128)(2,1)} %collective-permute-done.24.other_ref, ...), custom_call_target="tpu_custom_call" | custom-call | flops 5435817984 | bytes 21233664 | tf_op jit(solution)/shard_map/ffn_part/pallas_call | solution.py:340
  202.6 1.9 convolution_add_fusion.base_ref
  204.6 13.4 %ffn_part.3 = (f32[256,1536]{1,0:T(8,128)}, bf16[256,1536]{1,0:T(8,128)(2,1)}) custom-call(s32[2,32]{1,0:T(2,128)S(1)} %pad_add_fusion.spots_ref, s32[1]{0:T(128)} %bitcast.side_ref, f32[256,1536]{1,0:T(8,128)} %convolution_add_fusion.base_ref, bf16[256,768]{1,0:T(8,128)(2,1)S(1)} %collective-permute-done.28.other_ref, ...), custom_call_target="tpu_custom_call" | custom-call | flops 5435817984 | bytes 21233664 | tf_op jit(solution)/shard_map/ffn_part/pallas_call | solution.py:340
  217.9 1.6 collective-permute-start.29
  219.5 2.4 %collective-permute-done.27 = bf16[256,1536]{1,0:T(8,128)(2,1)S(1)} collective-permute-done((bf16[256,1536]{1,0:T(8,128)(2,1)}, bf16[256,1536]{1,0:T(8,128)(2,1)S(1)}, u32[]{:S(2)}, u32[]{:S(2)}) %collective-permute-start.27) | collective-permute-done | bytes 786464 | tf_op jit(solution)/shard_map/ppermute | solution.py:546
  222.2 15.4 %collective-permute-done.29 = bf16[256,1536]{1,0:T(8,128)(2,1)S(1)} collective-permute-done((bf16[256,1536]{1,0:T(8,128)(2,1)}, bf16[256,1536]{1,0:T(8,128)(2,1)S(1)}, u32[]{:S(2)}, u32[]{:S(2)}) %collective-permute-start.29) | collective-permute-done | bytes 786464 | tf_op jit(solution)/shard_map/ppermute | solution.py:546
  238.0 1.2 pad_maximum_fusion
  (158 shorter events, 28.1 us)
Async XLA Ops:
  2.6 13.7 %all-to-all-start = ((s32[16,1,32]{2,1,0:T(1,128)}), s32[16,1,32]{2,1,0:T(1,128)S(1)}, u32[]{:S(2)}, u32[]{:S(2)}) async-start(s32[16,1,32]{2,1,0:T(1,128)} %sub.101), calls=%async_computation | async-start | bytes 16384 | tf_op jit(solution)/shard_map/all_to_all | solution.py:409
  25.0 65.8 %all-to-all-start.1 = ((bf16[16,32,1536]{2,1,0:T(8,128)(2,1)}), bf16[16,32,1536]{2,1,0:T(8,128)(2,1)}, u32[]{:S(2)}, u32[]{:S(2)}) async-start(bf16[16,32,1536]{2,1,0:T(8,128)(2,1)} %bitcast.57), calls=%async_computation.1 | async-start | bytes 3145728 | tf_op jit(solution)/shard_map/all_to_all | solution.py:415
  36.7 1.9 collective-permute-start.1
  37.1 14.5 %collective-permute-start.2 = (bf16[2,48,2816]{2,1,0:T(8,128)(2,1)S(1)}, bf16[2,48,2816]{2,1,0:T(8,128)(2,1)S(1)}, u32[]{:S(2)}, u32[]{:S(2)}) collective-permute-start(bf16[2,48,2816]{2,1,0:T(8,128)(2,1)S(1)} %pad_maximum_fusion.4), channel_id=1, source_target_pairs={{0,16},{16,0},{1,17},{17,1},{2,18},{18,2},{3,19},{19,3},{4,20},{20... | collective-permute-start | bytes 1622024 | tf_op jit(solution)/shard_map/ppermute | solution.py:456
  51.6 1.6 collective-permute-start.3
  53.3 25.0 %copy-start.3 = (bf16[96,2816]{1,0:T(8,128)(2,1)}, bf16[96,2816]{1,0:T(8,128)(2,1)S(1)}, u32[]{:S(2)}) copy-start(bf16[96,2816]{1,0:T(8,128)(2,1)S(1)} %pad_maximum_fusion.5.refs_8_) | copy-start | bytes 1622020
  53.3 13.6 %collective-permute-start.4 = (bf16[96,2816]{1,0:T(8,128)(2,1)S(1)}, bf16[96,2816]{1,0:T(8,128)(2,1)S(1)}, u32[]{:S(2)}, u32[]{:S(2)}) collective-permute-start(bf16[96,2816]{1,0:T(8,128)(2,1)S(1)} %pad_maximum_fusion.3.refs_0_), channel_id=1, source_target_pairs={{0,4},{4,8},{8,12},{12,14},{14,10},{10,6},{6,2},{2,0},{5,1},{9,5},... | collective-permute-start | bytes 1622024 | tf_op jit(solution)/shard_map/ppermute | solution.py:48
  55.2 17.6 %collective-permute-start.6 = (bf16[96,2816]{1,0:T(8,128)(2,1)S(1)}, bf16[96,2816]{1,0:T(8,128)(2,1)S(1)}, u32[]{:S(2)}, u32[]{:S(2)}) collective-permute-start(bf16[96,2816]{1,0:T(8,128)(2,1)S(1)} %pad_maximum_fusion.5.refs_8_), channel_id=1, source_target_pairs={{0,4},{4,8},{8,12},{12,14},{14,10},{10,6},{6,2},{2,0},{5,1},{9,5},... | collective-permute-start | bytes 1622024 | tf_op jit(solution)/shard_map/ppermute | solution.py:48
  57.5 86.7 %collective-permute-start.25 = (bf16[384,1536]{1,0:T(8,128)(2,1)}, bf16[384,1536]{1,0:T(8,128)(2,1)}, u32[]{:S(2)}, u32[]{:S(2)}) collective-permute-start(bf16[384,1536]{1,0:T(8,128)(2,1)} %constant_dynamic-slice_fusion), channel_id=1, source_target_pairs={{0,16},{16,0},{1,17},{17,1},{2,18},{18,2},{3,19},{19,3},{4,20},{20... | collective-permute-start | bytes 3538952 | tf_op jit(solution)/shard_map/ppermute | solution.py:484
  67.0 22.9 %copy-start.5 = (bf16[96,2816]{1,0:T(8,128)(2,1)}, bf16[96,2816]{1,0:T(8,128)(2,1)S(1)}, u32[]{:S(2)}) copy-start(bf16[96,2816]{1,0:T(8,128)(2,1)S(1)} %collective-permute-done.4.refs_1_) | copy-start | bytes 1622020
  67.0 12.2 %collective-permute-start.5 = (bf16[96,2816]{1,0:T(8,128)(2,1)S(1)}, bf16[96,2816]{1,0:T(8,128)(2,1)S(1)}, u32[]{:S(2)}, u32[]{:S(2)}) collective-permute-start(bf16[96,2816]{1,0:T(8,128)(2,1)S(1)} %collective-permute-done.4.refs_1_), channel_id=1, source_target_pairs={{0,4},{4,8},{8,12},{12,14},{14,10},{10,6},{6,2},{2,0},{5,1},{9,5},... | collective-permute-start | bytes 1622024 | tf_op jit(solution)/shard_map/ppermute | solution.py:48
  72.8 17.1 %copy-start.7 = (bf16[96,2816]{1,0:T(8,128)(2,1)}, bf16[96,2816]{1,0:T(8,128)(2,1)S(1)}, u32[]{:S(2)}) copy-start(bf16[96,2816]{1,0:T(8,128)(2,1)S(1)} %collective-permute-done.6.refs_9_) | copy-start | bytes 1622020
  72.8 11.6 %collective-permute-start.8 = (bf16[96,2816]{1,0:T(8,128)(2,1)S(1)}, bf16[96,2816]{1,0:T(8,128)(2,1)S(1)}, u32[]{:S(2)}, u32[]{:S(2)}) collective-permute-start(bf16[96,2816]{1,0:T(8,128)(2,1)S(1)} %collective-permute-done.6.refs_9_), channel_id=1, source_target_pairs={{0,4},{4,8},{8,12},{12,14},{14,10},{10,6},{6,2},{2,0},{5,1},{9,5},... | collective-permute-start | bytes 1622024 | tf_op jit(solution)/shard_map/ppermute | solution.py:48
  84.3 11.6 %collective-permute-start.10 = (bf16[96,2816]{1,0:T(8,128)(2,1)S(1)}, bf16[96,2816]{1,0:T(8,128)(2,1)}, u32[]{:S(2)}, u32[]{:S(2)}) collective-permute-start(bf16[96,2816]{1,0:T(8,128)(2,1)S(1)} %collective-permute-done.8.refs_10_), channel_id=1, source_target_pairs={{0,4},{4,8},{8,12},{12,14},{14,10},{10,6},{6,2},{2,0},{5,1},{9,5},... | collective-permute-start | bytes 1622024 | tf_op jit(solution)/shard_map/ppermute | solution.py:48
  92.8 28.0 %copy-start.23 = (bf16[256,1536]{1,0:T(8,128)(2,1)}, bf16[256,1536]{1,0:T(8,128)(2,1)S(1)}, u32[]{:S(2)}) copy-start(bf16[256,1536]{1,0:T(8,128)(2,1)S(1)} %convolution_convert_fusion.own_ref) | copy-start | bytes 2359300
  92.8 9.4 %collective-permute-start.7 = (bf16[96,2816]{1,0:T(8,128)(2,1)S(1)}, bf16[96,2816]{1,0:T(8,128)(2,1)S(1)}, u32[]{:S(2)}, u32[]{:S(2)}) collective-permute-start(bf16[96,2816]{1,0:T(8,128)(2,1)S(1)} %collective-permute-done.5.refs_2_), channel_id=1, source_target_pairs={{0,4},{4,8},{8,12},{12,14},{14,10},{10,6},{6,2},{2,0},{5,1},{9,5},... | collective-permute-start | bytes 1622024 | tf_op jit(solution)/shard_map/ppermute | solution.py:48
  97.8 23.8 %collective-permute-start = (bf16[256,1536]{1,0:T(8,128)(2,1)S(1)}, bf16[256,1536]{1,0:T(8,128)(2,1)S(1)}, u32[]{:S(2)}, u32[]{:S(2)}) collective-permute-start(bf16[256,1536]{1,0:T(8,128)(2,1)S(1)} %convolution_convert_fusion.own_ref), channel_id=1, source_target_pairs={{0,16},{16,0},{1,17},{17,1},{2,18},{18,2},{3,19},{19,3},{4,20},{20... | collective-permute-start | bytes 2359304 | tf_op jit(solution)/shard_map/ppermute | solution.py:481
  102.2 19.4 %copy-start.11 = (bf16[96,2816]{1,0:T(8,128)(2,1)}, bf16[96,2816]{1,0:T(8,128)(2,1)S(1)}, u32[]{:S(2)}) copy-start(bf16[96,2816]{1,0:T(8,128)(2,1)S(1)} %collective-permute-done.7.refs_3_) | copy-start | bytes 1622020
  102.2 10.7 %collective-permute-start.9 = (bf16[96,2816]{1,0:T(8,128)(2,1)S(1)}, bf16[96,2816]{1,0:T(8,128)(2,1)S(1)}, u32[]{:S(2)}, u32[]{:S(2)}) collective-permute-start(bf16[96,2816]{1,0:T(8,128)(2,1)S(1)} %collective-permute-done.7.refs_3_), channel_id=1, source_target_pairs={{0,4},{4,8},{8,12},{12,14},{14,10},{10,6},{6,2},{2,0},{5,1},{9,5},... | collective-permute-start | bytes 1622024 | tf_op jit(solution)/shard_map/ppermute | solution.py:48
  104.7 14.0 %collective-permute-start.12 = (bf16[96,2816]{1,0:T(8,128)(2,1)}, bf16[96,2816]{1,0:T(8,128)(2,1)S(1)}, u32[]{:S(2)}, u32[]{:S(2)}) collective-permute-start(bf16[96,2816]{1,0:T(8,128)(2,1)} %collective-permute-done.10.refs_11_), channel_id=1, source_target_pairs={{0,4},{4,8},{8,12},{12,14},{14,10},{10,6},{6,2},{2,0},{5,1},{9,5},... | collective-permute-start | bytes 1622024 | tf_op jit(solution)/shard_map/ppermute | solution.py:48
  113.0 31.3 %copy-start.13 = (bf16[96,2816]{1,0:T(8,128)(2,1)}, bf16[96,2816]{1,0:T(8,128)(2,1)S(1)}, u32[]{:S(2)}) copy-start(bf16[96,2816]{1,0:T(8,128)(2,1)S(1)} %collective-permute-done.9.refs_4_) | copy-start | bytes 1622020
  113.0 11.6 %collective-permute-start.11 = (bf16[96,2816]{1,0:T(8,128)(2,1)S(1)}, bf16[96,2816]{1,0:T(8,128)(2,1)S(1)}, u32[]{:S(2)}, u32[]{:S(2)}) collective-permute-start(bf16[96,2816]{1,0:T(8,128)(2,1)S(1)} %collective-permute-done.9.refs_4_), channel_id=1, source_target_pairs={{0,4},{4,8},{8,12},{12,14},{14,10},{10,6},{6,2},{2,0},{5,1},{9,5},... | collective-permute-start | bytes 1622024 | tf_op jit(solution)/shard_map/ppermute | solution.py:48
  118.8 17.4 %copy-start.26 = (bf16[96,2816]{1,0:T(8,128)(2,1)}, bf16[96,2816]{1,0:T(8,128)(2,1)S(1)}, u32[]{:S(2)}) copy-start(bf16[96,2816]{1,0:T(8,128)(2,1)S(1)} %collective-permute-done.12.refs_12_) | copy-start | bytes 1622020
  118.8 11.6 %collective-permute-start.14 = (bf16[96,2816]{1,0:T(8,128)(2,1)S(1)}, bf16[96,2816]{1,0:T(8,128)(2,1)S(1)}, u32[]{:S(2)}, u32[]{:S(2)}) collective-permute-start(bf16[96,2816]{1,0:T(8,128)(2,1)S(1)} %collective-permute-done.12.refs_12_), channel_id=1, source_target_pairs={{0,4},{4,8},{8,12},{12,14},{14,10},{10,6},{6,2},{2,0},{5,1},{9,5},... | collective-permute-start | bytes 1622024 | tf_op jit(solution)/shard_map/ppermute | solution.py:48
  120.8 37.9 %collective-permute-start.18 = (bf16[5,96,2816]{2,1,0:T(8,128)(2,1)}, bf16[5,96,2816]{2,1,0:T(8,128)(2,1)}, u32[]{:S(2)}, u32[]{:S(2)}) collective-permute-start(bf16[5,96,2816]{2,1,0:T(8,128)(2,1)} %bitcast_dynamic-update-slice_fusion.5), channel_id=1, source_target_pairs={{0,1},{1,0},{2,3},{3,2},{4,5},{5,4},{6,7},{7,6},{8,9},{9,8},{10,11... | collective-permute-start | bytes 8110088 | tf_op jit(solution)/shard_map/ppermute | solution.py:489
  121.6 20.4 %copy-start.28 = (bf16[256,1536]{1,0:T(8,128)(2,1)}, bf16[256,1536]{1,0:T(8,128)(2,1)S(1)}, u32[]{:S(2)}) copy-start(bf16[256,1536]{1,0:T(8,128)(2,1)S(1)} %collective-permute-done.other_ref) | copy-start | bytes 2359300
  121.6 37.1 %collective-permute-start.21 = (bf16[5,96,2816]{2,1,0:T(8,128)(2,1)}, bf16[5,96,2816]{2,1,0:T(8,128)(2,1)}, u32[]{:S(2)}, u32[]{:S(2)}) collective-permute-start(bf16[5,96,2816]{2,1,0:T(8,128)(2,1)} %bitcast_dynamic-update-slice_fusion), channel_id=1, source_target_pairs={{0,1},{1,0},{2,3},{3,2},{4,5},{5,4},{6,7},{7,6},{8,9},{9,8},{10,11... | collective-permute-start | bytes 8110088 | tf_op jit(solution)/shard_map/ppermute | solution.py:489
  124.6 19.7 %copy-start.15 = (bf16[96,2816]{1,0:T(8,128)(2,1)}, bf16[96,2816]{1,0:T(8,128)(2,1)S(1)}, u32[]{:S(2)}) copy-start(bf16[96,2816]{1,0:T(8,128)(2,1)S(1)} %collective-permute-done.11.refs_5_) | copy-start | bytes 1622020
  124.6 11.6 %collective-permute-start.13 = (bf16[96,2816]{1,0:T(8,128)(2,1)S(1)}, bf16[96,2816]{1,0:T(8,128)(2,1)S(1)}, u32[]{:S(2)}, u32[]{:S(2)}) collective-permute-start(bf16[96,2816]{1,0:T(8,128)(2,1)S(1)} %collective-permute-done.11.refs_5_), channel_id=1, source_target_pairs={{0,4},{4,8},{8,12},{12,14},{14,10},{10,6},{6,2},{2,0},{5,1},{9,5},... | collective-permute-start | bytes 1622024 | tf_op jit(solution)/shard_map/ppermute | solution.py:48
  130.3 16.1 %copy-start.27 = (bf16[96,2816]{1,0:T(8,128)(2,1)}, bf16[96,2816]{1,0:T(8,128)(2,1)S(1)}, u32[]{:S(2)}) copy-start(bf16[96,2816]{1,0:T(8,128)(2,1)S(1)} %collective-permute-done.14.refs_13_) | copy-start | bytes 1622020
  130.4 11.7 %collective-permute-start.16 = (bf16[96,2816]{1,0:T(8,128)(2,1)S(1)}, bf16[96,2816]{1,0:T(8,128)(2,1)}, u32[]{:S(2)}, u32[]{:S(2)}) collective-permute-start(bf16[96,2816]{1,0:T(8,128)(2,1)S(1)} %collective-permute-done.14.refs_13_), channel_id=1, source_target_pairs={{0,4},{4,8},{8,12},{12,14},{14,10},{10,6},{6,2},{2,0},{5,1},{9,5},... | collective-permute-start | bytes 1622024 | tf_op jit(solution)/shard_map/ppermute | solution.py:48
  136.1 11.7 %collective-permute-start.15 = (bf16[96,2816]{1,0:T(8,128)(2,1)S(1)}, bf16[96,2816]{1,0:T(8,128)(2,1)}, u32[]{:S(2)}, u32[]{:S(2)}) collective-permute-start(bf16[96,2816]{1,0:T(8,128)(2,1)S(1)} %collective-permute-done.13.refs_6_), channel_id=1, source_target_pairs={{0,4},{4,8},{8,12},{12,14},{14,10},{10,6},{6,2},{2,0},{5,1},{9,5},... | collective-permute-start | bytes 1622024 | tf_op jit(solution)/shard_map/ppermute | solution.py:48
  142.0 11.6 %collective-permute-start.17 = (bf16[96,2816]{1,0:T(8,128)(2,1)}, bf16[96,2816]{1,0:T(8,128)(2,1)}, u32[]{:S(2)}, u32[]{:S(2)}) collective-permute-start(bf16[96,2816]{1,0:T(8,128)(2,1)} %collective-permute-done.16.refs_14_), channel_id=1, source_target_pairs={{0,4},{4,8},{8,12},{12,14},{14,10},{10,6},{6,2},{2,0},{5,1},{9,5},... | collective-permute-start | bytes 1622024 | tf_op jit(solution)/shard_map/ppermute | solution.py:48
  144.2 9.8 %collective-permute-start.19 = (bf16[2,96,2816]{2,1,0:T(8,128)(2,1)}, bf16[2,96,2816]{2,1,0:T(8,128)(2,1)}, u32[]{:S(2)}, u32[]{:S(2)}) collective-permute-start(bf16[2,96,2816]{2,1,0:T(8,128)(2,1)} %pad_maximum_fusion.1), channel_id=1, source_target_pairs={{0,1},{1,0},{2,3},{3,2},{4,5},{5,4},{6,7},{7,6},{8,9},{9,8},{10,11... | collective-permute-start | bytes 3244040 | tf_op jit(solution)/shard_map/ppermute | solution.py:489
  147.8 9.1 %collective-permute-start.22 = (bf16[2,96,2816]{2,1,0:T(8,128)(2,1)}, bf16[2,96,2816]{2,1,0:T(8,128)(2,1)}, u32[]{:S(2)}, u32[]{:S(2)}) collective-permute-start(bf16[2,96,2816]{2,1,0:T(8,128)(2,1)} %pad_maximum_fusion.2), channel_id=1, source_target_pairs={{0,1},{1,0},{2,3},{3,2},{4,5},{5,4},{6,7},{7,6},{8,9},{9,8},{10,11... | collective-permute-start | bytes 3244040 | tf_op jit(solution)/shard_map/ppermute | solution.py:489
  153.6 2.1 collective-permute-start.20
  154.0 34.6 %collective-permute-start.26 = (bf16[384,1536]{1,0:T(8,128)(2,1)}, bf16[384,1536]{1,0:T(8,128)(2,1)}, u32[]{:S(2)}, u32[]{:S(2)}) collective-permute-start(bf16[384,1536]{1,0:T(8,128)(2,1)} %collective-permute-done.25.w_first_ref), channel_id=1, source_target_pairs={{0,1},{1,0},{2,3},{3,2},{4,5},{5,4},{6,7},{7,6},{8,9},{9,8},{10,11... | collective-permute-start | bytes 3538952 | tf_op jit(solution)/shard_map/ppermute | solution.py:496
  156.6 2.1 collective-permute-start.23
  171.9 11.5 %collective-permute-start.24 = (bf16[256,768]{1,0:T(8,128)(2,1)}, bf16[256,768]{1,0:T(8,128)(2,1)}, u32[]{:S(2)}, u32[]{:S(2)}) collective-permute-start(bf16[256,768]{1,0:T(8,128)(2,1)} %get-tuple-element.52), channel_id=1, source_target_pairs={{0,16},{16,0},{1,17},{17,1},{2,18},{18,2},{3,19},{19,3},{4,20},{20... | collective-permute-start | bytes 1179656 | tf_op jit(solution)/shard_map/ppermute | solution.py:526
  187.0 15.6 %copy-start.24 = (bf16[256,1536]{1,0:T(8,128)(2,1)S(1)}, bf16[256,1536]{1,0:T(8,128)(2,1)}, u32[]{:S(2)}) copy-start(bf16[256,1536]{1,0:T(8,128)(2,1)} %copy-done.23) | copy-start | bytes 2359300
  187.0 15.6 %copy-start.29 = (bf16[256,1536]{1,0:T(8,128)(2,1)S(1)}, bf16[256,1536]{1,0:T(8,128)(2,1)}, u32[]{:S(2)}) copy-start(bf16[256,1536]{1,0:T(8,128)(2,1)} %copy-done.28) | copy-start | bytes 2359300
  187.0 17.6 %collective-permute-start.28 = (bf16[256,768]{1,0:T(8,128)(2,1)S(1)}, bf16[256,768]{1,0:T(8,128)(2,1)S(1)}, u32[]{:S(2)}, u32[]{:S(2)}) collective-permute-start(bf16[256,768]{1,0:T(8,128)(2,1)S(1)} %attention_late.1), channel_id=1, source_target_pairs={{0,16},{16,0},{1,17},{17,1},{2,18},{18,2},{3,19},{19,3},{4,20},{20... | collective-permute-start | bytes 1179656 | tf_op jit(solution)/shard_map/ppermute | solution.py:530
  202.0 19.9 %collective-permute-start.27 = (bf16[256,1536]{1,0:T(8,128)(2,1)}, bf16[256,1536]{1,0:T(8,128)(2,1)S(1)}, u32[]{:S(2)}, u32[]{:S(2)}) collective-permute-start(bf16[256,1536]{1,0:T(8,128)(2,1)} %get-tuple-element.56), channel_id=1, source_target_pairs={{0,16},{16,0},{1,17},{17,1},{2,18},{18,2},{3,19},{19,3},{4,20},{20... | collective-permute-start | bytes 2359304 | tf_op jit(solution)/shard_map/ppermute | solution.py:546
  204.5 17.4 %copy-start.32 = (f32[256,1536]{1,0:T(8,128)S(1)}, f32[256,1536]{1,0:T(8,128)}, u32[]{:S(2)}) copy-start(f32[256,1536]{1,0:T(8,128)} %get-tuple-element.55) | copy-start | bytes 4718596
  204.6 17.4 %copy-start.34 = (bf16[256,1536]{1,0:T(8,128)(2,1)S(1)}, bf16[256,1536]{1,0:T(8,128)(2,1)}, u32[]{:S(2)}) copy-start(bf16[256,1536]{1,0:T(8,128)(2,1)} %get-tuple-element.56) | copy-start | bytes 2359300
  217.9 19.7 %collective-permute-start.29 = (bf16[256,1536]{1,0:T(8,128)(2,1)}, bf16[256,1536]{1,0:T(8,128)(2,1)S(1)}, u32[]{:S(2)}, u32[]{:S(2)}) collective-permute-start(bf16[256,1536]{1,0:T(8,128)(2,1)} %get-tuple-element.62), channel_id=1, source_target_pairs={{0,16},{16,0},{1,17},{17,1},{2,18},{18,2},{3,19},{19,3},{4,20},{20... | collective-permute-start | bytes 2359304 | tf_op jit(solution)/shard_map/ppermute | solution.py:546
  221.9 15.7 %copy-start.33 = (f32[256,1536]{1,0:T(8,128)S(1)}, f32[256,1536]{1,0:T(8,128)}, u32[]{:S(2)}) copy-start(f32[256,1536]{1,0:T(8,128)} %get-tuple-element.61) | copy-start | bytes 4718596
  221.9 15.7 %copy-start.35 = (bf16[256,1536]{1,0:T(8,128)(2,1)S(1)}, bf16[256,1536]{1,0:T(8,128)(2,1)}, u32[]{:S(2)}) copy-start(bf16[256,1536]{1,0:T(8,128)(2,1)} %get-tuple-element.62) | copy-start | bytes 2359300
  (24 other events, 249.6 us)
